TPU v7x, 128 devices: a whole 4x4x4 slice. The times are simulated.
128 devices in a mesh: half: 2 (over core), ep: 64 (over z, x, y).
Axes of the slice: x: 4, y: 4, z: 4, core: 2. Of those that a mesh axis runs over, the one named last changes fastest.
Arguments:
- activations: bfloat16 [2, 28672, 2048], P('half', 'ep'), may hold values from -6 to 6
- routes: int32 [2, 28672, 1], P('half', 'ep'), may hold values from 0 to 63; in each aligned block of 448 rows (0 to 447, 448 to 895, ..., all dimensions but the last counted through in order) at most 14 rows name the same one
- blocks: int32 [2, 64], P('half'), may hold values from 1 to 7, as said below
- row_scale: bfloat16 [2, 28672], P('half', 'ep'), may hold values from -4 to 4
- gate_up: bfloat16 [64, 2048, 1536], P('ep'), may hold values from -0.125 to 0.125
- down_weight: bfloat16 [64, 768, 2048], P('ep'), may hold values from -0.21875 to 0.21875
- slot_map: int32 [64], replicated, may hold values from 0 to 63
Outputs:
- rows_out: bfloat16 [2, 28672, 2048], P('half', 'ep')
Inputs may be any that keep to these rules, and one draw needn't show every extreme that they name: `routes`: among the rows of one device, no destination appears more than 14 times, and some destination appears exactly 14 times. In each group some destination has exactly 7 blocks.
All inputs are finite; a program needn't handle non-finite values.
Results may differ from a plain program's by a relative error of at most 0.0099.
Values may be sent and summed in bfloat16 or wider, within the bound.
No kernel may reach another device: no remote copies, remote signals or barrier semaphores. Data moves between devices by JAX's collectives and lax.ppermute only.
A program may use at most 128 MiB of HBM per device.

v0:
```python
import math

import jax
import jax.numpy as jnp
from jax import lax
from jax.sharding import PartitionSpec as P

RDEV = 448
BLK = 128


def prefix(part, axis, combine, identity):
    place = lax.axis_index(axis)
    gathered = lax.all_gather(part, axis)
    state = jnp.zeros_like(part) + jnp.asarray(identity, part.dtype)

    def one(lap, state):
        return combine(state, lax.dynamic_index_in_dim(gathered, lap, 0, False))

    return lax.fori_loop(0, place, one, state)


def passed_along(value, axis, steps):
    count = lax.axis_size(axis)
    initial, last = (max(0, -steps), min(count, count - steps))
    return lax.ppermute(value, axis, [(source, source + steps) for source in range(initial, last)])


def silu_slope(value):
    sigma = jax.nn.sigmoid(value)
    return sigma * (1.0 + value * (1.0 - sigma))


def train_expert(inputs, scales, gate_up, down_weight):
    width = gate_up.shape[1] // 2
    projected = jnp.dot(inputs, gate_up, preferred_element_type=jnp.float32)
    gate = projected[:, :width]
    upward = projected[:, width:]
    hidden = (jax.nn.silu(gate) * upward).astype(jnp.bfloat16)
    output = jnp.dot(hidden, down_weight, preferred_element_type=jnp.float32)
    out_grad = (scales.astype(jnp.float32)[:, None] * output).astype(jnp.bfloat16)
    down_grad = lax.dot_general(
        hidden, out_grad, (((0,), (0,)), ((), ())), preferred_element_type=jnp.float32
    )
    hidden_grad = lax.dot_general(
        out_grad, down_weight, (((1,), (1,)), ((), ())), preferred_element_type=jnp.float32
    )
    both_grad = jnp.concatenate(
        [hidden_grad * upward * silu_slope(gate), hidden_grad * jax.nn.silu(gate)], axis=1
    ).astype(jnp.bfloat16)
    gate_grad = lax.dot_general(
        inputs, both_grad, (((0,), (0,)), ((), ())), preferred_element_type=jnp.float32
    )
    input_grad = lax.dot_general(
        both_grad, gate_up, (((1,), (1,)), ((), ())), preferred_element_type=jnp.float32
    ).astype(jnp.bfloat16)
    step_size = 0.03 / math.sqrt(RDEV)
    new_gate = (gate_up.astype(jnp.float32) - step_size * gate_grad).astype(jnp.bfloat16)
    new_down = (down_weight.astype(jnp.float32) - step_size * down_grad).astype(jnp.bfloat16)
    return (input_grad, new_gate, new_down)


def skip_train(inputs, scales, gate_up, down_weight):
    return (jnp.zeros_like(inputs), jnp.zeros_like(gate_up), jnp.zeros_like(down_weight))


def serve_expert(inputs, scales, gate_up, down_weight):
    width = gate_up.shape[1] // 2
    projected = jnp.dot(inputs, gate_up, preferred_element_type=jnp.float32)
    hidden = (jax.nn.silu(projected[:, :width]) * projected[:, width:]).astype(jnp.bfloat16)
    output = jnp.dot(hidden, down_weight, preferred_element_type=jnp.float32)
    return (scales.astype(jnp.float32)[:, None] * output).astype(jnp.bfloat16)


def skip_serve(inputs, scales, gate_up, down_weight):
    return jnp.zeros_like(inputs)


def add_counts(earlier, later):
    return earlier + later


def relay_weights(gate_part, down_part, slot_map):
    members = lax.axis_size("ep")
    pieces_gate = gate_part.reshape(members, gate_part.shape[0] // members, gate_part.shape[1])
    pieces_down = down_part.reshape(members, down_part.shape[0] // members, down_part.shape[1])
    spread_gate, spread_down = (
        lax.all_to_all(pieces_gate, "ep", split_axis=0, concat_axis=0, tiled=True),
        lax.all_to_all(pieces_down, "ep", split_axis=0, concat_axis=0, tiled=True),
    )
    chosen_gate = jnp.take(spread_gate, slot_map, axis=0)
    chosen_down = jnp.take(spread_down, slot_map, axis=0)
    whole_gate, whole_down = (
        lax.all_to_all(chosen_gate, "ep", split_axis=0, concat_axis=0, tiled=True),
        lax.all_to_all(chosen_down, "ep", split_axis=0, concat_axis=0, tiled=True),
    )
    return (whole_gate.reshape(gate_part.shape), whole_down.reshape(down_part.shape))


def shards(activations, routes, blocks, row_scale, gate_up, down_weight, slot_map):
    members = lax.axis_size("ep")
    row_count = activations.shape[1]
    model_width = activations.shape[2]
    capacity = 2 * row_count // members
    slot_total = members * capacity
    tokens = activations[0]
    scales = row_scale[0]
    target = routes[0, :, 0]
    limits = blocks[0] * BLK
    labels = jnp.arange(members, dtype=jnp.int32)
    onehot = (target[:, None] == labels[None, :]).astype(jnp.int32)
    local_order = jnp.sum((jnp.cumsum(onehot, axis=0) - onehot) * onehot, axis=1)
    counts = jnp.sum(onehot, axis=0)
    earlier = prefix(counts, "ep", add_counts, jnp.zeros_like(counts))
    global_order = local_order + jnp.sum(onehot * earlier[None, :], axis=1)
    kept_rows = global_order < jnp.sum(onehot * limits[None, :], axis=1)
    position = target * capacity + local_order
    slot_ids = jnp.arange(slot_total, dtype=jnp.int32)
    placer = ((slot_ids[:, None] == position[None, :]) & kept_rows[None, :]).astype(jnp.bfloat16)
    packed = jnp.dot(placer, tokens, preferred_element_type=jnp.float32).astype(jnp.bfloat16)
    packed = packed.reshape(members, capacity, model_width)
    packed_scale = jnp.dot(placer, scales[:, None], preferred_element_type=jnp.float32)[:, 0]
    packed_scale = packed_scale.astype(jnp.bfloat16).reshape(members, capacity)
    arrived, arrived_scale = (
        lax.all_to_all(packed, "ep", split_axis=0, concat_axis=0, tiled=True),
        lax.all_to_all(packed_scale, "ep", split_axis=0, concat_axis=0, tiled=True),
    )
    inputs = arrived.reshape(slot_total, model_width)
    in_scale = arrived_scale.reshape(slot_total)
    trainer = lax.axis_index("half") == 0
    input_grad, new_gate, new_down = lax.cond(
        trainer, train_expert, skip_train, inputs, in_scale, gate_up[0], down_weight[0]
    )
    moved_gate, moved_down = passed_along((new_gate, new_down), "half", 1)
    slot_gate, slot_down = relay_weights(moved_gate, moved_down, slot_map)
    served = lax.cond(trainer, skip_serve, serve_expert, inputs, in_scale, slot_gate, slot_down)
    answers = jnp.where(trainer, input_grad, served).reshape(members, capacity, model_width)
    returned = lax.all_to_all(answers, "ep", split_axis=0, concat_axis=0, tiled=True).reshape(
        slot_total, model_width
    )
    rows_out = lax.dot_general(
        placer, returned, (((0,), (0,)), ((), ())), preferred_element_type=jnp.float32
    )
    return rows_out.astype(jnp.bfloat16)[None]


def solution(mesh):
    placed = (
        P("half", "ep", None),
        P("half", "ep", None),
        P("half", None),
        P("half", "ep"),
        P("ep", None, None),
        P("ep", None, None),
        P(),
    )
    return jax.shard_map(
        shards, mesh=mesh, in_specs=placed, out_specs=P("half", "ep", None), check_vma=False
    )
```

profile of v0, /device:TPU:1, one launch (start us, length us, event | category | flops | bytes accessed | tf_op | source)
XLA Modules:
  0.0 905.5 jit_solution(9872243081597169962)
XLA Ops:
  4.6 296.0 %all-reduce.1 = s32[4096]{0:T(1024)S(1)} all-reduce(s32[4096]{0:T(1024)S(1)} %dynamic-update-slice), channel_id=2, replica_groups=mesh['half'=2,'ep'=64] {'ep'}, use_global_device_ids=true, to_apply=%add.1 | all-reduce | flops 4096 | bytes 32768
  306.3 4.6 all-to-all-start
  310.9 3.9 convolution_convert_fusion
  314.8 6.0 reshape.105
  320.8 10.0 %all-to-all-start.1 = ((bf16[64,14,2048]{2,1,0:T(8,128)(2,1)}), bf16[64,14,2048]{2,1,0:T(8,128)(2,1)}, u32[]{:S(2)}, u32[]{:S(2)}) async-start(bf16[64,14,2048]{2,1,0:T(8,128)(2,1)} %reshape.105), calls=%async_computation.1 | async-start | bytes 8388608 | tf_op jit(solution)/shard_map/all_to_all | solution.py:125
  331.1 30.0 %all-to-all-done.1 = bf16[64,14,2048]{2,1,0:T(8,128)(2,1)} async-done(((bf16[64,14,2048]{2,1,0:T(8,128)(2,1)}), bf16[64,14,2048]{2,1,0:T(8,128)(2,1)}, u32[]{:S(2)}, u32[]{:S(2)}) %all-to-all-start.1) | async-done | bytes 3670048 | tf_op jit(solution)/shard_map/all_to_all | solution.py:125
  361.2 6.0 reshape.106
  367.2 16.3 %conditional.2 = (bf16[896,2048]{1,0:T(8,128)(2,1)}, bf16[2048,1536]{0,1:T(8,128)(2,1)}, bf16[768,2048]{1,0:T(8,128)(2,1)}) conditional(s32[]{:T(128)} %convert_element_type.58, () %tuple.24, (bf16[896]{0:T(1024)(128)(2,1)S(1)}, bf16[1,2048,1536]{2,1,0:T(8,128)(2,1)}, bf16[896,2048]{1,0:T(8,128)(2,1)}, bf16[1,768,2048]{2,1,0:T(8,128)(2,1)}) %tuple.25), branch_computations={%region_8.9_spmd, %region_9.10_spmd} | conditional | flops 25415614464 | bytes 132719464 | solution.py:131
  371.5 3.4 broadcast.69
  383.4 8.7 copy.31
  394.7 119.9 %collective-permute-done.1 = bf16[768,2048]{1,0:T(8,128)(2,1)} collective-permute-done((bf16[768,2048]{1,0:T(8,128)(2,1)}, bf16[768,2048]{1,0:T(8,128)(2,1)}, u32[]{:S(2)}, u32[]{:S(2)}) %collective-permute-start.1) | collective-permute-done | bytes 3145760 | tf_op jit(solution)/shard_map/ppermute | solution.py:26
  514.6 6.1 reshape.108
  520.7 56.9 %all_to_all.36 = bf16[64,12,2048]{2,1,0:T(8,128)(2,1)} all-to-all(bf16[64,12,2048]{2,1,0:T(8,128)(2,1)} %reshape.108), channel_id=1, replica_groups=mesh['half'=2,'ep'=64] {'ep'}, dimensions={0} | all-to-all | bytes 6291456 | tf_op jit(solution)/shard_map/all_to_all | solution.py:89
  577.6 6.7 all-to-all-start.2
  584.4 4.9 gather_fusion.1
  589.3 4.6 broadcast_select_fusion.1
  593.9 73.5 %all-to-all-done.2 = bf16[64,32,1536]{2,1,0:T(8,128)(2,1)} async-done(((bf16[64,32,1536]{2,1,0:T(8,128)(2,1)}), bf16[64,32,1536]{2,1,0:T(8,128)(2,1)}, u32[]{:S(2)}, u32[]{:S(2)}) %all-to-all-start.2) | async-done | bytes 6291488 | tf_op jit(solution)/shard_map/all_to_all | solution.py:88
  667.4 9.0 all-to-all-start.5
  676.4 6.3 gather_fusion
  682.7 6.0 broadcast_select_fusion
  688.8 36.9 %all-to-all-done.5 = bf16[64,12,2048]{2,1,0:T(8,128)(2,1)} async-done(((bf16[64,12,2048]{2,1,0:T(8,128)(2,1)}), bf16[64,12,2048]{2,1,0:T(8,128)(2,1)}, u32[]{:S(2)}, u32[]{:S(2)}) %all-to-all-start.5) | async-done | bytes 3145760 | tf_op jit(solution)/shard_map/all_to_all | solution.py:95
  725.7 9.4 %all-to-all-start.3 = ((bf16[64,32,1536]{2,1,0:T(8,128)(2,1)}), bf16[64,32,1536]{2,1,0:T(8,128)(2,1)}, u32[]{:S(2)}, u32[]{:S(2)}) async-start(bf16[64,32,1536]{2,1,0:T(8,128)(2,1)} %broadcast_select_fusion), calls=%async_computation.3 | async-start | bytes 12582912 | tf_op jit(solution)/shard_map/all_to_all | solution.py:94
  735.1 80.5 %all-to-all-done.3 = bf16[64,32,1536]{2,1,0:T(8,128)(2,1)} async-done(((bf16[64,32,1536]{2,1,0:T(8,128)(2,1)}), bf16[64,32,1536]{2,1,0:T(8,128)(2,1)}, u32[]{:S(2)}, u32[]{:S(2)}) %all-to-all-start.3) | async-done | bytes 6291488 | tf_op jit(solution)/shard_map/all_to_all | solution.py:94
  815.6 20.0 %conditional.3 = (bf16[896,2048]{1,0:T(8,128)(2,1)}) conditional(s32[]{:T(128)} %convert_element_type.58, (bf16[896]{0:T(1024)(128)(2,1)S(1)}, bf16[64,32,1536]{2,1,0:T(8,128)(2,1)}, bf16[896,2048]{1,0:T(8,128)(2,1)}, bf16[64,12,2048]{2,1,0:T(8,128)(2,1)}) %tuple.26, () %tuple.27), branch_computations={%region_10.11_spmd, %region_11.12_spmd} | conditional | flops 8463516672 | bytes 46670628 | solution.py:136
  815.6 6.1 reshape.90
  821.8 9.2 %fusion.33 = f32[896,1536]{1,0:T(8,128)S(1)} fusion(bf16[896,2048]{1,0:T(8,128)(2,1)} %get-tuple-element.55, bf16[2048,1536]{1,0:T(8,128)(2,1)} %bitcast.4), kind=kOutput, calls=%fused_computation.67 | convolution fusion | flops 5637144576 | bytes 15466496 | tf_op jit(solution)/shard_map/cond/branch_0_fun/dot_general | solution.py:69
  831.0 4.6 multiply_convert_fusion.4
  835.6 4.3 broadcast_select_fusion.2
  839.9 6.0 reshape.109
  845.9 47.8 %all_to_all.37 = bf16[64,14,2048]{2,1,0:T(8,128)(2,1)} all-to-all(bf16[64,14,2048]{2,1,0:T(8,128)(2,1)} %reshape.109), channel_id=1, replica_groups=mesh['half'=2,'ep'=64] {'ep'}, dimensions={0} | all-to-all | bytes 7340032 | tf_op jit(solution)/shard_map/all_to_all | solution.py:138
  893.7 6.1 reshape.110
  899.9 5.4 fusion.18
  (44 shorter events, 16.8 us)
Async XLA Ops:
  0.0 310.9 %copy-start = (bf16[1,448,2048]{2,1,0:T(8,128)(2,1)S(1)}, bf16[1,448,2048]{2,1,0:T(8,128)(2,1)}, u32[]{:S(2)}) copy-start(bf16[1,448,2048]{2,1,0:T(8,128)(2,1)} %param.13) | copy-start | bytes 5505028
  306.3 14.5 %all-to-all-start = ((bf16[64,1,14]{2,1,0:T(2,128)(2,1)}), bf16[64,1,14]{2,1,0:T(2,128)(2,1)S(1)}, u32[]{:S(2)}, u32[]{:S(2)}) async-start(bf16[64,1,14]{2,1,0:T(2,128)(2,1)} %copy.29), calls=%async_computation | async-start | bytes 65536 | tf_op jit(solution)/shard_map/all_to_all | solution.py:126
  320.8 40.3 %all-to-all-start.1 = ((bf16[64,14,2048]{2,1,0:T(8,128)(2,1)}), bf16[64,14,2048]{2,1,0:T(8,128)(2,1)}, u32[]{:S(2)}, u32[]{:S(2)}) async-start(bf16[64,14,2048]{2,1,0:T(8,128)(2,1)} %reshape.105), calls=%async_computation.1 | async-start | bytes 8388608 | tf_op jit(solution)/shard_map/all_to_all | solution.py:125
  392.1 185.5 %collective-permute-start = (bf16[2048,1536]{1,0:T(8,128)(2,1)}, bf16[2048,1536]{1,0:T(8,128)(2,1)}, u32[]{:S(2)}, u32[]{:S(2)}) collective-permute-start(bf16[2048,1536]{1,0:T(8,128)(2,1)} %copy.31), channel_id=1, source_target_pairs={{0,64},{1,65},{2,66},{3,67},{4,68},{5,69},{6,70},{7,71},{8,72},{9,... | collective-permute-start | bytes 18874376 | tf_op jit(solution)/shard_map/ppermute | solution.py:26
  393.4 121.2 %collective-permute-start.1 = (bf16[768,2048]{1,0:T(8,128)(2,1)}, bf16[768,2048]{1,0:T(8,128)(2,1)}, u32[]{:S(2)}, u32[]{:S(2)}) collective-permute-start(bf16[768,2048]{1,0:T(8,128)(2,1)} %get-tuple-element.65), channel_id=1, source_target_pairs={{0,64},{1,65},{2,66},{3,67},{4,68},{5,69},{6,70},{7,71},{8,72},{9,... | collective-permute-start | bytes 9437192 | tf_op jit(solution)/shard_map/ppermute | solution.py:26
  577.6 6.8 copy-start.4
  577.6 89.8 %all-to-all-start.2 = ((bf16[64,32,1536]{2,1,0:T(8,128)(2,1)}), bf16[64,32,1536]{2,1,0:T(8,128)(2,1)}, u32[]{:S(2)}, u32[]{:S(2)}) async-start(bf16[64,32,1536]{2,1,0:T(8,128)(2,1)} %bitcast.12), calls=%async_computation.2 | async-start | bytes 12582912 | tf_op jit(solution)/shard_map/all_to_all | solution.py:88
  667.4 58.2 %all-to-all-start.5 = ((bf16[64,12,2048]{2,1,0:T(8,128)(2,1)}), bf16[64,12,2048]{2,1,0:T(8,128)(2,1)}, u32[]{:S(2)}, u32[]{:S(2)}) async-start(bf16[64,12,2048]{2,1,0:T(8,128)(2,1)} %broadcast_select_fusion.1), calls=%async_computation.5 | async-start | bytes 8388608 | tf_op jit(solution)/shard_map/all_to_all | solution.py:95
  725.7 90.0 %all-to-all-start.3 = ((bf16[64,32,1536]{2,1,0:T(8,128)(2,1)}), bf16[64,32,1536]{2,1,0:T(8,128)(2,1)}, u32[]{:S(2)}, u32[]{:S(2)}) async-start(bf16[64,32,1536]{2,1,0:T(8,128)(2,1)} %broadcast_select_fusion), calls=%async_computation.3 | async-start | bytes 12582912 | tf_op jit(solution)/shard_map/all_to_all | solution.py:94
  821.8 9.2 %copy-start.2 = (bf16[768,2048]{1,0:T(8,128)(2,1)S(1)}, bf16[768,2048]{1,0:T(8,128)(2,1)}, u32[]{:S(2)}) copy-start(bf16[768,2048]{1,0:T(8,128)(2,1)} %reshape.90) | copy-start | bytes 9437188 | tf_op jit(solution)/shard_map/cond
  893.7 11.5 %copy-start.1 = (bf16[1,448,2048]{2,1,0:T(8,128)(2,1)S(1)}, bf16[1,448,2048]{2,1,0:T(8,128)(2,1)}, u32[]{:S(2)}) copy-start(bf16[1,448,2048]{2,1,0:T(8,128)(2,1)} %param.13) | copy-start | bytes 5505028
where the time goes:
time: 913 us; the launch traced here: 905 us
  blocking collectives  401 us (44%)
  waiting for transfers between devices  341 us (37%)
  local copies, waits for them, and re-layouts  67 us (7%)
  starting transfers between devices  42.4 us (5%)
  matrix products  24.3 us (3%)
  other arithmetic  20.5 us (2%)
    unnamed x1, blocking collectives  296 us
    ppermute x2, waiting for transfers between devices, passed_along(): lax.ppermute(value, axis, [(source, source + steps) for source in range(i...  120 us
    all_to_all x1, waiting for transfers between devices, relay_weights(): lax.all_to_all(chosen_gate, 'ep', split_axis=0, concat_axis=0, tiled=True)  80.5 us
    all_to_all x1, waiting for transfers between devices, relay_weights(): lax.all_to_all(pieces_gate, 'ep', split_axis=0, concat_axis=0, tiled=True)  73.5 us
    all_to_all x1, blocking collectives, relay_weights(): lax.all_to_all(pieces_down, 'ep', split_axis=0, concat_axis=0, tiled=True)  56.9 us
    all_to_all x1, blocking collectives, shards(): lax.all_to_all(answers, 'ep', split_axis=0, concat_axis=0, tiled=True)  47.8 us
    all_to_all x1, waiting for transfers between devices, relay_weights(): lax.all_to_all(chosen_down, 'ep', split_axis=0, concat_axis=0, tiled=True)  36.9 us
    all_to_all x1, waiting for transfers between devices, shards(): lax.all_to_all(packed, 'ep', split_axis=0, concat_axis=0, tiled=True)  30 us
  transfers between devices with their start and end apart: 7, of which 5 were waited for; matrix products, arithmetic and copies ran while one was open for 4% of the time, Pallas kernels for 0%

commit v1 on v0

v1 whole, which is shorter than its diff:
```python
import math

import jax
import jax.numpy as jnp
from jax import lax
from jax.experimental import pallas as pl
from jax.experimental.pallas import tpu as pltpu
from jax.sharding import PartitionSpec as P

BLK = 128
PART = 7
BOX = 8
COUNT = 8
LANES = 128
SWAP = [(0, 1), (1, 0)]
F32 = jnp.float32
BF16 = jnp.bfloat16
NT = (((1,), (1,)), ((), ()))


def params(mib=56):
    return pltpu.CompilerParams(vmem_limit_bytes=mib << 20)


def iota(shape, dim):
    return lax.broadcasted_iota(jnp.int32, shape, dim)


def anywhere():
    return pl.BlockSpec(memory_space=pl.ANY)


def vmem():
    return pl.BlockSpec(memory_space=pltpu.VMEM)


def smem():
    return pl.BlockSpec(memory_space=pltpu.SMEM)


def order_of(target, members):
    rows = target.shape[1]
    named = iota((members, rows), 0) == target
    onehot = named.astype(BF16)
    upper = (iota((rows, rows), 0) < iota((rows, rows), 1)).astype(BF16)
    before = jnp.dot(onehot, upper, preferred_element_type=F32)
    return jnp.sum(jnp.where(named, before, 0.0), axis=0, keepdims=True).astype(jnp.int32)


def pack_kernel(group, members, scal, tok_a, tok_b, route_a, route_b, scale_a, scale_b, out, tok, sem):
    half = scal[0]
    own = half == group

    @pl.when(own)
    def _():
        pltpu.make_async_copy(tok_a, tok, sem).start()

    @pl.when(jnp.logical_not(own))
    def _():
        pltpu.make_async_copy(tok_b, tok, sem).start()

    target = jnp.where(own, route_a[...], route_b[...])
    scale = jnp.where(own, scale_a[...].astype(F32), scale_b[...].astype(F32))
    rows = target.shape[1]
    slots = members * BOX
    order = order_of(target, members) - PART * half
    inside = (order >= 0) & (order < PART)
    place = jnp.where(inside, target * BOX + order, -1)
    placer = (iota((slots, rows), 0) == place).astype(BF16)
    tags = (iota((slots, rows), 0) == target * BOX + PART).astype(BF16)
    lane = iota((LANES, rows), 0)
    told = jnp.where((lane == order) & inside, scale, jnp.where(lane == COUNT, 1.0, 0.0)).astype(BF16)
    info = lax.dot_general(tags, told, NT, preferred_element_type=F32)
    pltpu.make_async_copy(tok_a, tok, sem).wait()
    first = jnp.dot(placer, tok[:, :LANES], preferred_element_type=F32) + info
    out[:, :LANES] = first.astype(BF16)
    rest = tok.shape[1] - LANES
    out[:, LANES:] = jnp.dot(placer, tok[:, LANES:], preferred_element_type=F32).astype(BF16)


def pack(group, members, scal, tok_a, tok_b, route_a, route_b, scale_a, scale_b):
    slots = members * BOX
    width = tok_a.shape[1]
    return pl.pallas_call(
        lambda *refs: pack_kernel(group, members, *refs),
        out_shape=jax.ShapeDtypeStruct((slots, width), BF16),
        in_specs=[smem(), anywhere(), anywhere(), vmem(), vmem(), vmem(), vmem()],
        out_specs=vmem(),
        scratch_shapes=[pltpu.VMEM(tok_a.shape, BF16), pltpu.SemaphoreType.DMA],
        compiler_params=params(),
        name=f"pack{group}",
    )(scal, tok_a, tok_b, route_a, route_b, scale_a, scale_b)


def kept_and_scale(head, half, limit):
    slots = head.shape[0]
    row = iota((slots, slots), 0) // BOX
    col = iota((slots, slots), 1)
    tag = (col % BOX) == PART
    mine = (tag & (col // BOX == row)).astype(BF16)
    lower = (tag & (col // BOX < row)).astype(BF16)
    here = jnp.dot(mine, head, preferred_element_type=F32)
    below = jnp.dot(lower, head, preferred_element_type=F32)
    lane = iota((slots, LANES), 1)
    place = iota((slots, LANES), 0) % BOX
    scale = jnp.sum(jnp.where(lane == place, here, 0.0), axis=1, keepdims=True)
    total = jnp.sum(jnp.where(lane == COUNT, here, 0.0), axis=1, keepdims=True)
    ahead = jnp.sum(jnp.where(lane == COUNT, below, 0.0), axis=1, keepdims=True)
    k = iota((slots, 1), 0) % BOX
    index = (k + PART * half).astype(F32)
    kept = (k < PART) & (index < total) & (ahead + index < limit.astype(F32))
    return kept, scale


def limit_of(group, scal, blocks_a, blocks_b):
    own = scal[0] == group
    at = scal[1]
    return jnp.where(own, blocks_a[0, at], blocks_b[0, at]) * BLK


def train_kernel(scal, blocks_a, blocks_b, x_h, gu_h, dw_h, dg_own, dg_send, gg_own, gg_send, bg_h,
                 x, gu, dw, gate, up, hid, og, bg, hid_t, x_t, dg, gg, sem):
    half = scal[0]
    d, f2 = gu.shape
    f = f2 // 2
    fc, dc = 256, 512
    nf, nd = f // fc, d // dc

    def load_gu(i, which):
        cols = pl.ds(pl.multiple_of(which * f + i * fc, fc), fc)
        return pltpu.make_async_copy(gu_h.at[:, cols], gu.at[:, cols], sem.at[2 + 2 * i + which])

    load_x = pltpu.make_async_copy(x_h, x, sem.at[0])
    load_dw = pltpu.make_async_copy(dw_h, dw, sem.at[1])
    load_x.start()
    for i in range(nf):
        load_gu(i, 0).start()
        load_gu(i, 1).start()
    load_dw.start()
    load_x.wait()
    kept, scale = kept_and_scale(x[:, :LANES], half, limit_of(0, scal, blocks_a, blocks_b))
    keep = jnp.where(kept, 1.0, 0.0)

    def mask(c, _):
        cols = pl.ds(pl.multiple_of(c * fc, fc), fc)
        clean = (x[:, cols].astype(F32) * keep).astype(BF16)
        x[:, cols] = clean
        x_t[cols, :] = clean.T
        return 0

    lax.fori_loop(0, d // fc, mask, 0)

    def project(i, _):
        load_gu(i, 0).wait()
        load_gu(i, 1).wait()
        left = pl.ds(pl.multiple_of(i * fc, fc), fc)
        right = pl.ds(pl.multiple_of(f + i * fc, fc), fc)
        g = jnp.dot(x[...], gu[:, left], preferred_element_type=F32)
        u = jnp.dot(x[...], gu[:, right], preferred_element_type=F32)
        h = (g * jax.nn.sigmoid(g) * u).astype(BF16)
        gate[:, left] = g
        up[:, left] = u
        hid[:, left] = h
        hid_t[left, :] = h.T
        return 0

    lax.fori_loop(0, nf, project, 0)
    load_dw.wait()

    def outputs(c, _):
        cols = pl.ds(pl.multiple_of(c * dc, dc), dc)
        o = jnp.dot(hid[...], dw[:, cols], preferred_element_type=F32)
        og[:, cols] = (scale * o).astype(BF16)
        return 0

    lax.fori_loop(0, nd, outputs, 0)

    def down_part(c, _):
        cols = pl.ds(pl.multiple_of(c * dc, dc), dc)
        dg[:, cols] = jnp.dot(hid_t[...], og[:, cols], preferred_element_type=F32).astype(BF16)
        return 0

    lax.fori_loop(0, nd, down_part, 0)

    def store(src, own, send, lo, size, s):
        def copies(b):
            part = src.at[pl.ds(b * size, size)]
            return pltpu.make_async_copy(part, (own, send)[b != lo], sem.at[s + b])

        return copies

    for h in range(2):
        @pl.when(half == h)
        def _():
            for b in range(2):
                store(dg, dg_own, dg_send, h, f // 2, 2 + 2 * nf)(b).start()

    def hidden_back(i, _):
        left = pl.ds(pl.multiple_of(i * fc, fc), fc)
        right = pl.ds(pl.multiple_of(f + i * fc, fc), fc)
        hg = lax.dot_general(og[...], dw[left, :], NT, preferred_element_type=F32)
        g = gate[:, left]
        s = jax.nn.sigmoid(g)
        bg[:, left] = (hg * up[:, left] * (s * (1.0 + g * (1.0 - s)))).astype(BF16)
        bg[:, right] = (hg * (g * s)).astype(BF16)
        return 0

    lax.fori_loop(0, nf, hidden_back, 0)
    out_bg = pltpu.make_async_copy(bg, bg_h, sem.at[6 + 2 * nf])
    out_bg.start()
    for b in range(2):
        rows = pl.ds(b * (d // 2), d // 2)

        def gate_part(c, _):
            cols = pl.ds(pl.multiple_of(c * fc, fc), fc)
            gg[rows, cols] = jnp.dot(x_t[rows, :], bg[:, cols], preferred_element_type=F32).astype(BF16)
            return 0

        lax.fori_loop(0, f2 // fc, gate_part, 0)
        for h in range(2):
            @pl.when(half == h)
            def _():
                store(gg, gg_own, gg_send, h, d // 2, 4 + 2 * nf)(b).start()
    for b in range(2):
        store(dg, dg_own, dg_send, 0, f // 2, 2 + 2 * nf)(b).wait()
        store(gg, gg_own, gg_send, 0, d // 2, 4 + 2 * nf)(b).wait()
    out_bg.wait()


def train(scal, blocks_a, blocks_b, x, gate_up, down):
    slots, d = x.shape
    f2 = gate_up.shape[1]
    f = f2 // 2
    dg = jax.ShapeDtypeStruct((f // 2, d), BF16)
    gg = jax.ShapeDtypeStruct((d // 2, f2), BF16)
    nf = f // 256
    return pl.pallas_call(
        train_kernel,
        out_shape=(dg, dg, gg, gg, jax.ShapeDtypeStruct((slots, f2), BF16)),
        in_specs=[smem(), smem(), smem(), anywhere(), anywhere(), anywhere()],
        out_specs=(anywhere(),) * 5,
        scratch_shapes=[
            pltpu.VMEM((slots, d), BF16), pltpu.VMEM((d, f2), BF16), pltpu.VMEM((f, d), BF16),
            pltpu.VMEM((slots, f), F32), pltpu.VMEM((slots, f), F32), pltpu.VMEM((slots, f), BF16),
            pltpu.VMEM((slots, d), BF16), pltpu.VMEM((slots, f2), BF16), pltpu.VMEM((f, slots), BF16),
            pltpu.VMEM((d, slots), BF16), pltpu.VMEM((f, d), BF16), pltpu.VMEM((d, f2), BF16),
            pltpu.SemaphoreType.DMA((7 + 2 * nf,)),
        ],
        compiler_params=params(),
        name="train",
    )(scal, blocks_a, blocks_b, x, gate_up, down)


def update_down_kernel(eta, scal, a, b, w, out):
    new = w[...].astype(F32) - eta * (a[...].astype(F32) + b[...].astype(F32))
    high, wide = out.shape[2:]
    for i in range(out.shape[0]):
        for j in range(out.shape[1]):
            out[i, j] = new[i * high:(i + 1) * high, j * wide:(j + 1) * wide].astype(BF16)


def update_down(eta, scal, a, b, w):
    rows, d = a.shape
    high, wide, steps = rows // 8, d // 8, 4
    tall = rows // steps
    mine = pl.BlockSpec((tall, d), lambda i, s: (i, 0))
    return pl.pallas_call(
        lambda *refs: update_down_kernel(eta, *refs),
        out_shape=jax.ShapeDtypeStruct((8, 8, high, wide), BF16),
        grid_spec=pltpu.PrefetchScalarGridSpec(
            num_scalar_prefetch=1,
            grid=(steps,),
            in_specs=[mine, mine, pl.BlockSpec((tall, d), lambda i, s: (s[0] * steps + i, 0))],
            out_specs=pl.BlockSpec((8 // steps, 8, high, wide), lambda i, s: (i, 0, 0, 0)),
        ),
        compiler_params=params(),
        name="update_down",
    )(scal, a, b, w)


def update_gate_kernel(eta, scal, a, b, w, out):
    out[...] = (w[...].astype(F32) - eta * (a[...].astype(F32) + b[...].astype(F32))).astype(BF16)


def update_gate(eta, scal, a, b, w):
    rows, f2 = a.shape
    steps = 4
    tall = rows // steps
    mine = pl.BlockSpec((tall, f2), lambda i, s: (i, 0))
    return pl.pallas_call(
        lambda *refs: update_gate_kernel(eta, *refs),
        out_shape=jax.ShapeDtypeStruct((rows, f2), BF16),
        grid_spec=pltpu.PrefetchScalarGridSpec(
            num_scalar_prefetch=1,
            grid=(steps,),
            in_specs=[mine, mine, pl.BlockSpec((tall, f2), lambda i, s: (s[0] * steps + i, 0))],
            out_specs=mine,
        ),
        compiler_params=params(),
        name="update_gate",
    )(scal, a, b, w)


def choose_kernel(slot_map, src, out, sem):
    count = out.shape[0]

    def copy(i):
        return pltpu.make_async_copy(src.at[slot_map[i]], out.at[i], sem.at[i])

    def start(i, _):
        copy(i).start()
        return 0

    def wait(i, _):
        copy(i).wait()
        return 0

    lax.fori_loop(0, count, start, 0)
    lax.fori_loop(0, count, wait, 0)


def choose(name, slot_map, pieces):
    return pl.pallas_call(
        choose_kernel,
        out_shape=jax.ShapeDtypeStruct(pieces.shape, BF16),
        in_specs=[smem(), anywhere()],
        out_specs=anywhere(),
        scratch_shapes=[pltpu.SemaphoreType.DMA((pieces.shape[0],))],
        compiler_params=params(4),
        name=name,
    )(slot_map, pieces)


def serve_kernel(scal, blocks_a, blocks_b, x_h, gu_a, gu_b, dw_a, dw_b, out, x, gu, dw, hid, sem):
    half = scal[0]
    d, f2 = gu.shape
    f = f2 // 2
    fc, dc = 256, 512

    load_x = pltpu.make_async_copy(x_h, x, sem.at[0])

    def load_gu(src, place, s):
        rows = pl.ds(pl.multiple_of(place * (d // 2), d // 2), d // 2)
        return pltpu.make_async_copy(src, gu.at[rows], sem.at[s])

    def load_dw(src, place, j, s):
        wide = d // 8
        return pltpu.make_async_copy(src.at[:, j], dw.at[place, :, :, pl.ds(j * wide, wide)], sem.at[s + j])

    load_x.start()
    load_gu(gu_a, half, 1).start()
    load_gu(gu_b, 1 - half, 2).start()
    for j in range(8):
        load_dw(dw_a, half, j, 3).start()
        load_dw(dw_b, 1 - half, j, 11).start()
    load_x.wait()
    kept, scale = kept_and_scale(x[:, :LANES], half, limit_of(1, scal, blocks_a, blocks_b))
    load_gu(gu_a, half, 1).wait()
    load_gu(gu_b, 1 - half, 2).wait()

    def project(i, _):
        left = pl.ds(pl.multiple_of(i * fc, fc), fc)
        right = pl.ds(pl.multiple_of(f + i * fc, fc), fc)
        g = jnp.dot(x[...], gu[:, left], preferred_element_type=F32)
        u = jnp.dot(x[...], gu[:, right], preferred_element_type=F32)
        hid[:, left] = (g * jax.nn.sigmoid(g) * u).astype(BF16)
        return 0

    lax.fori_loop(0, f // fc, project, 0)
    for j in range(8):
        load_dw(dw_a, half, j, 3).wait()
        load_dw(dw_b, 1 - half, j, 11).wait()

    def outputs(c, _):
        cols = pl.ds(pl.multiple_of(c * dc, dc), dc)
        o = jnp.dot(hid[...], dw[:, :, :, cols].reshape(f, dc), preferred_element_type=F32)
        out[:, cols] = jnp.where(kept, scale * o, 0.0).astype(BF16)
        return 0

    lax.fori_loop(0, d // dc, outputs, 0)


def serve(scal, blocks_a, blocks_b, x, gu_a, gu_b, dw_a, dw_b):
    slots, d = x.shape
    f2 = gu_a.shape[1]
    high = dw_a.shape[2]
    return pl.pallas_call(
        serve_kernel,
        out_shape=jax.ShapeDtypeStruct((slots, d), BF16),
        in_specs=[smem(), smem(), smem()] + [anywhere()] * 5,
        out_specs=vmem(),
        scratch_shapes=[
            pltpu.VMEM((slots, d), BF16), pltpu.VMEM((d, f2), BF16), pltpu.VMEM((2, 8, high, d), BF16),
            pltpu.VMEM((slots, f2 // 2), BF16), pltpu.SemaphoreType.DMA((19,)),
        ],
        compiler_params=params(),
        name="serve",
    )(scal, blocks_a, blocks_b, x, gu_a, gu_b, dw_a, dw_b)


def unpack_kernel(members, scal, route, t_own, t_recv, p_own, p_recv, out, low, high, sem):
    half = scal[0]

    @pl.when(half == 0)
    def _():
        pltpu.make_async_copy(t_own, low, sem.at[0]).start()
        pltpu.make_async_copy(t_recv, high, sem.at[1]).start()

    @pl.when(half == 1)
    def _():
        pltpu.make_async_copy(p_recv, low, sem.at[0]).start()
        pltpu.make_async_copy(p_own, high, sem.at[1]).start()

    target = route[...]
    rows = target.shape[1]
    order = order_of(target, members)
    eye = (iota((rows, rows), 0) == iota((rows, rows), 1)).astype(BF16)
    pair = jnp.where(iota((BOX, rows), 0) == 0, target, order).astype(F32).astype(BF16)
    column = lax.dot_general(eye, pair, NT, preferred_element_type=F32).astype(jnp.int32)
    goal, rank = column[:, 0:1], column[:, 1:2]
    slots = members * BOX
    at = iota((rows, slots), 1)
    pick_low = (at == jnp.where(rank < PART, goal * BOX + rank, -1)).astype(BF16)
    pick_high = (at == jnp.where(rank >= PART, goal * BOX + rank - PART, -1)).astype(BF16)
    pltpu.make_async_copy(t_own, low, sem.at[0]).wait()
    pltpu.make_async_copy(t_own, high, sem.at[1]).wait()
    total = jnp.dot(pick_low, low[...], preferred_element_type=F32)
    total = total + jnp.dot(pick_high, high[...], preferred_element_type=F32)
    out[...] = total.astype(BF16)


def unpack(members, scal, route, t_own, t_recv, p_own, p_recv):
    slots, d = t_own.shape
    rows = route.shape[1]
    return pl.pallas_call(
        lambda *refs: unpack_kernel(members, *refs),
        out_shape=jax.ShapeDtypeStruct((rows, d), BF16),
        in_specs=[smem(), vmem()] + [anywhere()] * 4,
        out_specs=vmem(),
        scratch_shapes=[pltpu.VMEM((slots, d), BF16), pltpu.VMEM((slots, d), BF16), pltpu.SemaphoreType.DMA((2,))],
        compiler_params=params(),
        name="unpack",
    )(scal, route, t_own, t_recv, p_own, p_recv)


def swap(value):
    return lax.ppermute(value, "half", SWAP)


def spread(value):
    members = lax.axis_size("ep")
    shape = value.shape
    boxes = value.reshape((members, -1) + shape[-1:])
    return lax.all_to_all(boxes, "ep", split_axis=0, concat_axis=0, tiled=True).reshape(shape)


def shards(activations, routes, blocks, row_scale, gate_up, down_weight, slot_map):
    members = lax.axis_size("ep")
    tokens = activations[0]
    row_count = tokens.shape[0]
    route = routes.reshape(1, row_count)
    gate_up, down_weight = gate_up[0], down_weight[0]
    scal = jnp.stack([lax.axis_index("half"), lax.axis_index("ep")]).astype(jnp.int32)
    eta = 0.03 / math.sqrt(row_count)

    tokens_b, route_b, scale_b, blocks_b = swap(tokens), swap(route), swap(row_scale), swap(blocks)
    parts = (scal, tokens, tokens_b, route, route_b, row_scale, scale_b)
    train_rows = spread(pack(0, members, *parts))
    serve_rows = spread(pack(1, members, *parts))

    down_own, down_send, gate_own, gate_send, both_grad = train(
        scal, blocks, blocks_b, train_rows, gate_up, down_weight
    )
    new_down = update_down(eta, scal, down_own, swap(down_send), down_weight)
    high, wide = new_down.shape[2:]
    down_pieces = spread(new_down.reshape(members * high, wide)).reshape(members, high, wide)
    new_gate = update_gate(eta, scal, gate_own, swap(gate_send), gate_up)
    gate_pieces = spread(new_gate).reshape(members, -1, new_gate.shape[1])
    both_grad, _ = lax.optimization_barrier((both_grad, new_gate))
    input_grad = lax.dot_general(both_grad, gate_up, NT, preferred_element_type=F32).astype(BF16)
    train_back = spread(input_grad)
    train_other = swap(train_back)

    slot_down = spread(choose("choose_down", slot_map, down_pieces).reshape(members * high, wide))
    slot_down = slot_down.reshape(new_down.shape)
    down_other = swap(slot_down)
    slot_gate = spread(choose("choose_gate", slot_map, gate_pieces).reshape(new_gate.shape))
    gate_other = swap(slot_gate)
    served = serve(scal, blocks, blocks_b, serve_rows, slot_gate, gate_other, slot_down, down_other)
    serve_back = spread(served)
    serve_other = swap(serve_back)
    return unpack(members, scal, route, train_back, train_other, serve_back, serve_other)[None]


def solution(mesh):
    placed = (
        P("half", "ep", None),
        P("half", "ep", None),
        P("half", None),
        P("half", "ep"),
        P("ep", None, None),
        P("ep", None, None),
        P(),
    )
    return jax.shard_map(
        shards, mesh=mesh, in_specs=placed, out_specs=P("half", "ep", None), check_vma=False
    )
```

time: 913 us -> 357 us (0.39)
  blocking collectives: 401 us -> 0 us
  waiting for transfers between devices: 341 us -> 134 us
  Pallas kernels: 0 us -> 118 us
  local copies, waits for them, and re-layouts: 67 us -> 9.87 us
  starting transfers between devices: 42.4 us -> 84.8 us
  other arithmetic: 20.5 us -> 0.64 us
  matrix products: 24.3 us -> 8.09 us
    unnamed x1 -> x0, blocking collectives: 296 us -> none
    pallas_call x0 -> x9, Pallas kernels: none -> 118 us  [the longest x2 56 us: choose(): pl.pallas_call(choose_kernel, out_shape=jax.ShapeDtypeStruct(pieces.shape...]
    ppermute x2 -> x10, waiting for transfers between devices: 120 us -> 13.6 us  [swap(): return lax.ppermute(value, 'half', SWAP)]
    all_to_all x2 -> x0, blocking collectives: 105 us -> none  [the longest x1 56.9 us: relay_weights(): lax.all_to_all(pieces_down, 'ep', split_axis=0, concat_axis=0, tiled=True)]
    all_to_all x5 -> x8, waiting for transfers between devices: 221 us -> 120 us  [spread(): lax.all_to_all(boxes, 'ep', split_axis=0, concat_axis=0, tiled=True)]
    reshape x7 -> x0, local copies, waits for them, and re-layouts: 36.5 us -> none  [the longest x1 6.15 us: relay_weights(): whole_down.reshape(down_part.shape)]
    ppermute x2 -> x10, starting transfers between devices: 2.57 us -> 25.9 us  [swap(): return lax.ppermute(value, 'half', SWAP)]
    all_to_all x5 -> x8, starting transfers between devices: 39.8 us -> 58.9 us  [spread(): lax.all_to_all(boxes, 'ep', split_axis=0, concat_axis=0, tiled=True)]
  transfers between devices with their start and end apart: 7 -> 18, of which waited for: 5 -> 12; matrix products, arithmetic and copies ran while one was open for 4% -> 2% of each run, Pallas kernels for 0% -> 24%
where the time goes in v1:
time: 357 us; the launch traced here: 356 us
  waiting for transfers between devices  134 us (38%)
  Pallas kernels  118 us (33%)
  starting transfers between devices  84.8 us (24%)
  local copies, waits for them, and re-layouts  9.87 us (3%)
  matrix products  8.09 us (2%)
    all_to_all x8, waiting for transfers between devices, spread(): lax.all_to_all(boxes, 'ep', split_axis=0, concat_axis=0, tiled=True)  120 us
    all_to_all x8, starting transfers between devices, spread(): lax.all_to_all(boxes, 'ep', split_axis=0, concat_axis=0, tiled=True)  58.9 us
    pallas_call x2, Pallas kernels, choose(): pl.pallas_call(choose_kernel, out_shape=jax.ShapeDtypeStruct(pieces.shape...  56 us
    ppermute x10, starting transfers between devices, swap(): return lax.ppermute(value, 'half', SWAP)  25.9 us
    pallas_call x1, Pallas kernels, train(): pl.pallas_call(train_kernel, out_shape=(dg, dg, gg, gg, jax.ShapeDtypeStr...  22.1 us
    ppermute x10, waiting for transfers between devices, swap(): return lax.ppermute(value, 'half', SWAP)  13.6 us
    pallas_call x1, Pallas kernels, serve(): pl.pallas_call(serve_kernel, out_shape=jax.ShapeDtypeStruct((slots, d), B...  11.8 us
    pallas_call x2, Pallas kernels, pack(): pl.pallas_call(lambda *refs: pack_kernel(group, members, *refs), out_shap...  10.3 us
  transfers between devices with their start and end apart: 18, of which 12 were waited for; matrix products, arithmetic and copies ran while one was open for 2% of the time, Pallas kernels for 24%

profile of v1, /device:TPU:1, one launch (start us, length us, event | category | flops | bytes accessed | tf_op | source)
XLA Modules:
  0.0 356.2 jit_solution(3095425431329101955)
XLA Ops:
  6.8 5.2 %pack0.1 = bf16[512,2048]{1,0:T(8,128)(2,1)} custom-call(s32[2]{0:T(128)} %pad_add_fusion.refs_0_.scal, bf16[448,2048]{1,0:T(8,128)(2,1)} %bitcast.38, bf16[448,2048]{1,0:T(8,128)(2,1)} %copy-done.6, s32[1,448]{1,0:T(1,128)} %bitcast.42, s32[1,448]{1,0:T(1,128)} %copy-done.10, bf16[1,448]{1,0:T(2,128)(2,1)} %refs_5_.3, bf16[1,448]{1,0:T(2,128)(2,1)} %copy-done.11), custom_call_target="tpu_custom_call" | custom-call | tf_op jit(solution)/shard_map/pack0/pallas_call | solution.py:84
  12.0 11.3 %all-to-all-start = ((bf16[64,8,2048]{2,1,0:T(8,128)(2,1)}), bf16[64,8,2048]{2,1,0:T(8,128)(2,1)S(1)}, u32[]{:S(2)}, u32[]{:S(2)}) async-start(bf16[64,8,2048]{2,1,0:T(8,128)(2,1)} %bitcast.31), calls=%async_computation | async-start | bytes 4194304 | tf_op jit(solution)/shard_map/all_to_all | solution.py:454
  24.9 26.5 %all-to-all-done = bf16[64,8,2048]{2,1,0:T(8,128)(2,1)S(1)} async-done(((bf16[64,8,2048]{2,1,0:T(8,128)(2,1)}), bf16[64,8,2048]{2,1,0:T(8,128)(2,1)S(1)}, u32[]{:S(2)}, u32[]{:S(2)}) %all-to-all-start) | async-done | bytes 2097184 | tf_op jit(solution)/shard_map/all_to_all | solution.py:454
  52.7 22.1 %train.1 = (bf16[384,2048]{1,0:T(8,128)(2,1)}, bf16[384,2048]{1,0:T(8,128)(2,1)}, bf16[1024,1536]{1,0:T(8,128)(2,1)}, bf16[1024,1536]{1,0:T(8,128)(2,1)}, bf16[512,1536]{1,0:T(8,128)(2,1)}) custom-call(s32[2]{0:T(128)} %pad_add_fusion.refs_0_.scal, s32[1,64]{1,0:T(1,128)} %blocks_a.3, s32[1,64]{1,0:T(1,128)} %copy-done.13, bf16[512,2048]{1,0:T(8,128)(2,1)} %bitcast.35, ...), custom_call_target="tpu_custom_call" | custom-call | tf_op jit(solution)/shard_map/train/pallas_call | solution.py:237
  74.8 2.7 collective-permute-start.4
  77.5 5.1 %pack1.1 = bf16[512,2048]{1,0:T(8,128)(2,1)} custom-call(s32[2]{0:T(128)} %pad_add_fusion.refs_0_.scal, bf16[448,2048]{1,0:T(8,128)(2,1)} %bitcast.39, bf16[448,2048]{1,0:T(8,128)(2,1)} %copy-done.6, s32[1,448]{1,0:T(1,128)} %bitcast.43, s32[1,448]{1,0:T(1,128)} %copy-done.10, bf16[1,448]{1,0:T(2,128)(2,1)} %refs_5_.3, bf16[1,448]{1,0:T(2,128)(2,1)} %copy-done.11), custom_call_target="tpu_custom_call" | custom-call | tf_op jit(solution)/shard_map/pack1/pallas_call | solution.py:84
  82.6 6.1 %all-to-all-start.2 = ((bf16[64,8,2048]{2,1,0:T(8,128)(2,1)}), bf16[64,8,2048]{2,1,0:T(8,128)(2,1)S(1)}, u32[]{:S(2)}, u32[]{:S(2)}) async-start(bf16[64,8,2048]{2,1,0:T(8,128)(2,1)} %bitcast.30), calls=%async_computation.2 | async-start | bytes 4194304 | tf_op jit(solution)/shard_map/all_to_all | solution.py:454
  88.7 6.8 %update_gate.1 = bf16[1024,1536]{1,0:T(8,128)(2,1)} custom-call(s32[2]{0:T(128)} %pad_add_fusion.refs_0_.scal, bf16[1024,1536]{1,0:T(8,128)(2,1)} %get-tuple-element.12.refs_1_, bf16[1024,1536]{1,0:T(8,128)(2,1)} %collective-permute-done.4.refs_2_, bf16[2048,1536]{1,0:T(8,128)(2,1)} %bitcast.24), custom_call_target="tpu_custom_call" | custom-call | tf_op jit(solution)/shard_map/update_gate/pallas_call | solution.py:290
  95.6 21.9 %all-to-all-done.2 = bf16[64,8,2048]{2,1,0:T(8,128)(2,1)S(1)} async-done(((bf16[64,8,2048]{2,1,0:T(8,128)(2,1)}), bf16[64,8,2048]{2,1,0:T(8,128)(2,1)S(1)}, u32[]{:S(2)}, u32[]{:S(2)}) %all-to-all-start.2) | async-done | bytes 2097184 | tf_op jit(solution)/shard_map/all_to_all | solution.py:454
  118.9 6.1 %all-to-all-start.3 = ((bf16[64,16,1536]{2,1,0:T(8,128)(2,1)}), bf16[64,16,1536]{2,1,0:T(8,128)(2,1)S(1)}, u32[]{:S(2)}, u32[]{:S(2)}) async-start(bf16[64,16,1536]{2,1,0:T(8,128)(2,1)} %bitcast.27), calls=%async_computation.3 | async-start | bytes 6291456 | tf_op jit(solution)/shard_map/all_to_all | solution.py:454
  127.0 3.2 collective-permute-done.7.refs_2_
  131.4 5.1 %update_down.1 = bf16[8,8,48,256]{3,2,1,0:T(8,128)(2,1)} custom-call(s32[2]{0:T(128)} %pad_add_fusion.refs_0_.scal, bf16[384,2048]{1,0:T(8,128)(2,1)} %get-tuple-element.15.refs_1_, bf16[384,2048]{1,0:T(8,128)(2,1)} %copy-done.9, bf16[768,2048]{1,0:T(8,128)(2,1)} %bitcast.29), custom_call_target="tpu_custom_call" | custom-call | tf_op jit(solution)/shard_map/update_down/pallas_call | solution.py:267
  136.5 27.2 %all-to-all-done.3.src = bf16[64,16,1536]{2,1,0:T(8,128)(2,1)S(1)} async-done(((bf16[64,16,1536]{2,1,0:T(8,128)(2,1)}), bf16[64,16,1536]{2,1,0:T(8,128)(2,1)S(1)}, u32[]{:S(2)}, u32[]{:S(2)}) %all-to-all-start.3) | async-done | bytes 3145760 | tf_op jit(solution)/shard_map/all_to_all | solution.py:454
  163.7 7.4 %all-to-all-start.5 = ((bf16[64,48,256]{2,1,0:T(8,128)(2,1)}), bf16[64,48,256]{2,1,0:T(8,128)(2,1)}, u32[]{:S(2)}, u32[]{:S(2)}) async-start(bf16[64,48,256]{2,1,0:T(8,128)(2,1)} %bitcast.40), calls=%async_computation.5 | async-start | bytes 3145728 | tf_op jit(solution)/shard_map/all_to_all | solution.py:454
  171.2 6.2 %choose_gate.1 = bf16[64,16,1536]{2,1,0:T(8,128)(2,1)S(1)} custom-call(s32[64]{0:T(128)S(1)} %copy-done.1, bf16[64,16,1536]{2,1,0:T(8,128)(2,1)S(1)} %all-to-all-done.3.src), custom_call_target="tpu_custom_call" | custom-call | tf_op jit(solution)/shard_map/choose_gate/pallas_call | solution.py:323
  179.0 13.5 %all-to-all-done.5.src = bf16[64,48,256]{2,1,0:T(8,128)(2,1)} async-done(((bf16[64,48,256]{2,1,0:T(8,128)(2,1)}), bf16[64,48,256]{2,1,0:T(8,128)(2,1)}, u32[]{:S(2)}, u32[]{:S(2)}) %all-to-all-start.5) | async-done | bytes 1572896 | tf_op jit(solution)/shard_map/all_to_all | solution.py:454
  192.5 4.7 %all-to-all-start.4 = ((bf16[64,16,1536]{2,1,0:T(8,128)(2,1)}), bf16[64,16,1536]{2,1,0:T(8,128)(2,1)S(1)}, u32[]{:S(2)}, u32[]{:S(2)}) async-start(bf16[64,16,1536]{2,1,0:T(8,128)(2,1)} %copy-done), calls=%async_computation.4 | async-start | bytes 6291456 | tf_op jit(solution)/shard_map/all_to_all | solution.py:454
  197.2 49.9 %choose_down.1 = bf16[64,48,256]{2,1,0:T(8,128)(2,1)} custom-call(s32[64]{0:T(128)S(1)} %copy-done.1, bf16[64,48,256]{2,1,0:T(8,128)(2,1)} %all-to-all-done.5.src), custom_call_target="tpu_custom_call" | custom-call | tf_op jit(solution)/shard_map/choose_down/pallas_call | solution.py:323
  247.1 10.0 %all-to-all-start.6 = ((bf16[64,48,256]{2,1,0:T(8,128)(2,1)}), bf16[64,48,256]{2,1,0:T(8,128)(2,1)}, u32[]{:S(2)}, u32[]{:S(2)}) async-start(bf16[64,48,256]{2,1,0:T(8,128)(2,1)} %choose_down.1), calls=%async_computation.6 | async-start | bytes 3145728 | tf_op jit(solution)/shard_map/all_to_all | solution.py:454
  257.2 5.0 %collective-permute-start.6 = (bf16[1024,1536]{1,0:T(8,128)(2,1)S(1)}, bf16[1024,1536]{1,0:T(8,128)(2,1)}, u32[]{:S(2)}, u32[]{:S(2)}) collective-permute-start(bf16[1024,1536]{1,0:T(8,128)(2,1)S(1)} %bitcast.25), channel_id=1, source_target_pairs={{0,64},{64,0},{1,65},{65,1},{2,66},{66,2},{3,67},{67,3},{4,68},{68... | collective-permute-start | bytes 9437192 | tf_op jit(solution)/shard_map/ppermute | solution.py:447
  262.1 8.1 %fusion = bf16[64,8,2048]{2,1,0:T(8,128)(2,1)} fusion(bf16[512,1536]{1,0:T(8,128)(2,1)} %get-tuple-element.14, bf16[1,2048,1536]{2,1,0:T(8,128)(2,1)} %param.11), kind=kOutput, calls=%fused_computation.1 | convolution fusion | flops 3222274048 | bytes 9961472 | tf_op jit(solution)/shard_map/dot_general | solution.py:480
  270.2 6.2 %all-to-all-done.6 = bf16[64,48,256]{2,1,0:T(8,128)(2,1)} async-done(((bf16[64,48,256]{2,1,0:T(8,128)(2,1)}), bf16[64,48,256]{2,1,0:T(8,128)(2,1)}, u32[]{:S(2)}, u32[]{:S(2)}) %all-to-all-start.6) | async-done | bytes 1572896 | tf_op jit(solution)/shard_map/all_to_all | solution.py:454
  276.4 5.6 %all-to-all-start.1 = ((bf16[64,8,2048]{2,1,0:T(8,128)(2,1)}), bf16[64,8,2048]{2,1,0:T(8,128)(2,1)}, u32[]{:S(2)}, u32[]{:S(2)}) async-start(bf16[64,8,2048]{2,1,0:T(8,128)(2,1)} %fusion), calls=%async_computation.1 | async-start | bytes 4194304 | tf_op jit(solution)/shard_map/all_to_all | solution.py:454
  282.0 5.8 %collective-permute-start.8 = (bf16[8,8,48,256]{3,2,1,0:T(8,128)(2,1)}, bf16[8,8,48,256]{3,2,1,0:T(8,128)(2,1)S(1)}, u32[]{:S(2)}, u32[]{:S(2)}) collective-permute-start(bf16[8,8,48,256]{3,2,1,0:T(8,128)(2,1)} %bitcast.15.dw_a), channel_id=1, source_target_pairs={{0,64},{64,0},{1,65},{65,1},{2,66},{66,2},{3,67},{67,3},{4,68},{68... | collective-permute-start | bytes 4718600 | tf_op jit(solution)/shard_map/ppermute | solution.py:447
  287.8 3.2 collective-permute-done.8.dw_b
  292.2 11.8 %serve.1 = bf16[512,2048]{1,0:T(8,128)(2,1)} custom-call(s32[2]{0:T(128)} %pad_add_fusion.refs_0_.scal, s32[1,64]{1,0:T(1,128)} %blocks_a.3, s32[1,64]{1,0:T(1,128)} %copy-done.13, bf16[512,2048]{1,0:T(8,128)(2,1)} %bitcast.32, bf16[1024,1536]{1,0:T(8,128)(2,1)} %bitcast.26, bf16[1024,1536]{1,0:T(8,128)(2,1)} %collective-permute-done.6.gu_b, ...), custom_call_target="tpu_custom_call" | custom-call | tf_op jit(solution)/shard_map/serve/pallas_call | solution.py:387
  306.2 7.8 %all-to-all-start.7 = ((bf16[64,8,2048]{2,1,0:T(8,128)(2,1)}), bf16[64,8,2048]{2,1,0:T(8,128)(2,1)S(1)}, u32[]{:S(2)}, u32[]{:S(2)}) async-start(bf16[64,8,2048]{2,1,0:T(8,128)(2,1)} %bitcast.36), calls=%async_computation.7 | async-start | bytes 4194304 | tf_op jit(solution)/shard_map/all_to_all | solution.py:454
  314.0 4.0 %collective-permute-start.5 = (bf16[512,2048]{1,0:T(8,128)(2,1)}, bf16[512,2048]{1,0:T(8,128)(2,1)}, u32[]{:S(2)}, u32[]{:S(2)}) collective-permute-start(bf16[512,2048]{1,0:T(8,128)(2,1)} %bitcast.9.refs_2_), channel_id=1, source_target_pairs={{0,64},{64,0},{1,65},{65,1},{2,66},{66,2},{3,67},{67,3},{4,68},{68... | collective-permute-start | bytes 6291464 | tf_op jit(solution)/shard_map/ppermute | solution.py:447
  318.0 22.8 %all-to-all-done.7 = bf16[64,8,2048]{2,1,0:T(8,128)(2,1)S(1)} async-done(((bf16[64,8,2048]{2,1,0:T(8,128)(2,1)}), bf16[64,8,2048]{2,1,0:T(8,128)(2,1)S(1)}, u32[]{:S(2)}, u32[]{:S(2)}) %all-to-all-start.7) | async-done | bytes 2097184 | tf_op jit(solution)/shard_map/all_to_all | solution.py:454
  340.9 3.8 %collective-permute-start.9 = (bf16[512,2048]{1,0:T(8,128)(2,1)S(1)}, bf16[512,2048]{1,0:T(8,128)(2,1)S(1)}, u32[]{:S(2)}, u32[]{:S(2)}) collective-permute-start(bf16[512,2048]{1,0:T(8,128)(2,1)S(1)} %bitcast.33), channel_id=1, source_target_pairs={{0,64},{64,0},{1,65},{65,1},{2,66},{66,2},{3,67},{67,3},{4,68},{68... | collective-permute-start | bytes 6291464 | tf_op jit(solution)/shard_map/ppermute | solution.py:447
  344.6 3.8 %collective-permute-done.9.refs_5_ = bf16[512,2048]{1,0:T(8,128)(2,1)S(1)} collective-permute-done((bf16[512,2048]{1,0:T(8,128)(2,1)S(1)}, bf16[512,2048]{1,0:T(8,128)(2,1)S(1)}, u32[]{:S(2)}, u32[]{:S(2)}) %collective-permute-start.9) | collective-permute-done | bytes 2097184 | tf_op jit(solution)/shard_map/ppermute | solution.py:447
  349.8 6.2 %unpack.1 = bf16[448,2048]{1,0:T(8,128)(2,1)} custom-call(s32[2]{0:T(128)} %pad_add_fusion.refs_0_.scal, s32[1,448]{1,0:T(1,128)} %bitcast.44, bf16[512,2048]{1,0:T(8,128)(2,1)} %bitcast.9.refs_2_, bf16[512,2048]{1,0:T(8,128)(2,1)} %collective-permute-done.5.refs_3_, bf16[512,2048]{1,0:T(8,128)(2,1)} %bitcast.34, bf16[512,2048]{1,0:T(8,128)(2,1)} %copy-done.7), custom_call_target="tpu_custom_call" | custom-call | tf_op jit(solution)/shard_map/unpack/pallas_call | solution.py:435
  (43 shorter events, 20.7 us)
Async XLA Ops:
  0.0 5.0 %collective-permute-start.1 = (bf16[448,2048]{1,0:T(8,128)(2,1)}, bf16[448,2048]{1,0:T(8,128)(2,1)S(1)}, u32[]{:S(2)}, u32[]{:S(2)}) collective-permute-start(bf16[448,2048]{1,0:T(8,128)(2,1)} %bitcast.37), channel_id=1, source_target_pairs={{0,64},{64,0},{1,65},{65,1},{2,66},{66,2},{3,67},{67,3},{4,68},{68... | collective-permute-start | bytes 5505032 | tf_op jit(solution)/shard_map/ppermute | solution.py:447
  1.4 3.6 %collective-permute-start.2 = (s32[1,448]{1,0:T(1,128)}, s32[1,448]{1,0:T(1,128)S(1)}, u32[]{:S(2)}, u32[]{:S(2)}) collective-permute-start(s32[1,448]{1,0:T(1,128)} %bitcast.41), channel_id=1, source_target_pairs={{0,64},{64,0},{1,65},{65,1},{2,66},{66,2},{3,67},{67,3},{4,68},{68... | collective-permute-start | bytes 5384 | tf_op jit(solution)/shard_map/ppermute | solution.py:447
  1.4 3.6 %collective-permute-start.3 = (bf16[1,448]{1,0:T(2,128)(2,1)}, bf16[1,448]{1,0:T(2,128)(2,1)S(1)}, u32[]{:S(2)}, u32[]{:S(2)}) collective-permute-start(bf16[1,448]{1,0:T(2,128)(2,1)} %refs_5_.3), channel_id=1, source_target_pairs={{0,64},{64,0},{1,65},{65,1},{2,66},{66,2},{3,67},{67,3},{4,68},{68... | collective-permute-start | bytes 2696 | tf_op jit(solution)/shard_map/ppermute | solution.py:447
  5.0 0.6 copy-start.11
  5.0 0.6 copy-start.10
  5.6 1.2 copy-start.6
  12.0 11.3 %copy-start.12 = (s32[1,64]{1,0:T(1,128)S(1)}, s32[1,64]{1,0:T(1,128)}, u32[]{:S(2)}) copy-start(s32[1,64]{1,0:T(1,128)} %blocks_a.3) | copy-start | bytes 772
  12.0 39.3 %all-to-all-start = ((bf16[64,8,2048]{2,1,0:T(8,128)(2,1)}), bf16[64,8,2048]{2,1,0:T(8,128)(2,1)S(1)}, u32[]{:S(2)}, u32[]{:S(2)}) async-start(bf16[64,8,2048]{2,1,0:T(8,128)(2,1)} %bitcast.31), calls=%async_computation | async-start | bytes 4194304 | tf_op jit(solution)/shard_map/all_to_all | solution.py:454
  23.3 1.6 collective-permute-start
  24.9 26.5 %copy-start.13 = (s32[1,64]{1,0:T(1,128)}, s32[1,64]{1,0:T(1,128)S(1)}, u32[]{:S(2)}) copy-start(s32[1,64]{1,0:T(1,128)S(1)} %collective-permute-done.blocks_b) | copy-start | bytes 772
  51.3 1.4 copy-start.5
  74.8 13.9 %collective-permute-start.4 = (bf16[1024,1536]{1,0:T(8,128)(2,1)}, bf16[1024,1536]{1,0:T(8,128)(2,1)}, u32[]{:S(2)}, u32[]{:S(2)}) collective-permute-start(bf16[1024,1536]{1,0:T(8,128)(2,1)} %get-tuple-element.13), channel_id=1, source_target_pairs={{0,64},{64,0},{1,65},{65,1},{2,66},{66,2},{3,67},{67,3},{4,68},{68... | collective-permute-start | bytes 9437192 | tf_op jit(solution)/shard_map/ppermute | solution.py:447
  82.6 34.8 %all-to-all-start.2 = ((bf16[64,8,2048]{2,1,0:T(8,128)(2,1)}), bf16[64,8,2048]{2,1,0:T(8,128)(2,1)S(1)}, u32[]{:S(2)}, u32[]{:S(2)}) async-start(bf16[64,8,2048]{2,1,0:T(8,128)(2,1)} %bitcast.30), calls=%async_computation.2 | async-start | bytes 4194304 | tf_op jit(solution)/shard_map/all_to_all | solution.py:454
  117.5 1.4 copy-start.3
  118.9 44.8 %all-to-all-start.3 = ((bf16[64,16,1536]{2,1,0:T(8,128)(2,1)}), bf16[64,16,1536]{2,1,0:T(8,128)(2,1)S(1)}, u32[]{:S(2)}, u32[]{:S(2)}) async-start(bf16[64,16,1536]{2,1,0:T(8,128)(2,1)} %bitcast.27), calls=%async_computation.3 | async-start | bytes 6291456 | tf_op jit(solution)/shard_map/all_to_all | solution.py:454
  125.0 5.3 %collective-permute-start.7 = (bf16[384,2048]{1,0:T(8,128)(2,1)}, bf16[384,2048]{1,0:T(8,128)(2,1)S(1)}, u32[]{:S(2)}, u32[]{:S(2)}) collective-permute-start(bf16[384,2048]{1,0:T(8,128)(2,1)} %get-tuple-element.16), channel_id=1, source_target_pairs={{0,64},{64,0},{1,65},{65,1},{2,66},{66,2},{3,67},{67,3},{4,68},{68... | collective-permute-start | bytes 4718600 | tf_op jit(solution)/shard_map/ppermute | solution.py:447
  130.2 1.1 copy-start.9
  136.5 34.6 %copy-start.1 = (s32[64]{0:T(128)S(1)}, s32[64]{0:T(128)}, u32[]{:S(2)}) copy-start(s32[64]{0:T(128)} %slot_map.3) | copy-start | bytes 772
  163.7 28.8 %all-to-all-start.5 = ((bf16[64,48,256]{2,1,0:T(8,128)(2,1)}), bf16[64,48,256]{2,1,0:T(8,128)(2,1)}, u32[]{:S(2)}, u32[]{:S(2)}) async-start(bf16[64,48,256]{2,1,0:T(8,128)(2,1)} %bitcast.40), calls=%async_computation.5 | async-start | bytes 3145728 | tf_op jit(solution)/shard_map/all_to_all | solution.py:454
  177.3 1.6 copy-start
  192.5 54.6 %all-to-all-start.4 = ((bf16[64,16,1536]{2,1,0:T(8,128)(2,1)}), bf16[64,16,1536]{2,1,0:T(8,128)(2,1)S(1)}, u32[]{:S(2)}, u32[]{:S(2)}) async-start(bf16[64,16,1536]{2,1,0:T(8,128)(2,1)} %copy-done), calls=%async_computation.4 | async-start | bytes 6291456 | tf_op jit(solution)/shard_map/all_to_all | solution.py:454
  247.1 23.1 %copy-start.2 = (bf16[64,16,1536]{2,1,0:T(8,128)(2,1)}, bf16[64,16,1536]{2,1,0:T(8,128)(2,1)S(1)}, u32[]{:S(2)}) copy-start(bf16[64,16,1536]{2,1,0:T(8,128)(2,1)S(1)} %all-to-all-done.4) | copy-start | bytes 9437188
  247.1 29.3 %all-to-all-start.6 = ((bf16[64,48,256]{2,1,0:T(8,128)(2,1)}), bf16[64,48,256]{2,1,0:T(8,128)(2,1)}, u32[]{:S(2)}, u32[]{:S(2)}) async-start(bf16[64,48,256]{2,1,0:T(8,128)(2,1)} %choose_down.1), calls=%async_computation.6 | async-start | bytes 3145728 | tf_op jit(solution)/shard_map/all_to_all | solution.py:454
  257.2 33.9 %collective-permute-start.6 = (bf16[1024,1536]{1,0:T(8,128)(2,1)S(1)}, bf16[1024,1536]{1,0:T(8,128)(2,1)}, u32[]{:S(2)}, u32[]{:S(2)}) collective-permute-start(bf16[1024,1536]{1,0:T(8,128)(2,1)S(1)} %bitcast.25), channel_id=1, source_target_pairs={{0,64},{64,0},{1,65},{65,1},{2,66},{66,2},{3,67},{67,3},{4,68},{68... | collective-permute-start | bytes 9437192 | tf_op jit(solution)/shard_map/ppermute | solution.py:447
  276.4 29.8 %all-to-all-start.1 = ((bf16[64,8,2048]{2,1,0:T(8,128)(2,1)}), bf16[64,8,2048]{2,1,0:T(8,128)(2,1)}, u32[]{:S(2)}, u32[]{:S(2)}) async-start(bf16[64,8,2048]{2,1,0:T(8,128)(2,1)} %fusion), calls=%async_computation.1 | async-start | bytes 4194304 | tf_op jit(solution)/shard_map/all_to_all | solution.py:454
  282.0 9.0 %collective-permute-start.8 = (bf16[8,8,48,256]{3,2,1,0:T(8,128)(2,1)}, bf16[8,8,48,256]{3,2,1,0:T(8,128)(2,1)S(1)}, u32[]{:S(2)}, u32[]{:S(2)}) collective-permute-start(bf16[8,8,48,256]{3,2,1,0:T(8,128)(2,1)} %bitcast.15.dw_a), channel_id=1, source_target_pairs={{0,64},{64,0},{1,65},{65,1},{2,66},{66,2},{3,67},{67,3},{4,68},{68... | collective-permute-start | bytes 4718600 | tf_op jit(solution)/shard_map/ppermute | solution.py:447
  291.1 1.1 copy-start.8
  306.2 34.6 %all-to-all-start.7 = ((bf16[64,8,2048]{2,1,0:T(8,128)(2,1)}), bf16[64,8,2048]{2,1,0:T(8,128)(2,1)S(1)}, u32[]{:S(2)}, u32[]{:S(2)}) async-start(bf16[64,8,2048]{2,1,0:T(8,128)(2,1)} %bitcast.36), calls=%async_computation.7 | async-start | bytes 4194304 | tf_op jit(solution)/shard_map/all_to_all | solution.py:454
  314.0 30.6 %collective-permute-start.5 = (bf16[512,2048]{1,0:T(8,128)(2,1)}, bf16[512,2048]{1,0:T(8,128)(2,1)}, u32[]{:S(2)}, u32[]{:S(2)}) collective-permute-start(bf16[512,2048]{1,0:T(8,128)(2,1)} %bitcast.9.refs_2_), channel_id=1, source_target_pairs={{0,64},{64,0},{1,65},{65,1},{2,66},{66,2},{3,67},{67,3},{4,68},{68... | collective-permute-start | bytes 6291464 | tf_op jit(solution)/shard_map/ppermute | solution.py:447
  340.9 7.6 %copy-start.4 = (bf16[64,8,2048]{2,1,0:T(8,128)(2,1)}, bf16[64,8,2048]{2,1,0:T(8,128)(2,1)S(1)}, u32[]{:S(2)}) copy-start(bf16[64,8,2048]{2,1,0:T(8,128)(2,1)S(1)} %all-to-all-done.7) | copy-start | bytes 6291460
  340.9 7.6 %collective-permute-start.9 = (bf16[512,2048]{1,0:T(8,128)(2,1)S(1)}, bf16[512,2048]{1,0:T(8,128)(2,1)S(1)}, u32[]{:S(2)}, u32[]{:S(2)}) collective-permute-start(bf16[512,2048]{1,0:T(8,128)(2,1)S(1)} %bitcast.33), channel_id=1, source_target_pairs={{0,64},{64,0},{1,65},{65,1},{2,66},{66,2},{3,67},{67,3},{4,68},{68... | collective-permute-start | bytes 6291464 | tf_op jit(solution)/shard_map/ppermute | solution.py:447
  348.4 1.3 copy-start.7

commit v2 on v1

v2 whole, which is shorter than its diff:
```python
import math

import jax
import jax.numpy as jnp
from jax import lax
from jax.experimental import pallas as pl
from jax.experimental.pallas import tpu as pltpu
from jax.sharding import PartitionSpec as P


BLK = 128
PART = 7
BOX = 8
COUNT = 8
LANES = 128
SWAP = [(0, 1), (1, 0)]
F32 = jnp.float32
BF16 = jnp.bfloat16
NT = (((1,), (1,)), ((), ()))


def params(mib=56):
    return pltpu.CompilerParams(vmem_limit_bytes=mib << 20)


def iota(shape, dim):
    return lax.broadcasted_iota(jnp.int32, shape, dim)


def anywhere():
    return pl.BlockSpec(memory_space=pl.ANY)


def vmem():
    return pl.BlockSpec(memory_space=pltpu.VMEM)


def smem():
    return pl.BlockSpec(memory_space=pltpu.SMEM)


def order_of(target, members):
    rows = target.shape[1]
    named = iota((members, rows), 0) == target
    onehot = named.astype(BF16)
    upper = (iota((rows, rows), 0) < iota((rows, rows), 1)).astype(BF16)
    before = jnp.dot(onehot, upper, preferred_element_type=F32)
    return jnp.sum(jnp.where(named, before, 0.0), axis=0, keepdims=True).astype(jnp.int32)


def pack_kernel(group, members, scal, tok_a, tok_b, route_a, route_b, scale_a, scale_b, out, tok, sem):
    half = scal[0]
    own = half == group

    @pl.when(own)
    def _():
        pltpu.make_async_copy(tok_a, tok, sem).start()

    @pl.when(jnp.logical_not(own))
    def _():
        pltpu.make_async_copy(tok_b, tok, sem).start()

    target = jnp.where(own, route_a[...], route_b[...])
    scale = jnp.where(own, scale_a[...].astype(F32), scale_b[...].astype(F32))
    rows = target.shape[1]
    slots = members * BOX
    order = order_of(target, members) - PART * half
    inside = (order >= 0) & (order < PART)
    place = jnp.where(inside, target * BOX + order, -1)
    placer = (iota((slots, rows), 0) == place).astype(BF16)
    tags = (iota((slots, rows), 0) == target * BOX + PART).astype(BF16)
    lane = iota((LANES, rows), 0)
    told = jnp.where((lane == order) & inside, scale, jnp.where(lane == COUNT, 1.0, 0.0)).astype(BF16)
    info = lax.dot_general(tags, told, NT, preferred_element_type=F32)
    pltpu.make_async_copy(tok_a, tok, sem).wait()
    first = jnp.dot(placer, tok[:, :LANES], preferred_element_type=F32) + info
    out[:, :LANES] = first.astype(BF16)
    out[:, LANES:] = jnp.dot(placer, tok[:, LANES:], preferred_element_type=F32).astype(BF16)


def pack(group, members, scal, tok_a, tok_b, route_a, route_b, scale_a, scale_b):
    slots = members * BOX
    width = tok_a.shape[1]
    return pl.pallas_call(
        lambda *refs: pack_kernel(group, members, *refs),
        out_shape=jax.ShapeDtypeStruct((slots, width), BF16),
        in_specs=[smem(), anywhere(), anywhere(), vmem(), vmem(), vmem(), vmem()],
        out_specs=vmem(),
        scratch_shapes=[pltpu.VMEM(tok_a.shape, BF16), pltpu.SemaphoreType.DMA],
        compiler_params=params(),
    )(scal, tok_a, tok_b, route_a, route_b, scale_a, scale_b)


def kept_and_scale(head, half, limit):
    slots = head.shape[0]
    row = iota((slots, slots), 0) // BOX
    col = iota((slots, slots), 1)
    tag = (col % BOX) == PART
    mine = (tag & (col // BOX == row)).astype(BF16)
    lower = (tag & (col // BOX < row)).astype(BF16)
    here = jnp.dot(mine, head, preferred_element_type=F32)
    below = jnp.dot(lower, head, preferred_element_type=F32)
    lane = iota((slots, LANES), 1)
    place = iota((slots, LANES), 0) % BOX
    scale = jnp.sum(jnp.where(lane == place, here, 0.0), axis=1, keepdims=True)
    total = jnp.sum(jnp.where(lane == COUNT, here, 0.0), axis=1, keepdims=True)
    ahead = jnp.sum(jnp.where(lane == COUNT, below, 0.0), axis=1, keepdims=True)
    k = iota((slots, 1), 0) % BOX
    index = (k + PART * half).astype(F32)
    kept = (k < PART) & (index < total) & (ahead + index < limit.astype(F32))
    return kept, scale


def limit_of(group, scal, blocks_a, blocks_b):
    own = scal[0] == group
    at = scal[1]
    return jnp.where(own, blocks_a[0, at], blocks_b[0, at]) * BLK


def train_kernel(scal, blocks_a, blocks_b, x_h, gu_h, dw_h, hid_h, og_own, og_send, bg_h,
                 x, gu, dw, gate, up, hid, og, bg, sem):
    half = scal[0]
    d, f2 = gu.shape
    f = f2 // 2
    fc, dc = 256, 512
    nf, nd = f // fc, d // dc

    def load_gu(i, which):
        cols = pl.ds(pl.multiple_of(which * f + i * fc, fc), fc)
        return pltpu.make_async_copy(gu_h.at[:, cols], gu.at[:, cols], sem.at[2 + 2 * i + which])

    load_x = pltpu.make_async_copy(x_h, x, sem.at[0])
    load_dw = pltpu.make_async_copy(dw_h, dw, sem.at[1])
    load_x.start()
    for i in range(nf):
        load_gu(i, 0).start()
        load_gu(i, 1).start()
    load_dw.start()
    load_x.wait()
    kept, scale = kept_and_scale(x[:, :LANES], half, limit_of(0, scal, blocks_a, blocks_b))
    keep = jnp.where(kept, 1.0, 0.0)

    def project(i, _):
        load_gu(i, 0).wait()
        load_gu(i, 1).wait()
        left = pl.ds(pl.multiple_of(i * fc, fc), fc)
        right = pl.ds(pl.multiple_of(f + i * fc, fc), fc)
        g = jnp.dot(x[...], gu[:, left], preferred_element_type=F32)
        u = jnp.dot(x[...], gu[:, right], preferred_element_type=F32)
        gate[:, left] = g
        up[:, left] = u
        hid[:, left] = (keep * (g * jax.nn.sigmoid(g) * u)).astype(BF16)
        return 0

    lax.fori_loop(0, nf, project, 0)
    out_hid = pltpu.make_async_copy(hid, hid_h, sem.at[2 + 2 * nf])
    out_hid.start()
    load_dw.wait()

    def outputs(c, _):
        cols = pl.ds(pl.multiple_of(c * dc, dc), dc)
        o = jnp.dot(hid[...], dw[:, cols], preferred_element_type=F32)
        og[:, cols] = (scale * o).astype(BF16)
        return 0

    lax.fori_loop(0, nd, outputs, 0)

    def out_og(which, place):
        cols = pl.ds(pl.multiple_of(place * (d // 2), d // 2), d // 2)
        return pltpu.make_async_copy(og.at[:, cols], (og_own, og_send)[which], sem.at[3 + 2 * nf + which])

    out_og(0, half).start()
    out_og(1, 1 - half).start()

    def hidden_back(i, _):
        left = pl.ds(pl.multiple_of(i * fc, fc), fc)
        right = pl.ds(pl.multiple_of(f + i * fc, fc), fc)
        hg = lax.dot_general(og[...], dw[left, :], NT, preferred_element_type=F32)
        g = gate[:, left]
        s = jax.nn.sigmoid(g)
        bg[:, left] = (hg * up[:, left] * (s * (1.0 + g * (1.0 - s)))).astype(BF16)
        bg[:, right] = (hg * (g * s)).astype(BF16)
        return 0

    lax.fori_loop(0, nf, hidden_back, 0)
    out_bg = pltpu.make_async_copy(bg, bg_h, sem.at[5 + 2 * nf])
    out_bg.start()
    out_hid.wait()
    out_og(0, half).wait()
    out_og(1, 1 - half).wait()
    out_bg.wait()


def train(scal, blocks_a, blocks_b, x, gate_up, down):
    slots, d = x.shape
    f2 = gate_up.shape[1]
    f = f2 // 2
    half_rows = jax.ShapeDtypeStruct((slots, d // 2), BF16)
    return pl.pallas_call(
        train_kernel,
        out_shape=(
            jax.ShapeDtypeStruct((slots, f), BF16), half_rows, half_rows, jax.ShapeDtypeStruct((slots, f2), BF16)
        ),
        in_specs=[smem(), smem(), smem(), anywhere(), anywhere(), anywhere()],
        out_specs=(anywhere(),) * 4,
        scratch_shapes=[
            pltpu.VMEM((slots, d), BF16), pltpu.VMEM((d, f2), BF16), pltpu.VMEM((f, d), BF16),
            pltpu.VMEM((slots, f), F32), pltpu.VMEM((slots, f), F32), pltpu.VMEM((slots, f), BF16),
            pltpu.VMEM((slots, d), BF16), pltpu.VMEM((slots, f2), BF16),
            pltpu.SemaphoreType.DMA((6 + 2 * (f // 256),)),
        ],
        compiler_params=params(40),
        name="train",
    )(scal, blocks_a, blocks_b, x, gate_up, down)


def update_gate_kernel(eta, scal, x_a, x_b, bg_a, bg_b, gu_h, out, x, x_t, bg, w, stage, sem):
    slots = x.shape[1]
    wide = x.shape[2]
    groups, four, high, cols = stage.shape[1:]
    steps = stage.shape[0]
    mine = pl.ds(pl.multiple_of(scal[0] * wide, wide), wide)
    loads = [
        pltpu.make_async_copy(x_a.at[:, mine], x.at[0], sem.at[0]),
        pltpu.make_async_copy(x_b.at[:, mine], x.at[1], sem.at[1]),
        pltpu.make_async_copy(bg_a, bg.at[pl.ds(0, slots)], sem.at[2]),
        pltpu.make_async_copy(bg_b, bg.at[pl.ds(slots, slots)], sem.at[3]),
        pltpu.make_async_copy(gu_h.at[mine, :], w, sem.at[4]),
    ]
    for load in loads:
        load.start()
    for s in range(2):
        loads[s].wait()

        def turn(c, _):
            part = pl.ds(pl.multiple_of(c * 256, 256), 256)
            x_t[part, s * slots:(s + 1) * slots] = x[s, :, part].T
            return 0

        lax.fori_loop(0, wide // 256, turn, 0)
    for load in loads[2:]:
        load.wait()

    def save(n):
        return pltpu.make_async_copy(stage.at[n], out.at[:, :, pl.ds(pl.multiple_of(n * high, high), high), :], sem.at[5 + n])

    def one(n, _):
        part = pl.ds(pl.multiple_of(n * cols, cols), cols)
        grad = jnp.dot(x_t[...], bg[:, part], preferred_element_type=F32)
        new = (w[:, part].astype(F32) - eta * grad).astype(BF16)
        stage[n] = new.reshape(groups, four, high, cols)
        save(n).start()
        return 0

    lax.fori_loop(0, steps, one, 0)
    for n in range(steps):
        save(n).wait()


def update_gate(eta, scal, x_a, x_b, bg_a, bg_b, gate_up):
    slots, d = x_a.shape
    f2 = bg_a.shape[1]
    wide = d // 2
    high, cols = wide // 64, 256
    steps = f2 // cols
    tall = steps * high + (f2 // 2) // 16
    return pl.pallas_call(
        lambda *refs: update_gate_kernel(eta, *refs),
        out_shape=jax.ShapeDtypeStruct((16, 4, tall, cols), BF16),
        in_specs=[smem()] + [anywhere()] * 5,
        out_specs=anywhere(),
        scratch_shapes=[
            pltpu.VMEM((2, slots, wide), BF16), pltpu.VMEM((wide, 2 * slots), BF16),
            pltpu.VMEM((2 * slots, f2), BF16), pltpu.VMEM((wide, f2), BF16),
            pltpu.VMEM((steps, 16, 4, high, cols), BF16), pltpu.SemaphoreType.DMA((5 + steps,)),
        ],
        compiler_params=params(40),
        name="update_gate",
    )(scal, x_a, x_b, bg_a, bg_b, gate_up)


def update_down_kernel(eta, scal, hid_a, hid_b, og_a, og_b, dw_h, given, out, hid, hid_t, og, w, stage, sem):
    slots = hid.shape[1]
    wide = og.shape[1]
    steps, groups, high, cols = stage.shape
    base = out.shape[2] - high
    mine = pl.ds(pl.multiple_of(scal[0] * wide, wide), wide)
    loads = [
        pltpu.make_async_copy(hid_a, hid.at[0], sem.at[0]),
        pltpu.make_async_copy(hid_b, hid.at[1], sem.at[1]),
        pltpu.make_async_copy(og_a, og.at[pl.ds(0, slots)], sem.at[2]),
        pltpu.make_async_copy(og_b, og.at[pl.ds(slots, slots)], sem.at[3]),
        pltpu.make_async_copy(dw_h.at[:, mine], w, sem.at[4]),
    ]
    for load in loads:
        load.start()
    for s in range(2):
        loads[s].wait()

        def turn(c, _):
            part = pl.ds(pl.multiple_of(c * 256, 256), 256)
            hid_t[part, s * slots:(s + 1) * slots] = hid[s, :, part].T
            return 0

        lax.fori_loop(0, hid.shape[2] // 256, turn, 0)
    for load in loads[2:]:
        load.wait()

    def save(n):
        return pltpu.make_async_copy(stage.at[n], out.at[:, n, pl.ds(base, high), :], sem.at[5 + n])

    def one(n, _):
        part = pl.ds(pl.multiple_of(n * cols, cols), cols)
        grad = jnp.dot(hid_t[...], og[:, part], preferred_element_type=F32)
        new = (w[:, part].astype(F32) - eta * grad).astype(BF16)
        stage[n] = new.reshape(groups, high, cols)
        save(n).start()
        return 0

    lax.fori_loop(0, steps, one, 0)
    for n in range(steps):
        save(n).wait()


def update_down(eta, scal, hid_a, hid_b, og_a, og_b, down, given):
    slots, f = hid_a.shape
    wide = og_a.shape[1]
    cols = given.shape[3]
    steps = wide // cols
    high = f // 16
    return pl.pallas_call(
        lambda *refs: update_down_kernel(eta, *refs),
        out_shape=jax.ShapeDtypeStruct(given.shape, BF16),
        in_specs=[smem()] + [anywhere()] * 6,
        out_specs=anywhere(),
        scratch_shapes=[
            pltpu.VMEM((2, slots, f), BF16), pltpu.VMEM((f, 2 * slots), BF16),
            pltpu.VMEM((2 * slots, wide), BF16), pltpu.VMEM((f, wide), BF16),
            pltpu.VMEM((steps, 16, high, cols), BF16), pltpu.SemaphoreType.DMA((5 + steps,)),
        ],
        input_output_aliases={6: 0},
        compiler_params=params(40),
        name="update_down",
    )(scal, hid_a, hid_b, og_a, og_b, down, given)


def choose_kernel(slot_map, src, out, sem):
    count = out.shape[0]

    def copy(i):
        return pltpu.make_async_copy(src.at[slot_map[i]], out.at[i], sem.at[i])

    def start(i, _):
        copy(i).start()
        return 0

    def wait(i, _):
        copy(i).wait()
        return 0

    lax.fori_loop(0, count, start, 0)
    lax.fori_loop(0, count, wait, 0)


def choose(slot_map, pieces):
    return pl.pallas_call(
        choose_kernel,
        out_shape=jax.ShapeDtypeStruct(pieces.shape, BF16),
        in_specs=[smem(), anywhere()],
        out_specs=vmem(),
        scratch_shapes=[pltpu.SemaphoreType.DMA((pieces.shape[0],))],
        compiler_params=params(16),
        name="choose",
    )(slot_map, pieces)


def serve_kernel(scal, blocks_a, blocks_b, x_h, w_a, w_b, out, x, gu, dw, hid, sem):
    half = scal[0]
    d = x.shape[1]
    high, f2 = gu.shape[3:]
    f = f2 // 2
    fc, dc = 256, 512
    steps = f2 // fc
    deep = dw.shape[1]
    base = w_a.shape[2] - deep

    load_x = pltpu.make_async_copy(x_h, x, sem.at[0])

    def load_gu(s, n):
        src, place = ((w_a, half), (w_b, 1 - half))[s]
        return pltpu.make_async_copy(
            src.at[:, :, pl.ds(n * high, high), :], gu.at[place, :, :, :, pl.ds(n * fc, fc)], sem.at[1 + 2 * n + s]
        )

    def load_dw(s, n):
        src, place = ((w_a, half), (w_b, 1 - half))[s]
        cols = pl.ds(pl.multiple_of(place * (d // 2) + n * fc, fc), fc)
        return pltpu.make_async_copy(
            src.at[:, n, pl.ds(base, deep), :], dw.at[:, :, cols], sem.at[1 + 2 * steps + 2 * n + s]
        )

    load_x.start()
    for n in range(steps):
        for s in range(2):
            load_gu(s, n).start()
    for n in range(4):
        for s in range(2):
            load_dw(s, n).start()
    load_x.wait()
    kept, scale = kept_and_scale(x[:, :LANES], half, limit_of(1, scal, blocks_a, blocks_b))
    for n in range(steps):
        for s in range(2):
            load_gu(s, n).wait()

    def project(i, _):
        left = pl.ds(pl.multiple_of(i * fc, fc), fc)
        right = pl.ds(pl.multiple_of(f + i * fc, fc), fc)
        g = jnp.dot(x[...], gu[:, :, :, :, left].reshape(d, fc), preferred_element_type=F32)
        u = jnp.dot(x[...], gu[:, :, :, :, right].reshape(d, fc), preferred_element_type=F32)
        hid[:, left] = (g * jax.nn.sigmoid(g) * u).astype(BF16)
        return 0

    lax.fori_loop(0, f // fc, project, 0)
    for n in range(4):
        for s in range(2):
            load_dw(s, n).wait()

    def outputs(c, _):
        cols = pl.ds(pl.multiple_of(c * dc, dc), dc)
        o = jnp.dot(hid[...], dw[:, :, cols].reshape(f, dc), preferred_element_type=F32)
        out[:, cols] = jnp.where(kept, scale * o, 0.0).astype(BF16)
        return 0

    lax.fori_loop(0, d // dc, outputs, 0)


def serve(scal, blocks_a, blocks_b, x, w_a, w_b):
    slots, d = x.shape
    f = d * 3 // 8
    high = d // 2 // 64
    steps = 2 * f // 256
    return pl.pallas_call(
        serve_kernel,
        out_shape=jax.ShapeDtypeStruct((slots, d), BF16),
        in_specs=[smem(), smem(), smem()] + [anywhere()] * 3,
        out_specs=vmem(),
        scratch_shapes=[
            pltpu.VMEM((slots, d), BF16), pltpu.VMEM((2, 16, 4, high, 2 * f), BF16), pltpu.VMEM((16, f // 16, d), BF16),
            pltpu.VMEM((slots, f), BF16), pltpu.SemaphoreType.DMA((9 + 2 * steps,)),
        ],
        compiler_params=params(40),
        name="serve",
    )(scal, blocks_a, blocks_b, x, w_a, w_b)


def unpack_kernel(members, scal, route, t_own, t_recv, p_own, p_recv, out, low, high, sem):
    half = scal[0]

    @pl.when(half == 0)
    def _():
        pltpu.make_async_copy(t_own, low, sem.at[0]).start()
        pltpu.make_async_copy(t_recv, high, sem.at[1]).start()

    @pl.when(half == 1)
    def _():
        pltpu.make_async_copy(p_recv, low, sem.at[0]).start()
        pltpu.make_async_copy(p_own, high, sem.at[1]).start()

    target = route[...]
    rows = target.shape[1]
    order = order_of(target, members)
    eye = (iota((rows, rows), 0) == iota((rows, rows), 1)).astype(BF16)
    pair = jnp.where(iota((BOX, rows), 0) == 0, target, order).astype(F32).astype(BF16)
    column = lax.dot_general(eye, pair, NT, preferred_element_type=F32).astype(jnp.int32)
    goal, rank = column[:, 0:1], column[:, 1:2]
    slots = members * BOX
    at = iota((rows, slots), 1)
    pick_low = (at == jnp.where(rank < PART, goal * BOX + rank, -1)).astype(BF16)
    pick_high = (at == jnp.where(rank >= PART, goal * BOX + rank - PART, -1)).astype(BF16)
    pltpu.make_async_copy(t_own, low, sem.at[0]).wait()
    pltpu.make_async_copy(t_own, high, sem.at[1]).wait()
    total = jnp.dot(pick_low, low[...], preferred_element_type=F32)
    total = total + jnp.dot(pick_high, high[...], preferred_element_type=F32)
    out[...] = total.astype(BF16)


def unpack(members, scal, route, t_own, t_recv, p_own, p_recv):
    slots, d = t_own.shape
    rows = route.shape[1]
    return pl.pallas_call(
        lambda *refs: unpack_kernel(members, *refs),
        out_shape=jax.ShapeDtypeStruct((rows, d), BF16),
        in_specs=[smem(), vmem()] + [anywhere()] * 4,
        out_specs=vmem(),
        scratch_shapes=[pltpu.VMEM((slots, d), BF16), pltpu.VMEM((slots, d), BF16), pltpu.SemaphoreType.DMA((2,))],
        compiler_params=params(),
        name="unpack",
    )(scal, route, t_own, t_recv, p_own, p_recv)


def swap(value):
    return lax.ppermute(value, "half", SWAP)


def spread(value):
    return lax.all_to_all(value, "ep", split_axis=0, concat_axis=0, tiled=True)


def step(activations, routes, blocks, row_scale, gate_up, down_weight, slot_map):
    members = lax.axis_size("ep")
    tokens = activations[0]
    row_count, width = tokens.shape
    boxed = (members, BOX, width)
    flat = (members * BOX, width)
    route = routes.reshape(1, row_count)
    gate_up, down_weight = gate_up[0], down_weight[0]
    scal = jnp.stack([lax.axis_index("half"), lax.axis_index("ep")]).astype(jnp.int32)
    eta = 0.03 / math.sqrt(row_count)

    tokens_b, route_b, scale_b, blocks_b = swap(tokens), swap(route), swap(row_scale), swap(blocks)
    parts = (scal, tokens, tokens_b, route, route_b, row_scale, scale_b)
    train_rows = spread(pack(0, members, *parts).reshape(boxed)).reshape(flat)
    serve_rows = spread(pack(1, members, *parts).reshape(boxed)).reshape(flat)

    train_rows_b = swap(train_rows)
    hidden, grad_own, grad_send, both = train(scal, blocks, blocks_b, train_rows, gate_up, down_weight)
    both_b = swap(both)
    hidden_send, grad_send, _ = lax.optimization_barrier((hidden, grad_send, both_b))
    hidden_b, grad_b = swap(hidden_send), swap(grad_send)
    new = update_gate(eta, scal, train_rows, train_rows_b, both, both_b, gate_up)
    new = update_down(eta, scal, hidden, hidden_b, grad_own, grad_b, down_weight, new)
    laid = new.shape
    tiled = (members,) + laid[2:]
    pieces = spread(new.reshape(tiled))
    both, _ = lax.optimization_barrier((both, new))
    input_grad = lax.dot_general(both, gate_up, NT, preferred_element_type=F32).astype(BF16)
    chosen = choose(slot_map, pieces)
    slots = spread(chosen)
    input_grad, _ = lax.optimization_barrier((input_grad, slots))
    train_back = spread(input_grad.reshape(boxed)).reshape(flat)
    slots_b = swap(slots)
    served = serve(scal, blocks, blocks_b, serve_rows, slots.reshape(laid), slots_b.reshape(laid))
    serve_back = spread(served.reshape(boxed)).reshape(flat)
    train_other, serve_other = swap(train_back), swap(serve_back)
    return unpack(members, scal, route, train_back, train_other, serve_back, serve_other)[None]


def solution(mesh):
    placed = (
        P("half", "ep", None),
        P("half", "ep", None),
        P("half", None),
        P("half", "ep"),
        P("ep", None, None),
        P("ep", None, None),
        P(),
    )
    return jax.shard_map(step, mesh=mesh, in_specs=placed, out_specs=P("half", "ep", None), check_vma=False)
```

time: 357 us -> 343 us (0.961)
  blocking collectives: 0 us -> 124 us
  Pallas kernels: 118 us -> 58.2 us
  starting transfers between devices: 84.8 us -> 44.4 us
  waiting for transfers between devices: 134 us -> 99.2 us
    all_to_all x0 -> x2, blocking collectives: none -> 124 us  [spread(): return lax.all_to_all(value, 'ep', split_axis=0, concat_axis=0, tiled=True)]
    pallas_call x2 -> x1, Pallas kernels: 56 us -> 8.18 us  [choose(): pl.pallas_call(choose_kernel, out_shape=jax.ShapeDtypeStruct(pieces.shape...]
    all_to_all x8 -> x4, waiting for transfers between devices: 120 us -> 86.7 us  [spread(): return lax.all_to_all(value, 'ep', split_axis=0, concat_axis=0, tiled=True)]
    all_to_all x8 -> x4, starting transfers between devices: 58.9 us -> 28.2 us  [spread(): return lax.all_to_all(value, 'ep', split_axis=0, concat_axis=0, tiled=True)]
    pallas_call x1, Pallas kernels: 22.1 us -> 11.5 us  [train(): pl.pallas_call(train_kernel, out_shape=(jax.ShapeDtypeStruct((slots, f),...]
    ppermute x10 -> x11, starting transfers between devices: 25.9 us -> 16.2 us  [swap(): return lax.ppermute(value, 'half', SWAP)]
    unnamed x28 -> x26, local copies, waits for them, and re-layouts: 9.87 us -> 6.42 us
    ppermute x10 -> x11, waiting for transfers between devices: 13.6 us -> 12.5 us  [swap(): return lax.ppermute(value, 'half', SWAP)]
  transfers between devices with their start and end apart: 18 -> 15, of which waited for: 12 -> 9; matrix products, arithmetic and copies ran while one was open for 2% -> 3% of each run, Pallas kernels for 24% -> 7%
where the time goes in v2:
time: 343 us; the launch traced here: 342 us
  blocking collectives  124 us (36%)
  waiting for transfers between devices  99.2 us (29%)
  Pallas kernels  58.2 us (17%)
  starting transfers between devices  44.4 us (13%)
  matrix products  8.12 us (2%)
  local copies, waits for them, and re-layouts  6.42 us (2%)
    all_to_all x2, blocking collectives, spread(): return lax.all_to_all(value, 'ep', split_axis=0, concat_axis=0, tiled=True)  124 us
    all_to_all x4, waiting for transfers between devices, spread(): return lax.all_to_all(value, 'ep', split_axis=0, concat_axis=0, tiled=True)  86.7 us
    all_to_all x4, starting transfers between devices, spread(): return lax.all_to_all(value, 'ep', split_axis=0, concat_axis=0, tiled=True)  28.2 us
    ppermute x11, starting transfers between devices, swap(): return lax.ppermute(value, 'half', SWAP)  16.2 us
    ppermute x11, waiting for transfers between devices, swap(): return lax.ppermute(value, 'half', SWAP)  12.5 us
    pallas_call x1, Pallas kernels, train(): pl.pallas_call(train_kernel, out_shape=(jax.ShapeDtypeStruct((slots, f),...  11.5 us
    pallas_call x2, Pallas kernels, pack(): pl.pallas_call(lambda *refs: pack_kernel(group, members, *refs), out_shap...  10.3 us
    pallas_call x1, Pallas kernels, serve(): pl.pallas_call(serve_kernel, out_shape=jax.ShapeDtypeStruct((slots, d), B...  9.87 us
  transfers between devices with their start and end apart: 15, of which 9 were waited for; matrix products, arithmetic and copies ran while one was open for 3% of the time, Pallas kernels for 7%

profile of v2, /device:TPU:1, one launch (start us, length us, event | category | flops | bytes accessed | tf_op | source)
XLA Modules:
  0.0 341.8 jit_solution(4611274998961193954)
XLA Ops:
  0.0 1.4 collective-permute-start.1
  2.5 2.5 collective-permute-done.3.refs_6_
  5.6 1.2 copy-done.9
  6.8 5.2 %shard_map.73 = bf16[512,2048]{1,0:T(8,128)(2,1)} custom-call(s32[2]{0:T(128)} %pad_add_fusion.refs_0_.scal, bf16[448,2048]{1,0:T(8,128)(2,1)} %bitcast.36, bf16[448,2048]{1,0:T(8,128)(2,1)} %copy-done.9, s32[1,448]{1,0:T(1,128)} %bitcast.40, s32[1,448]{1,0:T(1,128)} %copy-done.11, bf16[1,448]{1,0:T(2,128)(2,1)} %refs_5_.3, bf16[1,448]{1,0:T(2,128)(2,1)} %copy-done.12), custom_call_target="tpu_custom_call" | custom-call | tf_op jit(solution)/shard_map/pallas_call | solution.py:84
  12.1 11.3 %all-to-all-start = ((bf16[64,8,2048]{2,1,0:T(8,128)(2,1)}), bf16[64,8,2048]{2,1,0:T(8,128)(2,1)S(1)}, u32[]{:S(2)}, u32[]{:S(2)}) async-start(bf16[64,8,2048]{2,1,0:T(8,128)(2,1)} %bitcast.31), calls=%async_computation | async-start | bytes 4194304 | tf_op jit(solution)/shard_map/all_to_all | solution.py:506
  24.9 26.5 %all-to-all-done = bf16[64,8,2048]{2,1,0:T(8,128)(2,1)S(1)} async-done(((bf16[64,8,2048]{2,1,0:T(8,128)(2,1)}), bf16[64,8,2048]{2,1,0:T(8,128)(2,1)S(1)}, u32[]{:S(2)}, u32[]{:S(2)}) %all-to-all-start) | async-done | bytes 2097184 | tf_op jit(solution)/shard_map/all_to_all | solution.py:506
  51.4 1.9 copy-done
  53.3 11.5 %train.1 = (bf16[512,768]{1,0:T(8,128)(2,1)S(1)}, bf16[512,1024]{1,0:T(8,128)(2,1)S(1)}, bf16[512,1024]{1,0:T(8,128)(2,1)S(1)}, bf16[512,1536]{1,0:T(8,128)(2,1)S(1)}) custom-call(s32[2]{0:T(128)S(1)} %copy-done.4, s32[1,64]{1,0:T(1,128)S(1)} %copy-done.6, s32[1,64]{1,0:T(1,128)S(1)} %collective-permute-done.blocks_b, bf16[512,2048]{1,0:T(8,128)(2,1)S(1)} %bitcast.22, ...), custom_call_target="tpu_custom_call" | custom-call | tf_op jit(solution)/shard_map/train/pallas_call | solution.py:199
  64.8 2.6 collective-permute-start.4
  67.5 2.9 collective-permute-done.4.refs_4_
  70.9 2.5 collective-permute-done.7.refs_2_
  73.4 7.7 %update_gate.1.refs_6_ = bf16[16,4,144,256]{3,2,1,0:T(8,128)(2,1)S(1)} custom-call(s32[2]{0:T(128)S(1)} %copy-done.4, bf16[512,2048]{1,0:T(8,128)(2,1)S(1)} %bitcast.24, bf16[512,2048]{1,0:T(8,128)(2,1)S(1)} %collective-permute-done.7.refs_2_, bf16[512,1536]{1,0:T(8,128)(2,1)S(1)} %get-tuple-element.19.refs_3_, ...), custom_call_target="tpu_custom_call" | custom-call | tf_op jit(solution)/shard_map/update_gate/pallas_call | solution.py:267
  81.1 4.4 %update_down.1 = bf16[16,4,144,256]{3,2,1,0:T(8,128)(2,1)S(1)} custom-call(s32[2]{0:T(128)S(1)} %copy-done.4, bf16[512,768]{1,0:T(8,128)(2,1)S(1)} %get-tuple-element.16.refs_1_, bf16[512,768]{1,0:T(8,128)(2,1)S(1)} %collective-permute-done.5.refs_2_, bf16[512,1024]{1,0:T(8,128)(2,1)S(1)} %get-tuple-element.17.refs_3_, ...), custom_call_target="tpu_custom_call", output_to_operand_aliasing={{}: (6, {})} | custom-call | tf_op jit(solution)/shard_map/update_down/pallas_call | solution.py:331
  85.6 63.1 %all_to_all.30.src = bf16[64,144,256]{2,1,0:T(8,128)(2,1)S(1)} all-to-all(bf16[64,144,256]{2,1,0:T(8,128)(2,1)S(1)} %bitcast.21), channel_id=1, replica_groups=mesh['half'=2,'ep'=64] {'ep'}, dimensions={0} | all-to-all | bytes 9437184 | tf_op jit(solution)/shard_map/all_to_all | solution.py:506
  148.6 8.2 %choose.1 = bf16[64,144,256]{2,1,0:T(8,128)(2,1)S(1)} custom-call(s32[64]{0:T(128)S(1)} %copy-done.7, bf16[64,144,256]{2,1,0:T(8,128)(2,1)S(1)} %all_to_all.30.src), custom_call_target="tpu_custom_call" | custom-call | tf_op jit(solution)/shard_map/choose/pallas_call | solution.py:366
  156.8 61.3 %all_to_all.31 = bf16[64,144,256]{2,1,0:T(8,128)(2,1)} all-to-all(bf16[64,144,256]{2,1,0:T(8,128)(2,1)S(1)} %choose.1), channel_id=1, replica_groups=mesh['half'=2,'ep'=64] {'ep'}, dimensions={0} | all-to-all | bytes 9437184 | tf_op jit(solution)/shard_map/all_to_all | solution.py:506
  218.2 3.3 collective-permute-start.9
  221.5 5.1 %shard_map.74 = bf16[512,2048]{1,0:T(8,128)(2,1)} custom-call(s32[2]{0:T(128)} %pad_add_fusion.refs_0_.scal, bf16[448,2048]{1,0:T(8,128)(2,1)} %bitcast.37, bf16[448,2048]{1,0:T(8,128)(2,1)} %copy-done.9, s32[1,448]{1,0:T(1,128)} %bitcast.41, s32[1,448]{1,0:T(1,128)} %copy-done.11, bf16[1,448]{1,0:T(2,128)(2,1)} %refs_5_.3, bf16[1,448]{1,0:T(2,128)(2,1)} %copy-done.12), custom_call_target="tpu_custom_call" | custom-call | tf_op jit(solution)/shard_map/pallas_call | solution.py:84
  226.6 4.9 %all-to-all-start.4 = ((bf16[64,8,2048]{2,1,0:T(8,128)(2,1)}), bf16[64,8,2048]{2,1,0:T(8,128)(2,1)S(1)}, u32[]{:S(2)}, u32[]{:S(2)}) async-start(bf16[64,8,2048]{2,1,0:T(8,128)(2,1)} %bitcast.32), calls=%async_computation.4 | async-start | bytes 4194304 | tf_op jit(solution)/shard_map/all_to_all | solution.py:506
  231.5 8.1 %convolution_convert_fusion = bf16[512,2048]{1,0:T(8,128)(2,1)} fusion(bf16[512,1536]{1,0:T(8,128)(2,1)} %copy-done.3, bf16[1,2048,1536]{2,1,0:T(8,128)(2,1)} %param.11), kind=kOutput, calls=%fused_computation | convolution fusion | flops 3222274048 | bytes 9961472 | tf_op jit(solution)/shard_map/dot_general | solution.py:536
  239.6 20.7 %all-to-all-done.4 = bf16[64,8,2048]{2,1,0:T(8,128)(2,1)S(1)} async-done(((bf16[64,8,2048]{2,1,0:T(8,128)(2,1)}), bf16[64,8,2048]{2,1,0:T(8,128)(2,1)S(1)}, u32[]{:S(2)}, u32[]{:S(2)}) %all-to-all-start.4) | async-done | bytes 2097184 | tf_op jit(solution)/shard_map/all_to_all | solution.py:506
  260.3 6.5 %all-to-all-start.3 = ((bf16[64,8,2048]{2,1,0:T(8,128)(2,1)}), bf16[64,8,2048]{2,1,0:T(8,128)(2,1)}, u32[]{:S(2)}, u32[]{:S(2)}) async-start(bf16[64,8,2048]{2,1,0:T(8,128)(2,1)} %bitcast.38), calls=%async_computation.3 | async-start | bytes 4194304 | tf_op jit(solution)/shard_map/all_to_all | solution.py:506
  266.8 9.9 %serve.1 = bf16[512,2048]{1,0:T(8,128)(2,1)S(1)} custom-call(s32[2]{0:T(128)S(1)} %copy-done.5, s32[1,64]{1,0:T(1,128)S(1)} %copy-done.6, s32[1,64]{1,0:T(1,128)S(1)} %collective-permute-done.blocks_b, bf16[512,2048]{1,0:T(8,128)(2,1)S(1)} %bitcast.27, bf16[16,4,144,256]{3,2,1,0:T(8,128)(2,1)} %bitcast.13.w_a, bf16[16,4,144,256]{3,2,1,0:T(8,128)(2,1)} %bitcast.14.w_b), custom_call_target="tpu_custom_call" | custom-call | tf_op jit(solution)/shard_map/serve/pallas_call | solution.py:442
  276.7 1.3 copy-done.2
  278.0 16.0 %all-to-all-done.3 = bf16[64,8,2048]{2,1,0:T(8,128)(2,1)} async-done(((bf16[64,8,2048]{2,1,0:T(8,128)(2,1)}), bf16[64,8,2048]{2,1,0:T(8,128)(2,1)}, u32[]{:S(2)}, u32[]{:S(2)}) %all-to-all-start.3) | async-done | bytes 2097184 | tf_op jit(solution)/shard_map/all_to_all | solution.py:506
  294.0 5.6 %all-to-all-start.5 = ((bf16[64,8,2048]{2,1,0:T(8,128)(2,1)}), bf16[64,8,2048]{2,1,0:T(8,128)(2,1)S(1)}, u32[]{:S(2)}, u32[]{:S(2)}) async-start(bf16[64,8,2048]{2,1,0:T(8,128)(2,1)} %bitcast.28), calls=%async_computation.5 | async-start | bytes 4194304 | tf_op jit(solution)/shard_map/all_to_all | solution.py:506
  299.6 3.4 %collective-permute-start.8 = (bf16[512,2048]{1,0:T(8,128)(2,1)}, bf16[512,2048]{1,0:T(8,128)(2,1)}, u32[]{:S(2)}, u32[]{:S(2)}) collective-permute-start(bf16[512,2048]{1,0:T(8,128)(2,1)} %bitcast.10.refs_2_), channel_id=1, source_target_pairs={{0,64},{64,0},{1,65},{65,1},{2,66},{66,2},{3,67},{67,3},{4,68},{68... | collective-permute-start | bytes 6291464 | tf_op jit(solution)/shard_map/ppermute | solution.py:502
  303.0 23.6 %all-to-all-done.5 = bf16[64,8,2048]{2,1,0:T(8,128)(2,1)S(1)} async-done(((bf16[64,8,2048]{2,1,0:T(8,128)(2,1)}), bf16[64,8,2048]{2,1,0:T(8,128)(2,1)S(1)}, u32[]{:S(2)}, u32[]{:S(2)}) %all-to-all-start.5) | async-done | bytes 2097184 | tf_op jit(solution)/shard_map/all_to_all | solution.py:506
  326.6 3.6 %collective-permute-start.10 = (bf16[512,2048]{1,0:T(8,128)(2,1)S(1)}, bf16[512,2048]{1,0:T(8,128)(2,1)S(1)}, u32[]{:S(2)}, u32[]{:S(2)}) collective-permute-start(bf16[512,2048]{1,0:T(8,128)(2,1)S(1)} %bitcast.33), channel_id=1, source_target_pairs={{0,64},{64,0},{1,65},{65,1},{2,66},{66,2},{3,67},{67,3},{4,68},{68... | collective-permute-start | bytes 6291464 | tf_op jit(solution)/shard_map/ppermute | solution.py:502
  330.2 3.8 %collective-permute-done.10.refs_5_ = bf16[512,2048]{1,0:T(8,128)(2,1)S(1)} collective-permute-done((bf16[512,2048]{1,0:T(8,128)(2,1)S(1)}, bf16[512,2048]{1,0:T(8,128)(2,1)S(1)}, u32[]{:S(2)}, u32[]{:S(2)}) %collective-permute-start.10) | collective-permute-done | bytes 2097184 | tf_op jit(solution)/shard_map/ppermute | solution.py:502
  334.0 1.4 copy-done.10
  335.4 6.2 %unpack.1 = bf16[448,2048]{1,0:T(8,128)(2,1)} custom-call(s32[2]{0:T(128)} %pad_add_fusion.refs_0_.scal, s32[1,448]{1,0:T(1,128)} %bitcast.42, bf16[512,2048]{1,0:T(8,128)(2,1)} %bitcast.10.refs_2_, bf16[512,2048]{1,0:T(8,128)(2,1)} %collective-permute-done.8.refs_3_, bf16[512,2048]{1,0:T(8,128)(2,1)} %bitcast.34, bf16[512,2048]{1,0:T(8,128)(2,1)} %copy-done.10), custom_call_target="tpu_custom_call" | custom-call | tf_op jit(solution)/shard_map/unpack/pallas_call | solution.py:490
  (36 shorter events, 4.0 us)
Async XLA Ops:
  0.0 5.0 %collective-permute-start.1 = (bf16[448,2048]{1,0:T(8,128)(2,1)}, bf16[448,2048]{1,0:T(8,128)(2,1)S(1)}, u32[]{:S(2)}, u32[]{:S(2)}) collective-permute-start(bf16[448,2048]{1,0:T(8,128)(2,1)} %bitcast.35), channel_id=1, source_target_pairs={{0,64},{64,0},{1,65},{65,1},{2,66},{66,2},{3,67},{67,3},{4,68},{68... | collective-permute-start | bytes 5505032 | tf_op jit(solution)/shard_map/ppermute | solution.py:502
  1.4 3.6 %collective-permute-start.2 = (s32[1,448]{1,0:T(1,128)}, s32[1,448]{1,0:T(1,128)S(1)}, u32[]{:S(2)}, u32[]{:S(2)}) collective-permute-start(s32[1,448]{1,0:T(1,128)} %bitcast.39), channel_id=1, source_target_pairs={{0,64},{64,0},{1,65},{65,1},{2,66},{66,2},{3,67},{67,3},{4,68},{68... | collective-permute-start | bytes 5384 | tf_op jit(solution)/shard_map/ppermute | solution.py:502
  1.4 3.6 %collective-permute-start.3 = (bf16[1,448]{1,0:T(2,128)(2,1)}, bf16[1,448]{1,0:T(2,128)(2,1)S(1)}, u32[]{:S(2)}, u32[]{:S(2)}) collective-permute-start(bf16[1,448]{1,0:T(2,128)(2,1)} %refs_5_.3), channel_id=1, source_target_pairs={{0,64},{64,0},{1,65},{65,1},{2,66},{66,2},{3,67},{67,3},{4,68},{68... | collective-permute-start | bytes 2696 | tf_op jit(solution)/shard_map/ppermute | solution.py:502
  5.0 0.6 copy-start.12
  5.0 0.6 copy-start.11
  5.6 1.2 copy-start.9
  12.0 11.3 %copy-start.6 = (s32[1,64]{1,0:T(1,128)S(1)}, s32[1,64]{1,0:T(1,128)}, u32[]{:S(2)}) copy-start(s32[1,64]{1,0:T(1,128)} %blocks_a.3) | copy-start | bytes 772
  12.0 39.3 %copy-start.4 = (s32[2]{0:T(128)S(1)}, s32[2]{0:T(128)}, u32[]{:S(2)}) copy-start(s32[2]{0:T(128)} %pad_add_fusion.refs_0_.scal) | copy-start | bytes 28
  12.1 39.3 %all-to-all-start = ((bf16[64,8,2048]{2,1,0:T(8,128)(2,1)}), bf16[64,8,2048]{2,1,0:T(8,128)(2,1)S(1)}, u32[]{:S(2)}, u32[]{:S(2)}) async-start(bf16[64,8,2048]{2,1,0:T(8,128)(2,1)} %bitcast.31), calls=%async_computation | async-start | bytes 4194304 | tf_op jit(solution)/shard_map/all_to_all | solution.py:506
  23.3 1.6 collective-permute-start
  51.4 1.9 copy-start
  64.8 16.3 %copy-start.3 = (bf16[512,1536]{1,0:T(8,128)(2,1)}, bf16[512,1536]{1,0:T(8,128)(2,1)S(1)}, u32[]{:S(2)}) copy-start(bf16[512,1536]{1,0:T(8,128)(2,1)S(1)} %get-tuple-element.19.refs_3_) | copy-start | bytes 4718596
  64.8 5.6 %collective-permute-start.4 = (bf16[512,1536]{1,0:T(8,128)(2,1)S(1)}, bf16[512,1536]{1,0:T(8,128)(2,1)S(1)}, u32[]{:S(2)}, u32[]{:S(2)}) collective-permute-start(bf16[512,1536]{1,0:T(8,128)(2,1)S(1)} %get-tuple-element.19.refs_3_), channel_id=1, source_target_pairs={{0,64},{64,0},{1,65},{65,1},{2,66},{66,2},{3,67},{67,3},{4,68},{68... | collective-permute-start | bytes 4718600 | tf_op jit(solution)/shard_map/ppermute | solution.py:502
  67.4 6.0 %collective-permute-start.7 = (bf16[512,2048]{1,0:T(8,128)(2,1)S(1)}, bf16[512,2048]{1,0:T(8,128)(2,1)S(1)}, u32[]{:S(2)}, u32[]{:S(2)}) collective-permute-start(bf16[512,2048]{1,0:T(8,128)(2,1)S(1)} %bitcast.23), channel_id=1, source_target_pairs={{0,64},{64,0},{1,65},{65,1},{2,66},{66,2},{3,67},{67,3},{4,68},{68... | collective-permute-start | bytes 6291464 | tf_op jit(solution)/shard_map/ppermute | solution.py:502
  70.4 10.7 %collective-permute-start.6 = (bf16[512,1024]{1,0:T(8,128)(2,1)S(1)}, bf16[512,1024]{1,0:T(8,128)(2,1)S(1)}, u32[]{:S(2)}, u32[]{:S(2)}) collective-permute-start(bf16[512,1024]{1,0:T(8,128)(2,1)S(1)} %get-tuple-element.18), channel_id=1, source_target_pairs={{0,64},{64,0},{1,65},{65,1},{2,66},{66,2},{3,67},{67,3},{4,68},{68... | collective-permute-start | bytes 3145736 | tf_op jit(solution)/shard_map/ppermute | solution.py:502
  70.8 10.3 %collective-permute-start.5 = (bf16[512,768]{1,0:T(8,128)(2,1)S(1)}, bf16[512,768]{1,0:T(8,128)(2,1)S(1)}, u32[]{:S(2)}, u32[]{:S(2)}) collective-permute-start(bf16[512,768]{1,0:T(8,128)(2,1)S(1)} %get-tuple-element.16.refs_1_), channel_id=1, source_target_pairs={{0,64},{64,0},{1,65},{65,1},{2,66},{66,2},{3,67},{67,3},{4,68},{68... | collective-permute-start | bytes 2359304 | tf_op jit(solution)/shard_map/ppermute | solution.py:502
  73.4 7.7 %copy-start.1 = (bf16[1,768,2048]{2,1,0:T(8,128)(2,1)S(1)}, bf16[1,768,2048]{2,1,0:T(8,128)(2,1)}, u32[]{:S(2)}) copy-start(bf16[1,768,2048]{2,1,0:T(8,128)(2,1)} %param.12) | copy-start | bytes 9437188
  85.6 63.1 %copy-start.7 = (s32[64]{0:T(128)S(1)}, s32[64]{0:T(128)}, u32[]{:S(2)}) copy-start(s32[64]{0:T(128)} %slot_map.1) | copy-start | bytes 772
  218.2 48.6 %collective-permute-start.9 = (bf16[64,144,256]{2,1,0:T(8,128)(2,1)}, bf16[64,144,256]{2,1,0:T(8,128)(2,1)}, u32[]{:S(2)}, u32[]{:S(2)}) collective-permute-start(bf16[64,144,256]{2,1,0:T(8,128)(2,1)} %all_to_all.31), channel_id=1, source_target_pairs={{0,64},{64,0},{1,65},{65,1},{2,66},{66,2},{3,67},{67,3},{4,68},{68... | collective-permute-start | bytes 14155784 | tf_op jit(solution)/shard_map/ppermute | solution.py:502
  226.6 33.6 %all-to-all-start.4 = ((bf16[64,8,2048]{2,1,0:T(8,128)(2,1)}), bf16[64,8,2048]{2,1,0:T(8,128)(2,1)S(1)}, u32[]{:S(2)}, u32[]{:S(2)}) async-start(bf16[64,8,2048]{2,1,0:T(8,128)(2,1)} %bitcast.32), calls=%async_computation.4 | async-start | bytes 4194304 | tf_op jit(solution)/shard_map/all_to_all | solution.py:506
  260.3 6.5 %copy-start.5 = (s32[2]{0:T(128)S(1)}, s32[2]{0:T(128)}, u32[]{:S(2)}) copy-start(s32[2]{0:T(128)} %pad_add_fusion.refs_0_.scal) | copy-start | bytes 28
  260.3 33.7 %all-to-all-start.3 = ((bf16[64,8,2048]{2,1,0:T(8,128)(2,1)}), bf16[64,8,2048]{2,1,0:T(8,128)(2,1)}, u32[]{:S(2)}, u32[]{:S(2)}) async-start(bf16[64,8,2048]{2,1,0:T(8,128)(2,1)} %bitcast.38), calls=%async_computation.3 | async-start | bytes 4194304 | tf_op jit(solution)/shard_map/all_to_all | solution.py:506
  276.6 1.3 copy-start.2
  294.0 32.6 %all-to-all-start.5 = ((bf16[64,8,2048]{2,1,0:T(8,128)(2,1)}), bf16[64,8,2048]{2,1,0:T(8,128)(2,1)S(1)}, u32[]{:S(2)}, u32[]{:S(2)}) async-start(bf16[64,8,2048]{2,1,0:T(8,128)(2,1)} %bitcast.28), calls=%async_computation.5 | async-start | bytes 4194304 | tf_op jit(solution)/shard_map/all_to_all | solution.py:506
  299.6 30.6 %collective-permute-start.8 = (bf16[512,2048]{1,0:T(8,128)(2,1)}, bf16[512,2048]{1,0:T(8,128)(2,1)}, u32[]{:S(2)}, u32[]{:S(2)}) collective-permute-start(bf16[512,2048]{1,0:T(8,128)(2,1)} %bitcast.10.refs_2_), channel_id=1, source_target_pairs={{0,64},{64,0},{1,65},{65,1},{2,66},{66,2},{3,67},{67,3},{4,68},{68... | collective-permute-start | bytes 6291464 | tf_op jit(solution)/shard_map/ppermute | solution.py:502
  326.6 7.4 %copy-start.8 = (bf16[64,8,2048]{2,1,0:T(8,128)(2,1)}, bf16[64,8,2048]{2,1,0:T(8,128)(2,1)S(1)}, u32[]{:S(2)}) copy-start(bf16[64,8,2048]{2,1,0:T(8,128)(2,1)S(1)} %all-to-all-done.5) | copy-start | bytes 6291460
  326.6 7.4 %collective-permute-start.10 = (bf16[512,2048]{1,0:T(8,128)(2,1)S(1)}, bf16[512,2048]{1,0:T(8,128)(2,1)S(1)}, u32[]{:S(2)}, u32[]{:S(2)}) collective-permute-start(bf16[512,2048]{1,0:T(8,128)(2,1)S(1)} %bitcast.33), channel_id=1, source_target_pairs={{0,64},{64,0},{1,65},{65,1},{2,66},{66,2},{3,67},{67,3},{4,68},{68... | collective-permute-start | bytes 6291464 | tf_op jit(solution)/shard_map/ppermute | solution.py:502
  334.0 1.4 copy-start.10

commit v3 on v2

--- a/solution.py
+++ b/solution.py
@@ -29,6 +29,10 @@
 
 def anywhere():
     return pl.BlockSpec(memory_space=pl.ANY)
+
+
+def in_hbm(*values):
+    return [pltpu.with_memory_space_constraint(value, pltpu.HBM) for value in values]
 
 
 def vmem():
@@ -83,11 +87,11 @@
     width = tok_a.shape[1]
     return pl.pallas_call(
         lambda *refs: pack_kernel(group, members, *refs),
-        out_shape=jax.ShapeDtypeStruct((slots, width), BF16),
+        out_shape=pltpu.HBM((slots, width), BF16),
         in_specs=[smem(), anywhere(), anywhere(), vmem(), vmem(), vmem(), vmem()],
         out_specs=vmem(),
         scratch_shapes=[pltpu.VMEM(tok_a.shape, BF16), pltpu.SemaphoreType.DMA],
-        compiler_params=params(),
+        compiler_params=params(24),
     )(scal, tok_a, tok_b, route_a, route_b, scale_a, scale_b)
 
 
@@ -118,7 +122,7 @@
 
 
 def train_kernel(scal, blocks_a, blocks_b, x_h, gu_h, dw_h, hid_h, og_own, og_send, bg_h,
-                 x, gu, dw, gate, up, hid, og, bg, sem):
+                 x, gu, dw, gate, up, hid, hid_t, og, bg, sem):
     half = scal[0]
     d, f2 = gu.shape
     f = f2 // 2
@@ -149,11 +153,13 @@
         u = jnp.dot(x[...], gu[:, right], preferred_element_type=F32)
         gate[:, left] = g
         up[:, left] = u
-        hid[:, left] = (keep * (g * jax.nn.sigmoid(g) * u)).astype(BF16)
+        h = (keep * (g * jax.nn.sigmoid(g) * u)).astype(BF16)
+        hid[:, left] = h
+        hid_t[left, :] = h.T
         return 0
 
     lax.fori_loop(0, nf, project, 0)
-    out_hid = pltpu.make_async_copy(hid, hid_h, sem.at[2 + 2 * nf])
+    out_hid = pltpu.make_async_copy(hid_t, hid_h, sem.at[2 + 2 * nf])
     out_hid.start()
     load_dw.wait()
 
@@ -199,14 +205,14 @@
     return pl.pallas_call(
         train_kernel,
         out_shape=(
-            jax.ShapeDtypeStruct((slots, f), BF16), half_rows, half_rows, jax.ShapeDtypeStruct((slots, f2), BF16)
+            jax.ShapeDtypeStruct((f, slots), BF16), half_rows, half_rows, pltpu.HBM((slots, f2), BF16)
         ),
         in_specs=[smem(), smem(), smem(), anywhere(), anywhere(), anywhere()],
         out_specs=(anywhere(),) * 4,
         scratch_shapes=[
             pltpu.VMEM((slots, d), BF16), pltpu.VMEM((d, f2), BF16), pltpu.VMEM((f, d), BF16),
             pltpu.VMEM((slots, f), F32), pltpu.VMEM((slots, f), F32), pltpu.VMEM((slots, f), BF16),
-            pltpu.VMEM((slots, d), BF16), pltpu.VMEM((slots, f2), BF16),
+            pltpu.VMEM((f, slots), BF16), pltpu.VMEM((slots, d), BF16), pltpu.VMEM((slots, f2), BF16),
             pltpu.SemaphoreType.DMA((6 + 2 * (f // 256),)),
         ],
         compiler_params=params(40),
@@ -214,19 +220,10 @@
     )(scal, blocks_a, blocks_b, x, gate_up, down)
 
 
-def update_gate_kernel(eta, scal, x_a, x_b, bg_a, bg_b, gu_h, out, x, x_t, bg, w, stage, sem):
-    slots = x.shape[1]
-    wide = x.shape[2]
-    groups, four, high, cols = stage.shape[1:]
-    steps = stage.shape[0]
+def turn_kernel(scal, x_a, x_b, out, x, sem):
+    slots, wide = x.shape[1:]
     mine = pl.ds(pl.multiple_of(scal[0] * wide, wide), wide)
-    loads = [
-        pltpu.make_async_copy(x_a.at[:, mine], x.at[0], sem.at[0]),
-        pltpu.make_async_copy(x_b.at[:, mine], x.at[1], sem.at[1]),
-        pltpu.make_async_copy(bg_a, bg.at[pl.ds(0, slots)], sem.at[2]),
-        pltpu.make_async_copy(bg_b, bg.at[pl.ds(slots, slots)], sem.at[3]),
-        pltpu.make_async_copy(gu_h.at[mine, :], w, sem.at[4]),
-    ]
+    loads = [pltpu.make_async_copy(src.at[:, mine], x.at[s], sem.at[s]) for s, src in enumerate((x_a, x_b))]
     for load in loads:
         load.start()
     for s in range(2):
@@ -234,20 +231,59 @@
 
         def turn(c, _):
             part = pl.ds(pl.multiple_of(c * 256, 256), 256)
-            x_t[part, s * slots:(s + 1) * slots] = x[s, :, part].T
+            out[part, s * slots:(s + 1) * slots] = x[s, :, part].T
             return 0
 
         lax.fori_loop(0, wide // 256, turn, 0)
-    for load in loads[2:]:
-        load.wait()
+
+
+def turned(scal, x_a, x_b):
+    slots, d = x_a.shape
+    wide = d // 2
+    return pl.pallas_call(
+        turn_kernel,
+        out_shape=jax.ShapeDtypeStruct((wide, 2 * slots), BF16),
+        in_specs=[smem(), anywhere(), anywhere()],
+        out_specs=vmem(),
+        scratch_shapes=[pltpu.VMEM((2, slots, wide), BF16), pltpu.SemaphoreType.DMA((2,))],
+        compiler_params=params(12),
+        name="turn",
+    )(scal, x_a, x_b)
+
+
+def update_gate_kernel(eta, scal, xt_h, bg_a, bg_b, gu_h, out, x_t, bg, w, stage, sem):
+    wide = x_t.shape[0]
+    slots = x_t.shape[1] // 2
+    groups, four, high, cols = stage.shape[1:]
+    steps = stage.shape[0]
+    mine = pl.ds(pl.multiple_of(scal[0] * wide, wide), wide)
+    load_x = pltpu.make_async_copy(xt_h, x_t, sem.at[0])
+
+    def part(n):
+        return pl.ds(pl.multiple_of(n * cols, cols), cols)
+
+    def loads(n):
+        return (
+            pltpu.make_async_copy(bg_a.at[:, part(n)], bg.at[pl.ds(0, slots), part(n)], sem.at[1 + 3 * n]),
+            pltpu.make_async_copy(bg_b.at[:, part(n)], bg.at[pl.ds(slots, slots), part(n)], sem.at[2 + 3 * n]),
+            pltpu.make_async_copy(gu_h.at[mine, part(n)], w.at[:, part(n)], sem.at[3 + 3 * n]),
+        )
 
     def save(n):
-        return pltpu.make_async_copy(stage.at[n], out.at[:, :, pl.ds(pl.multiple_of(n * high, high), high), :], sem.at[5 + n])
+        rows = pl.ds(pl.multiple_of(n * high, high), high)
+        return pltpu.make_async_copy(stage.at[n], out.at[:, :, rows, :], sem.at[1 + 3 * steps + n])
+
+    load_x.start()
+    for n in range(steps):
+        for load in loads(n):
+            load.start()
+    load_x.wait()
 
     def one(n, _):
-        part = pl.ds(pl.multiple_of(n * cols, cols), cols)
-        grad = jnp.dot(x_t[...], bg[:, part], preferred_element_type=F32)
-        new = (w[:, part].astype(F32) - eta * grad).astype(BF16)
+        for load in loads(n):
+            load.wait()
+        grad = jnp.dot(x_t[...], bg[:, part(n)], preferred_element_type=F32)
+        new = (w[:, part(n)].astype(F32) - eta * grad).astype(BF16)
         stage[n] = new.reshape(groups, four, high, cols)
         save(n).start()
         return 0
@@ -257,53 +293,42 @@
         save(n).wait()
 
 
-def update_gate(eta, scal, x_a, x_b, bg_a, bg_b, gate_up):
-    slots, d = x_a.shape
+def update_gate(eta, scal, x_t, bg_a, bg_b, gate_up):
+    wide, both = x_t.shape
     f2 = bg_a.shape[1]
-    wide = d // 2
     high, cols = wide // 64, 256
     steps = f2 // cols
     tall = steps * high + (f2 // 2) // 16
     return pl.pallas_call(
         lambda *refs: update_gate_kernel(eta, *refs),
-        out_shape=jax.ShapeDtypeStruct((16, 4, tall, cols), BF16),
-        in_specs=[smem()] + [anywhere()] * 5,
+        out_shape=pltpu.HBM((16, 4, tall, cols), BF16),
+        in_specs=[smem()] + [anywhere()] * 4,
         out_specs=anywhere(),
         scratch_shapes=[
-            pltpu.VMEM((2, slots, wide), BF16), pltpu.VMEM((wide, 2 * slots), BF16),
-            pltpu.VMEM((2 * slots, f2), BF16), pltpu.VMEM((wide, f2), BF16),
-            pltpu.VMEM((steps, 16, 4, high, cols), BF16), pltpu.SemaphoreType.DMA((5 + steps,)),
+            pltpu.VMEM((wide, both), BF16), pltpu.VMEM((both, f2), BF16), pltpu.VMEM((wide, f2), BF16),
+            pltpu.VMEM((steps, 16, 4, high, cols), BF16), pltpu.SemaphoreType.DMA((1 + 4 * steps,)),
         ],
-        compiler_params=params(40),
+        compiler_params=params(32),
         name="update_gate",
-    )(scal, x_a, x_b, bg_a, bg_b, gate_up)
-
-
-def update_down_kernel(eta, scal, hid_a, hid_b, og_a, og_b, dw_h, given, out, hid, hid_t, og, w, stage, sem):
-    slots = hid.shape[1]
+    )(scal, x_t, bg_a, bg_b, gate_up)
+
+
+def update_down_kernel(eta, scal, hid_a, hid_b, og_a, og_b, dw_h, given, out, hid_t, og, w, stage, sem):
+    slots = hid_t.shape[1] // 2
     wide = og.shape[1]
     steps, groups, high, cols = stage.shape
     base = out.shape[2] - high
     mine = pl.ds(pl.multiple_of(scal[0] * wide, wide), wide)
     loads = [
-        pltpu.make_async_copy(hid_a, hid.at[0], sem.at[0]),
-        pltpu.make_async_copy(hid_b, hid.at[1], sem.at[1]),
+        pltpu.make_async_copy(hid_a, hid_t.at[:, pl.ds(0, slots)], sem.at[0]),
+        pltpu.make_async_copy(hid_b, hid_t.at[:, pl.ds(slots, slots)], sem.at[1]),
         pltpu.make_async_copy(og_a, og.at[pl.ds(0, slots)], sem.at[2]),
         pltpu.make_async_copy(og_b, og.at[pl.ds(slots, slots)], sem.at[3]),
         pltpu.make_async_copy(dw_h.at[:, mine], w, sem.at[4]),
     ]
     for load in loads:
         load.start()
-    for s in range(2):
-        loads[s].wait()
-
-        def turn(c, _):
-            part = pl.ds(pl.multiple_of(c * 256, 256), 256)
-            hid_t[part, s * slots:(s + 1) * slots] = hid[s, :, part].T
-            return 0
-
-        lax.fori_loop(0, hid.shape[2] // 256, turn, 0)
-    for load in loads[2:]:
+    for load in loads:
         load.wait()
 
     def save(n):
@@ -323,23 +348,22 @@
 
 
 def update_down(eta, scal, hid_a, hid_b, og_a, og_b, down, given):
-    slots, f = hid_a.shape
+    f, slots = hid_a.shape
     wide = og_a.shape[1]
     cols = given.shape[3]
     steps = wide // cols
     high = f // 16
     return pl.pallas_call(
         lambda *refs: update_down_kernel(eta, *refs),
-        out_shape=jax.ShapeDtypeStruct(given.shape, BF16),
+        out_shape=pltpu.HBM(given.shape, BF16),
         in_specs=[smem()] + [anywhere()] * 6,
         out_specs=anywhere(),
         scratch_shapes=[
-            pltpu.VMEM((2, slots, f), BF16), pltpu.VMEM((f, 2 * slots), BF16),
-            pltpu.VMEM((2 * slots, wide), BF16), pltpu.VMEM((f, wide), BF16),
+            pltpu.VMEM((f, 2 * slots), BF16), pltpu.VMEM((2 * slots, wide), BF16), pltpu.VMEM((f, wide), BF16),
             pltpu.VMEM((steps, 16, high, cols), BF16), pltpu.SemaphoreType.DMA((5 + steps,)),
         ],
         input_output_aliases={6: 0},
-        compiler_params=params(40),
+        compiler_params=params(24),
         name="update_down",
     )(scal, hid_a, hid_b, og_a, og_b, down, given)
 
@@ -441,7 +465,7 @@
     steps = 2 * f // 256
     return pl.pallas_call(
         serve_kernel,
-        out_shape=jax.ShapeDtypeStruct((slots, d), BF16),
+        out_shape=pltpu.HBM((slots, d), BF16),
         in_specs=[smem(), smem(), smem()] + [anywhere()] * 3,
         out_specs=vmem(),
         scratch_shapes=[
@@ -493,7 +517,7 @@
         in_specs=[smem(), vmem()] + [anywhere()] * 4,
         out_specs=vmem(),
         scratch_shapes=[pltpu.VMEM((slots, d), BF16), pltpu.VMEM((slots, d), BF16), pltpu.SemaphoreType.DMA((2,))],
-        compiler_params=params(),
+        compiler_params=params(24),
         name="unpack",
     )(scal, route, t_own, t_recv, p_own, p_recv)
 
@@ -517,18 +541,22 @@
     scal = jnp.stack([lax.axis_index("half"), lax.axis_index("ep")]).astype(jnp.int32)
     eta = 0.03 / math.sqrt(row_count)
 
+    gate_h, down_h = in_hbm(gate_up, down_weight)
     tokens_b, route_b, scale_b, blocks_b = swap(tokens), swap(route), swap(row_scale), swap(blocks)
-    parts = (scal, tokens, tokens_b, route, route_b, row_scale, scale_b)
+    parts = (scal, *in_hbm(tokens), tokens_b, *in_hbm(route), route_b, *in_hbm(row_scale), scale_b)
     train_rows = spread(pack(0, members, *parts).reshape(boxed)).reshape(flat)
-    serve_rows = spread(pack(1, members, *parts).reshape(boxed)).reshape(flat)
+    packed = pack(1, members, *parts)
+    serve_rows = spread(packed.reshape(boxed)).reshape(flat)
 
     train_rows_b = swap(train_rows)
-    hidden, grad_own, grad_send, both = train(scal, blocks, blocks_b, train_rows, gate_up, down_weight)
+    hidden, grad_own, grad_send, both = train(scal, blocks, blocks_b, train_rows, gate_h, down_h)
     both_b = swap(both)
+    rows_t = turned(scal, train_rows, train_rows_b)
     hidden_send, grad_send, _ = lax.optimization_barrier((hidden, grad_send, both_b))
-    hidden_b, grad_b = swap(hidden_send), swap(grad_send)
-    new = update_gate(eta, scal, train_rows, train_rows_b, both, both_b, gate_up)
-    new = update_down(eta, scal, hidden, hidden_b, grad_own, grad_b, down_weight, new)
+    hidden_b = swap(hidden_send)
+    grad_b = swap(grad_send)
+    new = update_gate(eta, scal, rows_t, both, both_b, gate_h)
+    new = update_down(eta, scal, hidden, hidden_b, grad_own, grad_b, down_h, new)
     laid = new.shape
     tiled = (members,) + laid[2:]
     pieces = spread(new.reshape(tiled))

time: 343 us -> 344 us (level)
  Pallas kernels: 58.2 us -> 62 us
    pallas_call x4 -> x5, Pallas kernels: 33.5 us -> 38.7 us  [the longest x1 12.7 us: train(): pl.pallas_call(train_kernel, out_shape=(jax.ShapeDtypeStruct((f, slots),...]
  transfers between devices with their start and end apart: 15 -> 15, of which waited for: 9 -> 9; matrix products, arithmetic and copies ran while one was open for 3% -> 2% of each run, Pallas kernels for 7% -> 7%
where the time goes in v3:
time: 344 us; the launch traced here: 343 us
  blocking collectives  124 us (36%)
  waiting for transfers between devices  99.5 us (29%)
  Pallas kernels  62 us (18%)
  starting transfers between devices  45.6 us (13%)
  matrix products  8.02 us (2%)
    all_to_all x2, blocking collectives, spread(): return lax.all_to_all(value, 'ep', split_axis=0, concat_axis=0, tiled=True)  124 us
    all_to_all x4, waiting for transfers between devices, spread(): return lax.all_to_all(value, 'ep', split_axis=0, concat_axis=0, tiled=True)  86 us
    all_to_all x4, starting transfers between devices, spread(): return lax.all_to_all(value, 'ep', split_axis=0, concat_axis=0, tiled=True)  28.6 us
    ppermute x11, starting transfers between devices, swap(): return lax.ppermute(value, 'half', SWAP)  16.9 us
    ppermute x11, waiting for transfers between devices, swap(): return lax.ppermute(value, 'half', SWAP)  13.5 us
    pallas_call x1, Pallas kernels, train(): pl.pallas_call(train_kernel, out_shape=(jax.ShapeDtypeStruct((f, slots),...  12.7 us
    pallas_call x1, Pallas kernels, serve(): pl.pallas_call(serve_kernel, out_shape=pltpu.HBM((slots, d), BF16), in_sp...  11.3 us
    pallas_call x2, Pallas kernels, pack(): pl.pallas_call(lambda *refs: pack_kernel(group, members, *refs), out_shap...  9.5 us
  transfers between devices with their start and end apart: 15, of which 9 were waited for; matrix products, arithmetic and copies ran while one was open for 2% of the time, Pallas kernels for 7%

profile of v3, /device:TPU:1, one launch (start us, length us, event | category | flops | bytes accessed | tf_op | source)
XLA Modules:
  0.0 343.0 jit_solution(8768609490012440189)
XLA Ops:
  0.0 1.4 collective-permute-start.1
  2.0 3.0 collective-permute-done.3.refs_6_
  5.0 4.3 %shard_map.73 = bf16[512,2048]{1,0:T(8,128)(2,1)} custom-call(s32[2]{0:T(128)S(1)} %pad_add_fusion.refs_0_.scal, bf16[448,2048]{1,0:T(8,128)(2,1)} %bitcast.40, bf16[448,2048]{1,0:T(8,128)(2,1)S(1)} %collective-permute-done.1.refs_2_, s32[1,448]{1,0:T(1,128)} %bitcast.28, s32[1,448]{1,0:T(1,128)S(1)} %collective-permute-done.2.refs_4_, ...), custom_call_target="tpu_custom_call" | custom-call | tf_op jit(solution)/shard_map/pallas_call | solution.py:88
  9.4 11.3 %all-to-all-start = ((bf16[64,8,2048]{2,1,0:T(8,128)(2,1)}), bf16[64,8,2048]{2,1,0:T(8,128)(2,1)S(1)}, u32[]{:S(2)}, u32[]{:S(2)}) async-start(bf16[64,8,2048]{2,1,0:T(8,128)(2,1)} %bitcast.36), calls=%async_computation | async-start | bytes 4194304 | tf_op jit(solution)/shard_map/all_to_all | solution.py:530
  20.7 1.5 collective-permute-start
  23.0 25.2 %all-to-all-done = bf16[64,8,2048]{2,1,0:T(8,128)(2,1)S(1)} async-done(((bf16[64,8,2048]{2,1,0:T(8,128)(2,1)}), bf16[64,8,2048]{2,1,0:T(8,128)(2,1)S(1)}, u32[]{:S(2)}, u32[]{:S(2)}) %all-to-all-start) | async-done | bytes 2097184 | tf_op jit(solution)/shard_map/all_to_all | solution.py:530
  48.1 12.7 %train.1 = (bf16[768,512]{1,0:T(8,128)(2,1)S(1)}, bf16[512,1024]{1,0:T(8,128)(2,1)S(1)}, bf16[512,1024]{1,0:T(8,128)(2,1)S(1)}, bf16[512,1536]{1,0:T(8,128)(2,1)}) custom-call(s32[2]{0:T(128)S(1)} %pad_add_fusion.refs_0_.scal, s32[1,64]{1,0:T(1,128)S(1)} %copy-done.6, s32[1,64]{1,0:T(1,128)S(1)} %collective-permute-done.blocks_b, ...), custom_call_target="tpu_custom_call" | custom-call | tf_op jit(solution)/shard_map/train/pallas_call | solution.py:205
  60.8 3.2 collective-permute-start.4
  64.1 3.2 collective-permute-done.4.refs_3_
  67.8 2.5 collective-permute-done.7.x_b
  70.3 2.0 turn.1.refs_1_
  72.3 7.2 %update_gate.1.refs_6_ = bf16[16,4,144,256]{3,2,1,0:T(8,128)(2,1)} custom-call(s32[2]{0:T(128)S(1)} %pad_add_fusion.refs_0_.scal, bf16[1024,1024]{1,0:T(8,128)(2,1)S(1)} %turn.1.refs_1_, bf16[512,1536]{1,0:T(8,128)(2,1)S(1)} %copy-done.4, bf16[512,1536]{1,0:T(8,128)(2,1)S(1)} %collective-permute-done.4.refs_3_, bf16[2048,1536]{1,0:T(8,128)(2,1)} %bitcast.33), custom_call_target="tpu_custom_call" | custom-call | tf_op jit(solution)/shard_map/update_gate/pallas_call | solution.py:302
  79.5 5.6 %update_down.1 = bf16[16,4,144,256]{3,2,1,0:T(8,128)(2,1)} custom-call(s32[2]{0:T(128)S(1)} %pad_add_fusion.refs_0_.scal, bf16[768,512]{1,0:T(8,128)(2,1)S(1)} %get-tuple-element.16.refs_1_, bf16[768,512]{1,0:T(8,128)(2,1)S(1)} %collective-permute-done.5.refs_2_, bf16[512,1024]{1,0:T(8,128)(2,1)S(1)} %get-tuple-element.17.refs_3_, ...), custom_call_target="tpu_custom_call", output_to_operand_aliasing={{}: (6, {})} | custom-call | tf_op jit(solution)/shard_map/update_down/pallas_call | solution.py:356
  85.1 62.8 %all_to_all.30.src = bf16[64,144,256]{2,1,0:T(8,128)(2,1)S(1)} all-to-all(bf16[64,144,256]{2,1,0:T(8,128)(2,1)} %bitcast.31), channel_id=1, replica_groups=mesh['half'=2,'ep'=64] {'ep'}, dimensions={0} | all-to-all | bytes 9437184 | tf_op jit(solution)/shard_map/all_to_all | solution.py:530
  147.9 8.2 %choose.1 = bf16[64,144,256]{2,1,0:T(8,128)(2,1)S(1)} custom-call(s32[64]{0:T(128)S(1)} %copy-done.7, bf16[64,144,256]{2,1,0:T(8,128)(2,1)S(1)} %all_to_all.30.src), custom_call_target="tpu_custom_call" | custom-call | tf_op jit(solution)/shard_map/choose/pallas_call | solution.py:390
  156.1 61.6 %all_to_all.31 = bf16[64,144,256]{2,1,0:T(8,128)(2,1)} all-to-all(bf16[64,144,256]{2,1,0:T(8,128)(2,1)S(1)} %choose.1), channel_id=1, replica_groups=mesh['half'=2,'ep'=64] {'ep'}, dimensions={0} | all-to-all | bytes 9437184 | tf_op jit(solution)/shard_map/all_to_all | solution.py:530
  217.8 3.2 collective-permute-start.9
  220.9 5.2 %shard_map.74 = bf16[512,2048]{1,0:T(8,128)(2,1)} custom-call(s32[2]{0:T(128)S(1)} %pad_add_fusion.refs_0_.scal, bf16[448,2048]{1,0:T(8,128)(2,1)} %bitcast.41, bf16[448,2048]{1,0:T(8,128)(2,1)S(1)} %copy-done.3, s32[1,448]{1,0:T(1,128)} %bitcast.29, s32[1,448]{1,0:T(1,128)S(1)} %collective-permute-done.2.refs_4_, bf16[1,448]{1,0:T(2,128)(2,1)} %refs_5_.3, ...), custom_call_target="tpu_custom_call" | custom-call | tf_op jit(solution)/shard_map/pallas_call | solution.py:88
  226.1 4.8 %all-to-all-start.4 = ((bf16[64,8,2048]{2,1,0:T(8,128)(2,1)}), bf16[64,8,2048]{2,1,0:T(8,128)(2,1)S(1)}, u32[]{:S(2)}, u32[]{:S(2)}) async-start(bf16[64,8,2048]{2,1,0:T(8,128)(2,1)} %bitcast.37), calls=%async_computation.4 | async-start | bytes 4194304 | tf_op jit(solution)/shard_map/all_to_all | solution.py:530
  230.9 8.0 %convolution_convert_fusion = bf16[512,2048]{1,0:T(8,128)(2,1)} fusion(bf16[512,1536]{1,0:T(8,128)(2,1)} %get-tuple-element.19.refs_2_, bf16[1,2048,1536]{2,1,0:T(8,128)(2,1)} %param.11), kind=kOutput, calls=%fused_computation | convolution fusion | flops 3222274048 | bytes 9961472 | tf_op jit(solution)/shard_map/dot_general | solution.py:564
  238.9 22.0 %all-to-all-done.4 = bf16[64,8,2048]{2,1,0:T(8,128)(2,1)S(1)} async-done(((bf16[64,8,2048]{2,1,0:T(8,128)(2,1)}), bf16[64,8,2048]{2,1,0:T(8,128)(2,1)S(1)}, u32[]{:S(2)}, u32[]{:S(2)}) %all-to-all-start.4) | async-done | bytes 2097184 | tf_op jit(solution)/shard_map/all_to_all | solution.py:530
  260.9 1.4 copy-done
  262.4 6.2 %all-to-all-start.3 = ((bf16[64,8,2048]{2,1,0:T(8,128)(2,1)}), bf16[64,8,2048]{2,1,0:T(8,128)(2,1)S(1)}, u32[]{:S(2)}, u32[]{:S(2)}) async-start(bf16[64,8,2048]{2,1,0:T(8,128)(2,1)} %bitcast.42), calls=%async_computation.3 | async-start | bytes 4194304 | tf_op jit(solution)/shard_map/all_to_all | solution.py:530
  268.6 1.6 copy-done.1
  270.2 11.3 %serve.1 = bf16[512,2048]{1,0:T(8,128)(2,1)} custom-call(s32[2]{0:T(128)S(1)} %pad_add_fusion.refs_0_.scal, s32[1,64]{1,0:T(1,128)S(1)} %copy-done.6, s32[1,64]{1,0:T(1,128)S(1)} %collective-permute-done.blocks_b, bf16[512,2048]{1,0:T(8,128)(2,1)S(1)} %bitcast.26, bf16[16,4,144,256]{3,2,1,0:T(8,128)(2,1)} %bitcast.13.w_a, bf16[16,4,144,256]{3,2,1,0:T(8,128)(2,1)} %bitcast.14.w_b), custom_call_target="tpu_custom_call" | custom-call | tf_op jit(solution)/shard_map/serve/pallas_call | solution.py:466
  281.5 15.0 %all-to-all-done.3 = bf16[64,8,2048]{2,1,0:T(8,128)(2,1)S(1)} async-done(((bf16[64,8,2048]{2,1,0:T(8,128)(2,1)}), bf16[64,8,2048]{2,1,0:T(8,128)(2,1)S(1)}, u32[]{:S(2)}, u32[]{:S(2)}) %all-to-all-start.3) | async-done | bytes 2097184 | tf_op jit(solution)/shard_map/all_to_all | solution.py:530
  296.5 6.3 %all-to-all-start.5 = ((bf16[64,8,2048]{2,1,0:T(8,128)(2,1)}), bf16[64,8,2048]{2,1,0:T(8,128)(2,1)}, u32[]{:S(2)}, u32[]{:S(2)}) async-start(bf16[64,8,2048]{2,1,0:T(8,128)(2,1)} %bitcast.38), calls=%async_computation.5 | async-start | bytes 4194304 | tf_op jit(solution)/shard_map/all_to_all | solution.py:530
  302.8 2.9 collective-permute-start.8
  305.7 23.9 %all-to-all-done.5 = bf16[64,8,2048]{2,1,0:T(8,128)(2,1)} async-done(((bf16[64,8,2048]{2,1,0:T(8,128)(2,1)}), bf16[64,8,2048]{2,1,0:T(8,128)(2,1)}, u32[]{:S(2)}, u32[]{:S(2)}) %all-to-all-start.5) | async-done | bytes 2097184 | tf_op jit(solution)/shard_map/all_to_all | solution.py:530
  329.6 3.6 %collective-permute-start.10 = (bf16[512,2048]{1,0:T(8,128)(2,1)}, bf16[512,2048]{1,0:T(8,128)(2,1)S(1)}, u32[]{:S(2)}, u32[]{:S(2)}) collective-permute-start(bf16[512,2048]{1,0:T(8,128)(2,1)} %bitcast.16.refs_4_), channel_id=1, source_target_pairs={{0,64},{64,0},{1,65},{65,1},{2,66},{66,2},{3,67},{67,3},{4,68},{68... | collective-permute-start | bytes 6291464 | tf_op jit(solution)/shard_map/ppermute | solution.py:526
  333.3 4.0 %collective-permute-done.10.refs_5_ = bf16[512,2048]{1,0:T(8,128)(2,1)S(1)} collective-permute-done((bf16[512,2048]{1,0:T(8,128)(2,1)}, bf16[512,2048]{1,0:T(8,128)(2,1)S(1)}, u32[]{:S(2)}, u32[]{:S(2)}) %collective-permute-start.10) | collective-permute-done | bytes 2097184 | tf_op jit(solution)/shard_map/ppermute | solution.py:526
  337.3 5.6 %unpack.1 = bf16[448,2048]{1,0:T(8,128)(2,1)} custom-call(s32[2]{0:T(128)S(1)} %pad_add_fusion.refs_0_.scal, s32[1,448]{1,0:T(1,128)S(1)} %bitcast.30, bf16[512,2048]{1,0:T(8,128)(2,1)S(1)} %bitcast.25, bf16[512,2048]{1,0:T(8,128)(2,1)} %collective-permute-done.8.refs_3_, bf16[512,2048]{1,0:T(8,128)(2,1)} %bitcast.16.refs_4_, ...), custom_call_target="tpu_custom_call" | custom-call | tf_op jit(solution)/shard_map/unpack/pallas_call | solution.py:514
  (27 shorter events, 2.1 us)
Async XLA Ops:
  0.0 5.0 %collective-permute-start.1 = (bf16[448,2048]{1,0:T(8,128)(2,1)}, bf16[448,2048]{1,0:T(8,128)(2,1)S(1)}, u32[]{:S(2)}, u32[]{:S(2)}) collective-permute-start(bf16[448,2048]{1,0:T(8,128)(2,1)} %bitcast.39), channel_id=1, source_target_pairs={{0,64},{64,0},{1,65},{65,1},{2,66},{66,2},{3,67},{67,3},{4,68},{68... | collective-permute-start | bytes 5505032 | tf_op jit(solution)/shard_map/ppermute | solution.py:526
  1.4 3.6 %collective-permute-start.2 = (s32[1,448]{1,0:T(1,128)}, s32[1,448]{1,0:T(1,128)S(1)}, u32[]{:S(2)}, u32[]{:S(2)}) collective-permute-start(s32[1,448]{1,0:T(1,128)} %bitcast.27), channel_id=1, source_target_pairs={{0,64},{64,0},{1,65},{65,1},{2,66},{66,2},{3,67},{67,3},{4,68},{68... | collective-permute-start | bytes 5384 | tf_op jit(solution)/shard_map/ppermute | solution.py:526
  1.4 3.6 %collective-permute-start.3 = (bf16[1,448]{1,0:T(2,128)(2,1)}, bf16[1,448]{1,0:T(2,128)(2,1)S(1)}, u32[]{:S(2)}, u32[]{:S(2)}) collective-permute-start(bf16[1,448]{1,0:T(2,128)(2,1)} %refs_5_.3), channel_id=1, source_target_pairs={{0,64},{64,0},{1,65},{65,1},{2,66},{66,2},{3,67},{67,3},{4,68},{68... | collective-permute-start | bytes 2696 | tf_op jit(solution)/shard_map/ppermute | solution.py:526
  5.0 4.4 %copy-start.2 = (bf16[448,2048]{1,0:T(8,128)(2,1)}, bf16[448,2048]{1,0:T(8,128)(2,1)S(1)}, u32[]{:S(2)}) copy-start(bf16[448,2048]{1,0:T(8,128)(2,1)S(1)} %collective-permute-done.1.refs_2_) | copy-start | bytes 5505028
  9.4 11.3 %copy-start.6 = (s32[1,64]{1,0:T(1,128)S(1)}, s32[1,64]{1,0:T(1,128)}, u32[]{:S(2)}) copy-start(s32[1,64]{1,0:T(1,128)} %blocks_a.3) | copy-start | bytes 772
  9.4 38.7 %all-to-all-start = ((bf16[64,8,2048]{2,1,0:T(8,128)(2,1)}), bf16[64,8,2048]{2,1,0:T(8,128)(2,1)S(1)}, u32[]{:S(2)}, u32[]{:S(2)}) async-start(bf16[64,8,2048]{2,1,0:T(8,128)(2,1)} %bitcast.36), calls=%async_computation | async-start | bytes 4194304 | tf_op jit(solution)/shard_map/all_to_all | solution.py:530
  20.7 2.3 collective-permute-start
  60.8 6.5 %collective-permute-start.4 = (bf16[512,1536]{1,0:T(8,128)(2,1)}, bf16[512,1536]{1,0:T(8,128)(2,1)S(1)}, u32[]{:S(2)}, u32[]{:S(2)}) collective-permute-start(bf16[512,1536]{1,0:T(8,128)(2,1)} %get-tuple-element.19.refs_2_), channel_id=1, source_target_pairs={{0,64},{64,0},{1,65},{65,1},{2,66},{66,2},{3,67},{67,3},{4,68},{68... | collective-permute-start | bytes 4718600 | tf_op jit(solution)/shard_map/ppermute | solution.py:526
  64.1 6.2 %collective-permute-start.7 = (bf16[512,2048]{1,0:T(8,128)(2,1)S(1)}, bf16[512,2048]{1,0:T(8,128)(2,1)S(1)}, u32[]{:S(2)}, u32[]{:S(2)}) collective-permute-start(bf16[512,2048]{1,0:T(8,128)(2,1)S(1)} %bitcast.22), channel_id=1, source_target_pairs={{0,64},{64,0},{1,65},{65,1},{2,66},{66,2},{3,67},{67,3},{4,68},{68... | collective-permute-start | bytes 6291464 | tf_op jit(solution)/shard_map/ppermute | solution.py:526
  67.3 5.0 %copy-start.4 = (bf16[512,1536]{1,0:T(8,128)(2,1)S(1)}, bf16[512,1536]{1,0:T(8,128)(2,1)}, u32[]{:S(2)}) copy-start(bf16[512,1536]{1,0:T(8,128)(2,1)} %get-tuple-element.19.refs_2_) | copy-start | bytes 4718596
  67.3 12.2 %collective-permute-start.6 = (bf16[512,1024]{1,0:T(8,128)(2,1)S(1)}, bf16[512,1024]{1,0:T(8,128)(2,1)S(1)}, u32[]{:S(2)}, u32[]{:S(2)}) collective-permute-start(bf16[512,1024]{1,0:T(8,128)(2,1)S(1)} %get-tuple-element.18), channel_id=1, source_target_pairs={{0,64},{64,0},{1,65},{65,1},{2,66},{66,2},{3,67},{67,3},{4,68},{68... | collective-permute-start | bytes 3145736 | tf_op jit(solution)/shard_map/ppermute | solution.py:526
  67.7 11.8 %collective-permute-start.5 = (bf16[768,512]{1,0:T(8,128)(2,1)S(1)}, bf16[768,512]{1,0:T(8,128)(2,1)S(1)}, u32[]{:S(2)}, u32[]{:S(2)}) collective-permute-start(bf16[768,512]{1,0:T(8,128)(2,1)S(1)} %get-tuple-element.16.refs_1_), channel_id=1, source_target_pairs={{0,64},{64,0},{1,65},{65,1},{2,66},{66,2},{3,67},{67,3},{4,68},{68... | collective-permute-start | bytes 2359304 | tf_op jit(solution)/shard_map/ppermute | solution.py:526
  85.1 62.9 %copy-start.7 = (s32[64]{0:T(128)S(1)}, s32[64]{0:T(128)}, u32[]{:S(2)}) copy-start(s32[64]{0:T(128)} %slot_map.1) | copy-start | bytes 772
  156.1 64.8 %copy-start.3 = (bf16[448,2048]{1,0:T(8,128)(2,1)S(1)}, bf16[448,2048]{1,0:T(8,128)(2,1)}, u32[]{:S(2)}) copy-start(bf16[448,2048]{1,0:T(8,128)(2,1)} %copy-done.2) | copy-start | bytes 5505028
  217.8 50.8 %collective-permute-start.9 = (bf16[64,144,256]{2,1,0:T(8,128)(2,1)}, bf16[64,144,256]{2,1,0:T(8,128)(2,1)}, u32[]{:S(2)}, u32[]{:S(2)}) collective-permute-start(bf16[64,144,256]{2,1,0:T(8,128)(2,1)} %all_to_all.31), channel_id=1, source_target_pairs={{0,64},{64,0},{1,65},{65,1},{2,66},{66,2},{3,67},{67,3},{4,68},{68... | collective-permute-start | bytes 14155784 | tf_op jit(solution)/shard_map/ppermute | solution.py:526
  226.1 34.8 %all-to-all-start.4 = ((bf16[64,8,2048]{2,1,0:T(8,128)(2,1)}), bf16[64,8,2048]{2,1,0:T(8,128)(2,1)S(1)}, u32[]{:S(2)}, u32[]{:S(2)}) async-start(bf16[64,8,2048]{2,1,0:T(8,128)(2,1)} %bitcast.37), calls=%async_computation.4 | async-start | bytes 4194304 | tf_op jit(solution)/shard_map/all_to_all | solution.py:530
  260.9 1.4 copy-start
  262.4 34.1 %all-to-all-start.3 = ((bf16[64,8,2048]{2,1,0:T(8,128)(2,1)}), bf16[64,8,2048]{2,1,0:T(8,128)(2,1)S(1)}, u32[]{:S(2)}, u32[]{:S(2)}) async-start(bf16[64,8,2048]{2,1,0:T(8,128)(2,1)} %bitcast.42), calls=%async_computation.3 | async-start | bytes 4194304 | tf_op jit(solution)/shard_map/all_to_all | solution.py:530
  268.6 1.6 copy-start.1
  296.5 40.8 %copy-start.5 = (s32[1,448,1]{1,2,0:T(1,128)S(1)}, s32[1,448,1]{1,2,0:T(1,128)}, u32[]{:S(2)}) copy-start(s32[1,448,1]{1,2,0:T(1,128)} %param.8) | copy-start | bytes 5380
  296.5 33.2 %all-to-all-start.5 = ((bf16[64,8,2048]{2,1,0:T(8,128)(2,1)}), bf16[64,8,2048]{2,1,0:T(8,128)(2,1)}, u32[]{:S(2)}, u32[]{:S(2)}) async-start(bf16[64,8,2048]{2,1,0:T(8,128)(2,1)} %bitcast.38), calls=%async_computation.5 | async-start | bytes 4194304 | tf_op jit(solution)/shard_map/all_to_all | solution.py:530
  302.8 30.5 %collective-permute-start.8 = (bf16[512,2048]{1,0:T(8,128)(2,1)S(1)}, bf16[512,2048]{1,0:T(8,128)(2,1)}, u32[]{:S(2)}, u32[]{:S(2)}) collective-permute-start(bf16[512,2048]{1,0:T(8,128)(2,1)S(1)} %bitcast.24), channel_id=1, source_target_pairs={{0,64},{64,0},{1,65},{65,1},{2,66},{66,2},{3,67},{67,3},{4,68},{68... | collective-permute-start | bytes 6291464 | tf_op jit(solution)/shard_map/ppermute | solution.py:526
  329.6 7.6 %collective-permute-start.10 = (bf16[512,2048]{1,0:T(8,128)(2,1)}, bf16[512,2048]{1,0:T(8,128)(2,1)S(1)}, u32[]{:S(2)}, u32[]{:S(2)}) collective-permute-start(bf16[512,2048]{1,0:T(8,128)(2,1)} %bitcast.16.refs_4_), channel_id=1, source_target_pairs={{0,64},{64,0},{1,65},{65,1},{2,66},{66,2},{3,67},{67,3},{4,68},{68... | collective-permute-start | bytes 6291464 | tf_op jit(solution)/shard_map/ppermute | solution.py:526

commit v4 on v3

--- a/solution.py
+++ b/solution.py
@@ -52,47 +52,98 @@
     return jnp.sum(jnp.where(named, before, 0.0), axis=0, keepdims=True).astype(jnp.int32)
 
 
-def pack_kernel(group, members, scal, tok_a, tok_b, route_a, route_b, scale_a, scale_b, out, tok, sem):
+def prepare_kernel(members, scal, route_a, route_b, scale_a, scale_b, train_p, train_i, serve_p, serve_i, own_p, recv_p):
     half = scal[0]
-    own = half == group
+    slots = members * BOX
+    rows = route_a.shape[1]
+    order_a, order_b = order_of(route_a[...], members), order_of(route_b[...], members)
+    for group, placer, info in ((0, train_p, train_i), (1, serve_p, serve_i)):
+        own = half == group
+        target = jnp.where(own, route_a[...], route_b[...])
+        scale = jnp.where(own, scale_a[...].astype(F32), scale_b[...].astype(F32))
+        order = jnp.where(own, order_a, order_b) - PART * half
+        inside = (order >= 0) & (order < PART)
+        place = jnp.where(inside, target * BOX + order, -1)
+        placer[...] = (iota((slots, rows), 0) == place).astype(BF16)
+        tags = (iota((slots, rows), 0) == target * BOX + PART).astype(BF16)
+        lane = iota((LANES, rows), 0)
+        told = jnp.where((lane == order) & inside, scale, jnp.where(lane == COUNT, 1.0, 0.0)).astype(BF16)
+        info[...] = lax.dot_general(tags, told, NT, preferred_element_type=F32).astype(BF16)
+    eye = (iota((rows, rows), 0) == iota((rows, rows), 1)).astype(BF16)
+    pair = jnp.where(iota((BOX, rows), 0) == 0, route_a[...], order_a).astype(F32).astype(BF16)
+    column = lax.dot_general(eye, pair, NT, preferred_element_type=F32).astype(jnp.int32)
+    goal, rank = column[:, 0:1], column[:, 1:2]
+    for first, pick in ((PART * half, own_p), (PART * (1 - half), recv_p)):
+        k = rank - first
+        at = jnp.where((k >= 0) & (k < PART), goal * BOX + k, -1)
+        pick[...] = (iota((rows, slots), 1) == at).astype(BF16)
+
+
+def prepare(members, scal, route_a, route_b, scale_a, scale_b):
+    rows = route_a.shape[1]
+    slots = members * BOX
+    placer = jax.ShapeDtypeStruct((slots, rows), BF16)
+    info = jax.ShapeDtypeStruct((slots, LANES), BF16)
+    pick = jax.ShapeDtypeStruct((rows, slots), BF16)
+    return pl.pallas_call(
+        lambda *refs: prepare_kernel(members, *refs),
+        out_shape=(placer, info, placer, info, pick, pick),
+        in_specs=[smem()] + [vmem()] * 4,
+        out_specs=(vmem(),) * 6,
+        compiler_params=params(16),
+        name="prepare",
+    )(scal, route_a, route_b, scale_a, scale_b)
+
+
+def pack_kernel(group, scal, tok_a, tok_b, placer, info, out, tok, packed, sem):
+    own = scal[0] == group
+    wide = tok.shape[2]
+    steps = tok.shape[0]
+
+    def load(src, c):
+        return pltpu.make_async_copy(src.at[:, pl.ds(c * wide, wide)], tok.at[c], sem.at[c])
+
+    def save(c):
+        return pltpu.make_async_copy(packed.at[c], out.at[:, pl.ds(c * wide, wide)], sem.at[steps + c])
 
     @pl.when(own)
     def _():
-        pltpu.make_async_copy(tok_a, tok, sem).start()
+        for c in range(steps):
+            load(tok_a, c).start()
 
     @pl.when(jnp.logical_not(own))
     def _():
-        pltpu.make_async_copy(tok_b, tok, sem).start()
-
-    target = jnp.where(own, route_a[...], route_b[...])
-    scale = jnp.where(own, scale_a[...].astype(F32), scale_b[...].astype(F32))
-    rows = target.shape[1]
-    slots = members * BOX
-    order = order_of(target, members) - PART * half
-    inside = (order >= 0) & (order < PART)
-    place = jnp.where(inside, target * BOX + order, -1)
-    placer = (iota((slots, rows), 0) == place).astype(BF16)
-    tags = (iota((slots, rows), 0) == target * BOX + PART).astype(BF16)
-    lane = iota((LANES, rows), 0)
-    told = jnp.where((lane == order) & inside, scale, jnp.where(lane == COUNT, 1.0, 0.0)).astype(BF16)
-    info = lax.dot_general(tags, told, NT, preferred_element_type=F32)
-    pltpu.make_async_copy(tok_a, tok, sem).wait()
-    first = jnp.dot(placer, tok[:, :LANES], preferred_element_type=F32) + info
-    out[:, :LANES] = first.astype(BF16)
-    out[:, LANES:] = jnp.dot(placer, tok[:, LANES:], preferred_element_type=F32).astype(BF16)
-
-
-def pack(group, members, scal, tok_a, tok_b, route_a, route_b, scale_a, scale_b):
-    slots = members * BOX
+        for c in range(steps):
+            load(tok_b, c).start()
+
+    for c in range(steps):
+        load(tok_a, c).wait()
+        box = jnp.dot(placer[...], tok[c], preferred_element_type=F32)
+        if c == 0:
+            packed[c, :, :LANES] = (box[:, :LANES] + info[...].astype(F32)).astype(BF16)
+            packed[c, :, LANES:] = box[:, LANES:].astype(BF16)
+        else:
+            packed[c] = box.astype(BF16)
+        save(c).start()
+    for c in range(steps):
+        save(c).wait()
+
+
+def pack(group, scal, tok_a, tok_b, placer, info):
+    slots, rows = placer.shape
     width = tok_a.shape[1]
-    return pl.pallas_call(
-        lambda *refs: pack_kernel(group, members, *refs),
+    steps = 4
+    return pl.pallas_call(
+        lambda *refs: pack_kernel(group, *refs),
         out_shape=pltpu.HBM((slots, width), BF16),
-        in_specs=[smem(), anywhere(), anywhere(), vmem(), vmem(), vmem(), vmem()],
-        out_specs=vmem(),
-        scratch_shapes=[pltpu.VMEM(tok_a.shape, BF16), pltpu.SemaphoreType.DMA],
-        compiler_params=params(24),
-    )(scal, tok_a, tok_b, route_a, route_b, scale_a, scale_b)
+        in_specs=[smem(), anywhere(), anywhere(), vmem(), vmem()],
+        out_specs=anywhere(),
+        scratch_shapes=[
+            pltpu.VMEM((steps, rows, width // steps), BF16), pltpu.VMEM((steps, slots, width // steps), BF16),
+            pltpu.SemaphoreType.DMA((2 * steps,)),
+        ],
+        compiler_params=params(16),
+    )(scal, tok_a, tok_b, placer, info)
 
 
 def kept_and_scale(head, half, limit):
@@ -369,21 +420,12 @@
 
 
 def choose_kernel(slot_map, src, out, sem):
-    count = out.shape[0]
-
-    def copy(i):
-        return pltpu.make_async_copy(src.at[slot_map[i]], out.at[i], sem.at[i])
-
     def start(i, _):
-        copy(i).start()
-        return 0
-
-    def wait(i, _):
-        copy(i).wait()
-        return 0
-
-    lax.fori_loop(0, count, start, 0)
-    lax.fori_loop(0, count, wait, 0)
+        pltpu.make_async_copy(src.at[slot_map[i]], out.at[i], sem).start()
+        return 0
+
+    lax.fori_loop(0, out.shape[0], start, 0, unroll=8)
+    pltpu.make_async_copy(src, out, sem).wait()
 
 
 def choose(slot_map, pieces):
@@ -392,7 +434,7 @@
         out_shape=jax.ShapeDtypeStruct(pieces.shape, BF16),
         in_specs=[smem(), anywhere()],
         out_specs=vmem(),
-        scratch_shapes=[pltpu.SemaphoreType.DMA((pieces.shape[0],))],
+        scratch_shapes=[pltpu.SemaphoreType.DMA],
         compiler_params=params(16),
         name="choose",
     )(slot_map, pieces)
@@ -477,49 +519,55 @@
     )(scal, blocks_a, blocks_b, x, w_a, w_b)
 
 
-def unpack_kernel(members, scal, route, t_own, t_recv, p_own, p_recv, out, low, high, sem):
+def unpack_kernel(first, scal, pick, train, serve, given, out, box, done, sem):
     half = scal[0]
+    steps = box.shape[0]
+    wide = box.shape[2]
+
+    def load(src, c):
+        return pltpu.make_async_copy(src.at[:, pl.ds(c * wide, wide)], box.at[c], sem.at[c])
+
+    def save(c):
+        return pltpu.make_async_copy(done.at[c], out.at[:, pl.ds(c * wide, wide)], sem.at[steps + c])
 
     @pl.when(half == 0)
     def _():
-        pltpu.make_async_copy(t_own, low, sem.at[0]).start()
-        pltpu.make_async_copy(t_recv, high, sem.at[1]).start()
+        for c in range(steps):
+            load(train, c).start()
 
     @pl.when(half == 1)
     def _():
-        pltpu.make_async_copy(p_recv, low, sem.at[0]).start()
-        pltpu.make_async_copy(p_own, high, sem.at[1]).start()
-
-    target = route[...]
-    rows = target.shape[1]
-    order = order_of(target, members)
-    eye = (iota((rows, rows), 0) == iota((rows, rows), 1)).astype(BF16)
-    pair = jnp.where(iota((BOX, rows), 0) == 0, target, order).astype(F32).astype(BF16)
-    column = lax.dot_general(eye, pair, NT, preferred_element_type=F32).astype(jnp.int32)
-    goal, rank = column[:, 0:1], column[:, 1:2]
-    slots = members * BOX
-    at = iota((rows, slots), 1)
-    pick_low = (at == jnp.where(rank < PART, goal * BOX + rank, -1)).astype(BF16)
-    pick_high = (at == jnp.where(rank >= PART, goal * BOX + rank - PART, -1)).astype(BF16)
-    pltpu.make_async_copy(t_own, low, sem.at[0]).wait()
-    pltpu.make_async_copy(t_own, high, sem.at[1]).wait()
-    total = jnp.dot(pick_low, low[...], preferred_element_type=F32)
-    total = total + jnp.dot(pick_high, high[...], preferred_element_type=F32)
-    out[...] = total.astype(BF16)
-
-
-def unpack(members, scal, route, t_own, t_recv, p_own, p_recv):
-    slots, d = t_own.shape
-    rows = route.shape[1]
-    return pl.pallas_call(
-        lambda *refs: unpack_kernel(members, *refs),
+        for c in range(steps):
+            load(serve, c).start()
+
+    for c in range(steps):
+        load(train, c).wait()
+        rows = jnp.dot(pick[...], box[c], preferred_element_type=F32)
+        if not first:
+            rows = rows + given[:, c * wide:(c + 1) * wide].astype(F32)
+        done[c] = rows.astype(BF16)
+        save(c).start()
+    for c in range(steps):
+        save(c).wait()
+
+
+def unpack(scal, pick, train, serve, given=None):
+    rows, slots = pick.shape
+    d = train.shape[1]
+    steps = 4
+    first = given is None
+    return pl.pallas_call(
+        lambda *refs: unpack_kernel(first, *refs),
         out_shape=jax.ShapeDtypeStruct((rows, d), BF16),
-        in_specs=[smem(), vmem()] + [anywhere()] * 4,
-        out_specs=vmem(),
-        scratch_shapes=[pltpu.VMEM((slots, d), BF16), pltpu.VMEM((slots, d), BF16), pltpu.SemaphoreType.DMA((2,))],
-        compiler_params=params(24),
-        name="unpack",
-    )(scal, route, t_own, t_recv, p_own, p_recv)
+        in_specs=[smem(), vmem(), anywhere(), anywhere(), smem() if first else vmem()],
+        out_specs=anywhere(),
+        scratch_shapes=[
+            pltpu.VMEM((steps, slots, d // steps), BF16), pltpu.VMEM((steps, rows, d // steps), BF16),
+            pltpu.SemaphoreType.DMA((2 * steps,)),
+        ],
+        compiler_params=params(16),
+        name="unpack" if first else "unpack_rest",
+    )(scal, pick, train, serve, scal if first else given)
 
 
 def swap(value):
@@ -542,10 +590,17 @@
     eta = 0.03 / math.sqrt(row_count)
 
     gate_h, down_h = in_hbm(gate_up, down_weight)
-    tokens_b, route_b, scale_b, blocks_b = swap(tokens), swap(route), swap(row_scale), swap(blocks)
-    parts = (scal, *in_hbm(tokens), tokens_b, *in_hbm(route), route_b, *in_hbm(row_scale), scale_b)
-    train_rows = spread(pack(0, members, *parts).reshape(boxed)).reshape(flat)
-    packed = pack(1, members, *parts)
+    tokens_b = swap(tokens)
+    route_b = swap(route)
+    scale_b = swap(row_scale)
+    blocks_b = swap(blocks)
+    train_p, train_i, serve_p, serve_i, own_p, recv_p = prepare(
+        members, scal, *in_hbm(route), route_b, *in_hbm(row_scale), scale_b
+    )
+    tokens_h = in_hbm(tokens)[0]
+    packed = pack(0, scal, tokens_h, tokens_b, train_p, train_i)
+    train_rows = spread(packed.reshape(boxed)).reshape(flat)
+    packed = pack(1, scal, tokens_h, tokens_b, serve_p, serve_i)
     serve_rows = spread(packed.reshape(boxed)).reshape(flat)
 
     train_rows_b = swap(train_rows)
@@ -569,8 +624,10 @@
     slots_b = swap(slots)
     served = serve(scal, blocks, blocks_b, serve_rows, slots.reshape(laid), slots_b.reshape(laid))
     serve_back = spread(served.reshape(boxed)).reshape(flat)
-    train_other, serve_other = swap(train_back), swap(serve_back)
-    return unpack(members, scal, route, train_back, train_other, serve_back, serve_other)[None]
+    train_other = swap(train_back)
+    serve_other = swap(serve_back)
+    rows = unpack(scal, own_p, train_back, serve_back)
+    return unpack(scal, recv_p, train_other, serve_other, rows)[None]
 
 
 def solution(mesh):

time: 344 us -> 341 us (level)
    ppermute x11, waiting for transfers between devices: 13.5 us -> 10.1 us  [swap(): return lax.ppermute(value, 'half', SWAP)]
    pallas_call x3 -> x5, Pallas kernels: 15.1 us -> 16.7 us  [the longest x2 7.61 us: pack(): pl.pallas_call(lambda *refs: pack_kernel(group, *refs), out_shape=pltpu.H...]
  transfers between devices with their start and end apart: 15 -> 15, of which waited for: 9 -> 9; matrix products, arithmetic and copies ran while one was open for 2% -> 2% of each run, Pallas kernels for 7% -> 9%
where the time goes in v4:
time: 341 us; the launch traced here: 340 us
  blocking collectives  124 us (36%)
  waiting for transfers between devices  96.2 us (28%)
  Pallas kernels  62.2 us (18%)
  starting transfers between devices  45.7 us (13%)
  matrix products  8.02 us (2%)
    all_to_all x2, blocking collectives, spread(): return lax.all_to_all(value, 'ep', split_axis=0, concat_axis=0, tiled=True)  124 us
    all_to_all x4, waiting for transfers between devices, spread(): return lax.all_to_all(value, 'ep', split_axis=0, concat_axis=0, tiled=True)  86.1 us
    all_to_all x4, starting transfers between devices, spread(): return lax.all_to_all(value, 'ep', split_axis=0, concat_axis=0, tiled=True)  28.5 us
    ppermute x11, starting transfers between devices, swap(): return lax.ppermute(value, 'half', SWAP)  17.3 us
    pallas_call x1, Pallas kernels, train(): pl.pallas_call(train_kernel, out_shape=(jax.ShapeDtypeStruct((f, slots),...  12.7 us
    pallas_call x1, Pallas kernels, serve(): pl.pallas_call(serve_kernel, out_shape=pltpu.HBM((slots, d), BF16), in_sp...  11.3 us
    ppermute x11, waiting for transfers between devices, swap(): return lax.ppermute(value, 'half', SWAP)  10.1 us
    dot_general x1, matrix products, step(): lax.dot_general(both, gate_up, NT, preferred_element_type=F32).astype(BF16)  8.02 us
  transfers between devices with their start and end apart: 15, of which 9 were waited for; matrix products, arithmetic and copies ran while one was open for 2% of the time, Pallas kernels for 9%

profile of v4, /device:TPU:1, one launch (start us, length us, event | category | flops | bytes accessed | tf_op | source)
XLA Modules:
  0.0 339.8 jit_solution(4985202514590864607)
XLA Ops:
  2.0 3.0 collective-permute-done.1.refs_4_
  5.0 2.3 prepare.1
  7.4 3.4 shard_map.73
  10.8 11.3 %all-to-all-start = ((bf16[64,8,2048]{2,1,0:T(8,128)(2,1)}), bf16[64,8,2048]{2,1,0:T(8,128)(2,1)S(1)}, u32[]{:S(2)}, u32[]{:S(2)}) async-start(bf16[64,8,2048]{2,1,0:T(8,128)(2,1)} %bitcast.32), calls=%async_computation | async-start | bytes 4194304 | tf_op jit(solution)/shard_map/all_to_all | solution.py:578
  22.0 1.7 collective-permute-start.2
  24.6 25.0 %all-to-all-done = bf16[64,8,2048]{2,1,0:T(8,128)(2,1)S(1)} async-done(((bf16[64,8,2048]{2,1,0:T(8,128)(2,1)}), bf16[64,8,2048]{2,1,0:T(8,128)(2,1)S(1)}, u32[]{:S(2)}, u32[]{:S(2)}) %all-to-all-start) | async-done | bytes 2097184 | tf_op jit(solution)/shard_map/all_to_all | solution.py:578
  49.5 12.7 %train.1 = (bf16[768,512]{1,0:T(8,128)(2,1)S(1)}, bf16[512,1024]{1,0:T(8,128)(2,1)S(1)}, bf16[512,1024]{1,0:T(8,128)(2,1)S(1)}, bf16[512,1536]{1,0:T(8,128)(2,1)}) custom-call(s32[2]{0:T(128)S(1)} %pad_add_fusion.refs_0_.scal.refs_4_, s32[1,64]{1,0:T(1,128)S(1)} %copy-done.7, s32[1,64]{1,0:T(1,128)S(1)} %collective-permute-done.2.blocks_b, ...), custom_call_target="tpu_custom_call" | custom-call | tf_op jit(solution)/shard_map/train/pallas_call | solution.py:256
  62.2 3.2 collective-permute-start.4
  65.5 3.2 collective-permute-done.4.refs_3_
  69.2 2.5 collective-permute-done.7.x_b
  71.7 1.9 turn.1.refs_1_
  73.6 7.1 %update_gate.1.refs_6_ = bf16[16,4,144,256]{3,2,1,0:T(8,128)(2,1)} custom-call(s32[2]{0:T(128)S(1)} %pad_add_fusion.refs_0_.scal.refs_4_, bf16[1024,1024]{1,0:T(8,128)(2,1)S(1)} %turn.1.refs_1_, bf16[512,1536]{1,0:T(8,128)(2,1)S(1)} %copy-done.4, bf16[512,1536]{1,0:T(8,128)(2,1)S(1)} %collective-permute-done.4.refs_3_, bf16[2048,1536]{1,0:T(8,128)(2,1)} %bitcast.29), custom_call_target="tpu_custom_call" | custom-call | tf_op jit(solution)/shard_map/update_gate/pallas_call | solution.py:353
  80.8 5.5 %update_down.1 = bf16[16,4,144,256]{3,2,1,0:T(8,128)(2,1)} custom-call(s32[2]{0:T(128)S(1)} %pad_add_fusion.refs_0_.scal.refs_4_, bf16[768,512]{1,0:T(8,128)(2,1)S(1)} %get-tuple-element.25.refs_1_, bf16[768,512]{1,0:T(8,128)(2,1)S(1)} %collective-permute-done.5.refs_2_, ...), custom_call_target="tpu_custom_call", output_to_operand_aliasing={{}: (6, {})} | custom-call | tf_op jit(solution)/shard_map/update_down/pallas_call | solution.py:407
  86.3 62.7 %all_to_all.30.src = bf16[64,144,256]{2,1,0:T(8,128)(2,1)S(1)} all-to-all(bf16[64,144,256]{2,1,0:T(8,128)(2,1)} %bitcast.27), channel_id=1, replica_groups=mesh['half'=2,'ep'=64] {'ep'}, dimensions={0} | all-to-all | bytes 9437184 | tf_op jit(solution)/shard_map/all_to_all | solution.py:578
  149.1 6.9 %choose.1 = bf16[64,144,256]{2,1,0:T(8,128)(2,1)S(1)} custom-call(s32[64]{0:T(128)S(1)} %copy-done.8, bf16[64,144,256]{2,1,0:T(8,128)(2,1)S(1)} %all_to_all.30.src), custom_call_target="tpu_custom_call" | custom-call | tf_op jit(solution)/shard_map/choose/pallas_call | solution.py:432
  156.0 61.4 %all_to_all.31 = bf16[64,144,256]{2,1,0:T(8,128)(2,1)} all-to-all(bf16[64,144,256]{2,1,0:T(8,128)(2,1)S(1)} %choose.1), channel_id=1, replica_groups=mesh['half'=2,'ep'=64] {'ep'}, dimensions={0} | all-to-all | bytes 9437184 | tf_op jit(solution)/shard_map/all_to_all | solution.py:578
  217.5 3.3 collective-permute-start.9
  220.8 4.2 %shard_map.74 = bf16[512,2048]{1,0:T(8,128)(2,1)} custom-call(s32[2]{0:T(128)S(1)} %pad_add_fusion.refs_0_.scal.refs_4_, bf16[448,2048]{1,0:T(8,128)(2,1)} %bitcast.37, bf16[448,2048]{1,0:T(8,128)(2,1)S(1)} %copy-done.3, bf16[512,448]{1,0:T(8,128)(2,1)S(1)} %get-tuple-element.30.refs_3_, bf16[512,128]{1,0:T(8,128)(2,1)S(1)} %copy-done.6), custom_call_target="tpu_custom_call" | custom-call | tf_op jit(solution)/shard_map/pallas_call | solution.py:136
  225.0 4.9 %all-to-all-start.4 = ((bf16[64,8,2048]{2,1,0:T(8,128)(2,1)}), bf16[64,8,2048]{2,1,0:T(8,128)(2,1)S(1)}, u32[]{:S(2)}, u32[]{:S(2)}) async-start(bf16[64,8,2048]{2,1,0:T(8,128)(2,1)} %bitcast.33), calls=%async_computation.4 | async-start | bytes 4194304 | tf_op jit(solution)/shard_map/all_to_all | solution.py:578
  229.9 8.0 %convolution_convert_fusion = bf16[512,2048]{1,0:T(8,128)(2,1)} fusion(bf16[512,1536]{1,0:T(8,128)(2,1)} %get-tuple-element.28.refs_2_, bf16[1,2048,1536]{2,1,0:T(8,128)(2,1)} %param.11), kind=kOutput, calls=%fused_computation | convolution fusion | flops 3222274048 | bytes 9961472 | tf_op jit(solution)/shard_map/dot_general | solution.py:619
  237.9 22.2 %all-to-all-done.4 = bf16[64,8,2048]{2,1,0:T(8,128)(2,1)S(1)} async-done(((bf16[64,8,2048]{2,1,0:T(8,128)(2,1)}), bf16[64,8,2048]{2,1,0:T(8,128)(2,1)S(1)}, u32[]{:S(2)}, u32[]{:S(2)}) %all-to-all-start.4) | async-done | bytes 2097184 | tf_op jit(solution)/shard_map/all_to_all | solution.py:578
  260.2 1.4 copy-done
  261.6 6.1 %all-to-all-start.3 = ((bf16[64,8,2048]{2,1,0:T(8,128)(2,1)}), bf16[64,8,2048]{2,1,0:T(8,128)(2,1)S(1)}, u32[]{:S(2)}, u32[]{:S(2)}) async-start(bf16[64,8,2048]{2,1,0:T(8,128)(2,1)} %bitcast.38), calls=%async_computation.3 | async-start | bytes 4194304 | tf_op jit(solution)/shard_map/all_to_all | solution.py:578
  267.7 1.6 copy-done.1
  269.3 11.3 %serve.1 = bf16[512,2048]{1,0:T(8,128)(2,1)} custom-call(s32[2]{0:T(128)S(1)} %pad_add_fusion.refs_0_.scal.refs_4_, s32[1,64]{1,0:T(1,128)S(1)} %copy-done.7, s32[1,64]{1,0:T(1,128)S(1)} %collective-permute-done.2.blocks_b, bf16[512,2048]{1,0:T(8,128)(2,1)S(1)} %bitcast.26, bf16[16,4,144,256]{3,2,1,0:T(8,128)(2,1)} %bitcast.13.w_a, ...), custom_call_target="tpu_custom_call" | custom-call | tf_op jit(solution)/shard_map/serve/pallas_call | solution.py:508
  280.6 15.0 %all-to-all-done.3 = bf16[64,8,2048]{2,1,0:T(8,128)(2,1)S(1)} async-done(((bf16[64,8,2048]{2,1,0:T(8,128)(2,1)}), bf16[64,8,2048]{2,1,0:T(8,128)(2,1)S(1)}, u32[]{:S(2)}, u32[]{:S(2)}) %all-to-all-start.3) | async-done | bytes 2097184 | tf_op jit(solution)/shard_map/all_to_all | solution.py:578
  295.6 6.2 %all-to-all-start.5 = ((bf16[64,8,2048]{2,1,0:T(8,128)(2,1)}), bf16[64,8,2048]{2,1,0:T(8,128)(2,1)}, u32[]{:S(2)}, u32[]{:S(2)}) async-start(bf16[64,8,2048]{2,1,0:T(8,128)(2,1)} %bitcast.34), calls=%async_computation.5 | async-start | bytes 4194304 | tf_op jit(solution)/shard_map/all_to_all | solution.py:578
  301.9 2.9 collective-permute-start.8
  304.8 23.9 %all-to-all-done.5 = bf16[64,8,2048]{2,1,0:T(8,128)(2,1)} async-done(((bf16[64,8,2048]{2,1,0:T(8,128)(2,1)}), bf16[64,8,2048]{2,1,0:T(8,128)(2,1)}, u32[]{:S(2)}, u32[]{:S(2)}) %all-to-all-start.5) | async-done | bytes 2097184 | tf_op jit(solution)/shard_map/all_to_all | solution.py:578
  328.7 3.6 %collective-permute-start.10 = (bf16[512,2048]{1,0:T(8,128)(2,1)}, bf16[512,2048]{1,0:T(8,128)(2,1)S(1)}, u32[]{:S(2)}, u32[]{:S(2)}) collective-permute-start(bf16[512,2048]{1,0:T(8,128)(2,1)} %bitcast.16.refs_3_), channel_id=1, source_target_pairs={{0,64},{64,0},{1,65},{65,1},{2,66},{66,2},{3,67},{67,3},{4,68},{68... | collective-permute-start | bytes 6291464 | tf_op jit(solution)/shard_map/ppermute | solution.py:574
  332.3 3.4 %unpack.1.refs_4_ = bf16[448,2048]{1,0:T(8,128)(2,1)S(1)} custom-call(s32[2]{0:T(128)S(1)} %pad_add_fusion.refs_0_.scal.refs_4_, bf16[448,512]{1,0:T(8,128)(2,1)S(1)} %get-tuple-element.32.refs_1_, bf16[512,2048]{1,0:T(8,128)(2,1)S(1)} %bitcast.25, bf16[512,2048]{1,0:T(8,128)(2,1)} %bitcast.16.refs_3_, s32[2]{0:T(128)S(1)} %pad_add_fusion.refs_0_.scal.refs_4_), custom_call_target="tpu_custom_call" | custom-call | tf_op jit(solution)/shard_map/unpack/pallas_call | solution.py:559
  336.3 3.3 unpack_rest.1
  (31 shorter events, 4.0 us)
Async XLA Ops:
  0.0 7.3 %collective-permute-start.3 = (bf16[448,2048]{1,0:T(8,128)(2,1)}, bf16[448,2048]{1,0:T(8,128)(2,1)S(1)}, u32[]{:S(2)}, u32[]{:S(2)}) collective-permute-start(bf16[448,2048]{1,0:T(8,128)(2,1)} %bitcast.35), channel_id=1, source_target_pairs={{0,64},{64,0},{1,65},{65,1},{2,66},{66,2},{3,67},{67,3},{4,68},{68... | collective-permute-start | bytes 5505032 | tf_op jit(solution)/shard_map/ppermute | solution.py:574
  1.4 3.6 %collective-permute-start = (s32[1,448]{1,0:T(1,128)}, s32[1,448]{1,0:T(1,128)S(1)}, u32[]{:S(2)}, u32[]{:S(2)}) collective-permute-start(s32[1,448]{1,0:T(1,128)} %bitcast.39), channel_id=1, source_target_pairs={{0,64},{64,0},{1,65},{65,1},{2,66},{66,2},{3,67},{67,3},{4,68},{68... | collective-permute-start | bytes 5384 | tf_op jit(solution)/shard_map/ppermute | solution.py:574
  1.4 3.6 %collective-permute-start.1 = (bf16[1,448]{1,0:T(2,128)(2,1)}, bf16[1,448]{1,0:T(2,128)(2,1)S(1)}, u32[]{:S(2)}, u32[]{:S(2)}) collective-permute-start(bf16[1,448]{1,0:T(2,128)(2,1)} %refs_3_.1), channel_id=1, source_target_pairs={{0,64},{64,0},{1,65},{65,1},{2,66},{66,2},{3,67},{67,3},{4,68},{68... | collective-permute-start | bytes 2696 | tf_op jit(solution)/shard_map/ppermute | solution.py:574
  7.3 3.4 %copy-start.5 = (bf16[512,128]{1,0:T(8,128)(2,1)}, bf16[512,128]{1,0:T(8,128)(2,1)S(1)}, u32[]{:S(2)}) copy-start(bf16[512,128]{1,0:T(8,128)(2,1)S(1)} %get-tuple-element.31.refs_4_) | copy-start | bytes 393220
  7.3 3.4 %copy-start.2 = (bf16[448,2048]{1,0:T(8,128)(2,1)}, bf16[448,2048]{1,0:T(8,128)(2,1)S(1)}, u32[]{:S(2)}) copy-start(bf16[448,2048]{1,0:T(8,128)(2,1)S(1)} %collective-permute-done.3.refs_2_) | copy-start | bytes 5505028
  10.8 11.3 %copy-start.7 = (s32[1,64]{1,0:T(1,128)S(1)}, s32[1,64]{1,0:T(1,128)}, u32[]{:S(2)}) copy-start(s32[1,64]{1,0:T(1,128)} %blocks_a.3) | copy-start | bytes 772
  10.8 38.8 %all-to-all-start = ((bf16[64,8,2048]{2,1,0:T(8,128)(2,1)}), bf16[64,8,2048]{2,1,0:T(8,128)(2,1)S(1)}, u32[]{:S(2)}, u32[]{:S(2)}) async-start(bf16[64,8,2048]{2,1,0:T(8,128)(2,1)} %bitcast.32), calls=%async_computation | async-start | bytes 4194304 | tf_op jit(solution)/shard_map/all_to_all | solution.py:578
  22.0 2.5 collective-permute-start.2
  62.2 6.5 %collective-permute-start.4 = (bf16[512,1536]{1,0:T(8,128)(2,1)}, bf16[512,1536]{1,0:T(8,128)(2,1)S(1)}, u32[]{:S(2)}, u32[]{:S(2)}) collective-permute-start(bf16[512,1536]{1,0:T(8,128)(2,1)} %get-tuple-element.28.refs_2_), channel_id=1, source_target_pairs={{0,64},{64,0},{1,65},{65,1},{2,66},{66,2},{3,67},{67,3},{4,68},{68... | collective-permute-start | bytes 4718600 | tf_op jit(solution)/shard_map/ppermute | solution.py:574
  65.4 6.2 %collective-permute-start.7 = (bf16[512,2048]{1,0:T(8,128)(2,1)S(1)}, bf16[512,2048]{1,0:T(8,128)(2,1)S(1)}, u32[]{:S(2)}, u32[]{:S(2)}) collective-permute-start(bf16[512,2048]{1,0:T(8,128)(2,1)S(1)} %bitcast.22), channel_id=1, source_target_pairs={{0,64},{64,0},{1,65},{65,1},{2,66},{66,2},{3,67},{67,3},{4,68},{68... | collective-permute-start | bytes 6291464 | tf_op jit(solution)/shard_map/ppermute | solution.py:574
  68.7 4.9 %copy-start.4 = (bf16[512,1536]{1,0:T(8,128)(2,1)S(1)}, bf16[512,1536]{1,0:T(8,128)(2,1)}, u32[]{:S(2)}) copy-start(bf16[512,1536]{1,0:T(8,128)(2,1)} %get-tuple-element.28.refs_2_) | copy-start | bytes 4718596
  68.7 12.1 %collective-permute-start.6 = (bf16[512,1024]{1,0:T(8,128)(2,1)S(1)}, bf16[512,1024]{1,0:T(8,128)(2,1)S(1)}, u32[]{:S(2)}, u32[]{:S(2)}) collective-permute-start(bf16[512,1024]{1,0:T(8,128)(2,1)S(1)} %get-tuple-element.27), channel_id=1, source_target_pairs={{0,64},{64,0},{1,65},{65,1},{2,66},{66,2},{3,67},{67,3},{4,68},{68... | collective-permute-start | bytes 3145736 | tf_op jit(solution)/shard_map/ppermute | solution.py:574
  69.1 11.7 %collective-permute-start.5 = (bf16[768,512]{1,0:T(8,128)(2,1)S(1)}, bf16[768,512]{1,0:T(8,128)(2,1)S(1)}, u32[]{:S(2)}, u32[]{:S(2)}) collective-permute-start(bf16[768,512]{1,0:T(8,128)(2,1)S(1)} %get-tuple-element.25.refs_1_), channel_id=1, source_target_pairs={{0,64},{64,0},{1,65},{65,1},{2,66},{66,2},{3,67},{67,3},{4,68},{68... | collective-permute-start | bytes 2359304 | tf_op jit(solution)/shard_map/ppermute | solution.py:574
  86.3 62.7 %copy-start.8 = (s32[64]{0:T(128)S(1)}, s32[64]{0:T(128)}, u32[]{:S(2)}) copy-start(s32[64]{0:T(128)} %slot_map.1) | copy-start | bytes 772
  156.0 64.8 %copy-start.3 = (bf16[448,2048]{1,0:T(8,128)(2,1)S(1)}, bf16[448,2048]{1,0:T(8,128)(2,1)}, u32[]{:S(2)}) copy-start(bf16[448,2048]{1,0:T(8,128)(2,1)} %copy-done.2) | copy-start | bytes 5505028
  156.0 64.8 %copy-start.6 = (bf16[512,128]{1,0:T(8,128)(2,1)S(1)}, bf16[512,128]{1,0:T(8,128)(2,1)}, u32[]{:S(2)}) copy-start(bf16[512,128]{1,0:T(8,128)(2,1)} %copy-done.5) | copy-start | bytes 393220
  217.5 50.2 %collective-permute-start.9 = (bf16[64,144,256]{2,1,0:T(8,128)(2,1)}, bf16[64,144,256]{2,1,0:T(8,128)(2,1)}, u32[]{:S(2)}, u32[]{:S(2)}) collective-permute-start(bf16[64,144,256]{2,1,0:T(8,128)(2,1)} %all_to_all.31), channel_id=1, source_target_pairs={{0,64},{64,0},{1,65},{65,1},{2,66},{66,2},{3,67},{67,3},{4,68},{68... | collective-permute-start | bytes 14155784 | tf_op jit(solution)/shard_map/ppermute | solution.py:574
  225.0 35.1 %all-to-all-start.4 = ((bf16[64,8,2048]{2,1,0:T(8,128)(2,1)}), bf16[64,8,2048]{2,1,0:T(8,128)(2,1)S(1)}, u32[]{:S(2)}, u32[]{:S(2)}) async-start(bf16[64,8,2048]{2,1,0:T(8,128)(2,1)} %bitcast.33), calls=%async_computation.4 | async-start | bytes 4194304 | tf_op jit(solution)/shard_map/all_to_all | solution.py:578
  260.2 1.4 copy-start
  261.6 34.0 %all-to-all-start.3 = ((bf16[64,8,2048]{2,1,0:T(8,128)(2,1)}), bf16[64,8,2048]{2,1,0:T(8,128)(2,1)S(1)}, u32[]{:S(2)}, u32[]{:S(2)}) async-start(bf16[64,8,2048]{2,1,0:T(8,128)(2,1)} %bitcast.38), calls=%async_computation.3 | async-start | bytes 4194304 | tf_op jit(solution)/shard_map/all_to_all | solution.py:578
  267.7 1.6 copy-start.1
  295.6 33.1 %all-to-all-start.5 = ((bf16[64,8,2048]{2,1,0:T(8,128)(2,1)}), bf16[64,8,2048]{2,1,0:T(8,128)(2,1)}, u32[]{:S(2)}, u32[]{:S(2)}) async-start(bf16[64,8,2048]{2,1,0:T(8,128)(2,1)} %bitcast.34), calls=%async_computation.5 | async-start | bytes 4194304 | tf_op jit(solution)/shard_map/all_to_all | solution.py:578
  301.9 33.9 %collective-permute-start.8 = (bf16[512,2048]{1,0:T(8,128)(2,1)S(1)}, bf16[512,2048]{1,0:T(8,128)(2,1)}, u32[]{:S(2)}, u32[]{:S(2)}) collective-permute-start(bf16[512,2048]{1,0:T(8,128)(2,1)S(1)} %bitcast.24), channel_id=1, source_target_pairs={{0,64},{64,0},{1,65},{65,1},{2,66},{66,2},{3,67},{67,3},{4,68},{68... | collective-permute-start | bytes 6291464 | tf_op jit(solution)/shard_map/ppermute | solution.py:574
  328.7 7.6 %collective-permute-start.10 = (bf16[512,2048]{1,0:T(8,128)(2,1)}, bf16[512,2048]{1,0:T(8,128)(2,1)S(1)}, u32[]{:S(2)}, u32[]{:S(2)}) collective-permute-start(bf16[512,2048]{1,0:T(8,128)(2,1)} %bitcast.16.refs_3_), channel_id=1, source_target_pairs={{0,64},{64,0},{1,65},{65,1},{2,66},{66,2},{3,67},{67,3},{4,68},{68... | collective-permute-start | bytes 6291464 | tf_op jit(solution)/shard_map/ppermute | solution.py:574

commit v5 on v4

--- a/solution.py
+++ b/solution.py
@@ -75,8 +75,8 @@
     goal, rank = column[:, 0:1], column[:, 1:2]
     for first, pick in ((PART * half, own_p), (PART * (1 - half), recv_p)):
         k = rank - first
-        at = jnp.where((k >= 0) & (k < PART), goal * BOX + k, -1)
-        pick[...] = (iota((rows, slots), 1) == at).astype(BF16)
+        at = jnp.where((k >= 0) & (k < PART), k * members + goal, -1)
+        pick[...] = (iota(pick.shape, 1) == at).astype(BF16)
 
 
 def prepare(members, scal, route_a, route_b, scale_a, scale_b):
@@ -84,7 +84,7 @@
     slots = members * BOX
     placer = jax.ShapeDtypeStruct((slots, rows), BF16)
     info = jax.ShapeDtypeStruct((slots, LANES), BF16)
-    pick = jax.ShapeDtypeStruct((rows, slots), BF16)
+    pick = jax.ShapeDtypeStruct((rows, members * PART), BF16)
     return pl.pallas_call(
         lambda *refs: prepare_kernel(members, *refs),
         out_shape=(placer, info, placer, info, pick, pick),
@@ -369,26 +369,38 @@
     wide = og.shape[1]
     steps, groups, high, cols = stage.shape
     base = out.shape[2] - high
-    mine = pl.ds(pl.multiple_of(scal[0] * wide, wide), wide)
-    loads = [
+    first = [
         pltpu.make_async_copy(hid_a, hid_t.at[:, pl.ds(0, slots)], sem.at[0]),
         pltpu.make_async_copy(hid_b, hid_t.at[:, pl.ds(slots, slots)], sem.at[1]),
-        pltpu.make_async_copy(og_a, og.at[pl.ds(0, slots)], sem.at[2]),
-        pltpu.make_async_copy(og_b, og.at[pl.ds(slots, slots)], sem.at[3]),
-        pltpu.make_async_copy(dw_h.at[:, mine], w, sem.at[4]),
     ]
-    for load in loads:
+
+    def part(n):
+        return pl.ds(pl.multiple_of(n * cols, cols), cols)
+
+    def loads(n):
+        theirs = pl.ds(pl.multiple_of(scal[0] * wide + n * cols, cols), cols)
+        return (
+            pltpu.make_async_copy(og_a.at[:, part(n)], og.at[pl.ds(0, slots), part(n)], sem.at[2 + 3 * n]),
+            pltpu.make_async_copy(og_b.at[:, part(n)], og.at[pl.ds(slots, slots), part(n)], sem.at[3 + 3 * n]),
+            pltpu.make_async_copy(dw_h.at[:, theirs], w.at[:, part(n)], sem.at[4 + 3 * n]),
+        )
+
+    for load in first:
         load.start()
-    for load in loads:
+    for n in range(steps):
+        for load in loads(n):
+            load.start()
+    for load in first:
         load.wait()
 
     def save(n):
-        return pltpu.make_async_copy(stage.at[n], out.at[:, n, pl.ds(base, high), :], sem.at[5 + n])
+        return pltpu.make_async_copy(stage.at[n], out.at[:, n, pl.ds(base, high), :], sem.at[2 + 3 * steps + n])
 
     def one(n, _):
-        part = pl.ds(pl.multiple_of(n * cols, cols), cols)
-        grad = jnp.dot(hid_t[...], og[:, part], preferred_element_type=F32)
-        new = (w[:, part].astype(F32) - eta * grad).astype(BF16)
+        for load in loads(n):
+            load.wait()
+        grad = jnp.dot(hid_t[...], og[:, part(n)], preferred_element_type=F32)
+        new = (w[:, part(n)].astype(F32) - eta * grad).astype(BF16)
         stage[n] = new.reshape(groups, high, cols)
         save(n).start()
         return 0
@@ -411,7 +423,7 @@
         out_specs=anywhere(),
         scratch_shapes=[
             pltpu.VMEM((f, 2 * slots), BF16), pltpu.VMEM((2 * slots, wide), BF16), pltpu.VMEM((f, wide), BF16),
-            pltpu.VMEM((steps, 16, high, cols), BF16), pltpu.SemaphoreType.DMA((5 + steps,)),
+            pltpu.VMEM((steps, 16, high, cols), BF16), pltpu.SemaphoreType.DMA((2 + 4 * steps,)),
         ],
         input_output_aliases={6: 0},
         compiler_params=params(24),
@@ -440,12 +452,76 @@
     )(slot_map, pieces)
 
 
-def serve_kernel(scal, blocks_a, blocks_b, x_h, w_a, w_b, out, x, gu, dw, hid, sem):
+def fold(rows, chunk, c, boxed):
+    tiles = chunk.shape[0]
+    members = rows.shape[0] // BOX
+    for i in range(tiles):
+        chunk[i] = rows[:, i * LANES:(i + 1) * LANES]
+        for k in range(PART):
+            boxed[k * tiles + i, pl.ds(c, members, stride=BOX), :] = chunk[i, pl.ds(k, members, stride=BOX), :]
+
+
+def rounded(boxed, out):
+    for i in range(boxed.shape[0]):
+        out[:, i * LANES:(i + 1) * LANES] = boxed[i].astype(BF16)
+
+
+def back_kernel(bg_h, gu_h, out, bg, gu, chunk, boxed, done, sem):
+    steps, wide = gu.shape[:2]
+    load_bg = pltpu.make_async_copy(bg_h, bg, sem.at[0])
+
+    def load(c):
+        return pltpu.make_async_copy(gu_h.at[pl.ds(pl.multiple_of(c * wide, wide), wide)], gu.at[c], sem.at[1 + c])
+
+    load_bg.start()
+    for c in range(steps):
+        load(c).start()
+    load_bg.wait()
+
+    def one(c, _):
+        load(c).wait()
+        fold(lax.dot_general(bg[...], gu[c], NT, preferred_element_type=F32), chunk, c, boxed)
+        return 0
+
+    lax.fori_loop(0, steps, one, 0)
+    rounded(boxed, done)
+    save = pltpu.make_async_copy(done, out, sem.at[1 + steps])
+    save.start()
+    save.wait()
+
+
+def folded(members, d):
+    wide = d // BOX
+    return [
+        pltpu.VMEM((wide // LANES, members * BOX, LANES), F32),
+        pltpu.VMEM((PART * wide // LANES, members * BOX, LANES), F32),
+    ]
+
+
+def back(members, bg, gate_up):
+    slots, f2 = bg.shape
+    d = gate_up.shape[0]
+    wide = d // BOX
+    shape = (members * BOX, PART * wide)
+    return pl.pallas_call(
+        back_kernel,
+        out_shape=pltpu.HBM(shape, BF16),
+        in_specs=[anywhere()] * 2,
+        out_specs=anywhere(),
+        scratch_shapes=[pltpu.VMEM((slots, f2), BF16), pltpu.VMEM((BOX, wide, f2), BF16)] + folded(members, d) + [
+            pltpu.VMEM(shape, BF16), pltpu.SemaphoreType.DMA((2 + BOX,)),
+        ],
+        compiler_params=params(32),
+        name="back",
+    )(bg, gate_up)
+
+
+def serve_kernel(scal, blocks_a, blocks_b, x_h, w_a, w_b, out, x, gu, dw, hid, chunk, boxed, sem):
     half = scal[0]
     d = x.shape[1]
     high, f2 = gu.shape[3:]
     f = f2 // 2
-    fc, dc = 256, 512
+    fc = 256
     steps = f2 // fc
     deep = dw.shape[1]
     base = w_a.shape[2] - deep
@@ -491,70 +567,92 @@
         for s in range(2):
             load_dw(s, n).wait()
 
+    wide = d // BOX
+
     def outputs(c, _):
-        cols = pl.ds(pl.multiple_of(c * dc, dc), dc)
-        o = jnp.dot(hid[...], dw[:, :, cols].reshape(f, dc), preferred_element_type=F32)
-        out[:, cols] = jnp.where(kept, scale * o, 0.0).astype(BF16)
-        return 0
-
-    lax.fori_loop(0, d // dc, outputs, 0)
-
-
-def serve(scal, blocks_a, blocks_b, x, w_a, w_b):
+        cols = pl.ds(pl.multiple_of(c * wide, wide), wide)
+        o = jnp.dot(hid[...], dw[:, :, cols].reshape(f, wide), preferred_element_type=F32)
+        fold(jnp.where(kept, scale * o, 0.0), chunk, c, boxed)
+        return 0
+
+    lax.fori_loop(0, BOX, outputs, 0)
+    rounded(boxed, out)
+
+
+def serve(members, scal, blocks_a, blocks_b, x, w_a, w_b):
     slots, d = x.shape
     f = d * 3 // 8
     high = d // 2 // 64
     steps = 2 * f // 256
     return pl.pallas_call(
         serve_kernel,
-        out_shape=pltpu.HBM((slots, d), BF16),
+        out_shape=pltpu.HBM((members * BOX, PART * d // BOX), BF16),
         in_specs=[smem(), smem(), smem()] + [anywhere()] * 3,
         out_specs=vmem(),
         scratch_shapes=[
             pltpu.VMEM((slots, d), BF16), pltpu.VMEM((2, 16, 4, high, 2 * f), BF16), pltpu.VMEM((16, f // 16, d), BF16),
-            pltpu.VMEM((slots, f), BF16), pltpu.SemaphoreType.DMA((9 + 2 * steps,)),
+            pltpu.VMEM((slots, f), BF16), *folded(members, d), pltpu.SemaphoreType.DMA((9 + 2 * steps,)),
         ],
         compiler_params=params(40),
         name="serve",
     )(scal, blocks_a, blocks_b, x, w_a, w_b)
 
 
-def unpack_kernel(first, scal, pick, train, serve, given, out, box, done, sem):
+def unpack_kernel(first, scal, pick, train, serve, given, out, box, wide_box, rows, done, sem):
     half = scal[0]
-    steps = box.shape[0]
-    wide = box.shape[2]
-
-    def load(src, c):
-        return pltpu.make_async_copy(src.at[:, pl.ds(c * wide, wide)], box.at[c], sem.at[c])
+    parts = 4
+    high = box.shape[0] // parts
+    wide = box.shape[1] // PART
+    members = box.shape[0] // BOX
+    tiles = wide // LANES
+
+    def load(src, i):
+        part = pl.ds(i * high, high)
+        return pltpu.make_async_copy(src.at[part], box.at[part], sem.at[i])
 
     def save(c):
-        return pltpu.make_async_copy(done.at[c], out.at[:, pl.ds(c * wide, wide)], sem.at[steps + c])
+        cols = pl.ds(pl.multiple_of(c * wide, wide), wide)
+        return pltpu.make_async_copy(done.at[:, cols], out.at[:, cols], sem.at[parts + c])
 
     @pl.when(half == 0)
     def _():
-        for c in range(steps):
-            load(train, c).start()
+        for i in range(parts):
+            load(train, i).start()
 
     @pl.when(half == 1)
     def _():
-        for c in range(steps):
-            load(serve, c).start()
-
-    for c in range(steps):
-        load(train, c).wait()
-        rows = jnp.dot(pick[...], box[c], preferred_element_type=F32)
+        for i in range(parts):
+            load(serve, i).start()
+
+    for i in range(parts):
+        load(train, i).wait()
+        part = slice(i * high, (i + 1) * high)
+        for j in range(wide_box.shape[0]):
+            wide_box[j, part, :] = box[part, j * LANES:(j + 1) * LANES].astype(F32)
+
+    def one(c, _):
+        cols = pl.ds(pl.multiple_of(c * wide, wide), wide)
+        for k in range(PART):
+            for i in range(tiles):
+                rows[k * members:(k + 1) * members, i * LANES:(i + 1) * LANES] = wide_box[
+                    k * tiles + i, pl.ds(c, members, stride=BOX), :
+                ].astype(BF16)
+        total = jnp.dot(pick[...], rows[...], preferred_element_type=F32)
         if not first:
-            rows = rows + given[:, c * wide:(c + 1) * wide].astype(F32)
-        done[c] = rows.astype(BF16)
+            total = total + given[:, cols].astype(F32)
+        done[:, cols] = total.astype(BF16)
         save(c).start()
-    for c in range(steps):
+        return 0
+
+    lax.fori_loop(0, BOX, one, 0)
+    for c in range(BOX):
         save(c).wait()
 
 
 def unpack(scal, pick, train, serve, given=None):
     rows, slots = pick.shape
-    d = train.shape[1]
-    steps = 4
+    wide = train.shape[1] // PART
+    d = wide * BOX
     first = given is None
     return pl.pallas_call(
         lambda *refs: unpack_kernel(first, *refs),
@@ -562,8 +660,9 @@
         in_specs=[smem(), vmem(), anywhere(), anywhere(), smem() if first else vmem()],
         out_specs=anywhere(),
         scratch_shapes=[
-            pltpu.VMEM((steps, slots, d // steps), BF16), pltpu.VMEM((steps, rows, d // steps), BF16),
-            pltpu.SemaphoreType.DMA((2 * steps,)),
+            pltpu.VMEM(train.shape, BF16), pltpu.VMEM((train.shape[1] // LANES, train.shape[0], LANES), F32),
+            pltpu.VMEM((slots, wide), BF16),
+            pltpu.VMEM((rows, d), BF16), pltpu.SemaphoreType.DMA((4 + BOX,)),
         ],
         compiler_params=params(16),
         name="unpack" if first else "unpack_rest",
@@ -616,14 +715,14 @@
     tiled = (members,) + laid[2:]
     pieces = spread(new.reshape(tiled))
     both, _ = lax.optimization_barrier((both, new))
-    input_grad = lax.dot_general(both, gate_up, NT, preferred_element_type=F32).astype(BF16)
+    input_grad = back(members, both, gate_h)
     chosen = choose(slot_map, pieces)
     slots = spread(chosen)
     input_grad, _ = lax.optimization_barrier((input_grad, slots))
-    train_back = spread(input_grad.reshape(boxed)).reshape(flat)
+    train_back = spread(input_grad.reshape((members, BOX, -1))).reshape(input_grad.shape)
     slots_b = swap(slots)
-    served = serve(scal, blocks, blocks_b, serve_rows, slots.reshape(laid), slots_b.reshape(laid))
-    serve_back = spread(served.reshape(boxed)).reshape(flat)
+    served = serve(members, scal, blocks, blocks_b, serve_rows, slots.reshape(laid), slots_b.reshape(laid))
+    serve_back = spread(served.reshape((members, BOX, -1))).reshape(served.shape)
     train_other = swap(train_back)
     serve_other = swap(serve_back)
     rows = unpack(scal, own_p, train_back, serve_back)

time: 341 us -> 337 us (0.988)
  Pallas kernels: 62.2 us -> 77.2 us
  matrix products: 8.02 us -> 0 us
  waiting for transfers between devices: 96.2 us -> 88.2 us
    pallas_call x1 -> x2, Pallas kernels: 11.3 us -> 21.6 us  [the longest x1 13.2 us: serve(): pl.pallas_call(serve_kernel, out_shape=pltpu.HBM((members * BOX, PART * d...]
    dot_general x1 -> x0, matrix products: 8.02 us -> none  [step(): lax.dot_general(both, gate_up, NT, preferred_element_type=F32).astype(BF16)]
    all_to_all x4, waiting for transfers between devices: 86.1 us -> 78.7 us  [spread(): return lax.all_to_all(value, 'ep', split_axis=0, concat_axis=0, tiled=True)]
    pallas_call x2, Pallas kernels: 6.79 us -> 11.9 us  [unpack(): pl.pallas_call(lambda *refs: unpack_kernel(first, *refs), out_shape=jax.S...]
  transfers between devices with their start and end apart: 15 -> 15, of which waited for: 9 -> 8; matrix products, arithmetic and copies ran while one was open for 2% -> 0% of each run, Pallas kernels for 9% -> 13%
where the time goes in v5:
time: 337 us
  blocking collectives  124 us (37%)
  waiting for transfers between devices  88.2 us (26%)
  Pallas kernels  77.2 us (23%)
  starting transfers between devices  45.1 us (13%)
    all_to_all x2, blocking collectives, spread(): return lax.all_to_all(value, 'ep', split_axis=0, concat_axis=0, tiled=True)  124 us
    all_to_all x4, waiting for transfers between devices, spread(): return lax.all_to_all(value, 'ep', split_axis=0, concat_axis=0, tiled=True)  78.7 us
    all_to_all x4, starting transfers between devices, spread(): return lax.all_to_all(value, 'ep', split_axis=0, concat_axis=0, tiled=True)  28 us
    ppermute x11, starting transfers between devices, swap(): return lax.ppermute(value, 'half', SWAP)  17.2 us
    pallas_call x1, Pallas kernels, serve(): pl.pallas_call(serve_kernel, out_shape=pltpu.HBM((members * BOX, PART * d...  13.2 us
    pallas_call x1, Pallas kernels, train(): pl.pallas_call(train_kernel, out_shape=(jax.ShapeDtypeStruct((f, slots),...  12.8 us
    pallas_call x2, Pallas kernels, unpack(): pl.pallas_call(lambda *refs: unpack_kernel(first, *refs), out_shape=jax.S...  11.9 us
    ppermute x11, waiting for transfers between devices, swap(): return lax.ppermute(value, 'half', SWAP)  9.52 us
  transfers between devices with their start and end apart: 15, of which 8 were waited for; matrix products, arithmetic and copies ran while one was open for 0% of the time, Pallas kernels for 13%

profile of v5, /device:TPU:1, one launch (start us, length us, event | category | flops | bytes accessed | tf_op | source)
XLA Modules:
  0.0 336.6 jit_solution(355369908428129662)
XLA Ops:
  0.0 1.4 collective-permute-start.3
  2.0 3.0 collective-permute-done.1.refs_4_
  5.0 2.2 prepare.1
  7.2 3.4 shard_map.73
  10.6 11.3 %all-to-all-start = ((bf16[64,8,2048]{2,1,0:T(8,128)(2,1)}), bf16[64,8,2048]{2,1,0:T(8,128)(2,1)S(1)}, u32[]{:S(2)}, u32[]{:S(2)}) async-start(bf16[64,8,2048]{2,1,0:T(8,128)(2,1)} %bitcast.30), calls=%async_computation | async-start | bytes 4194304 | tf_op jit(solution)/shard_map/all_to_all | solution.py:677
  21.9 1.7 collective-permute-start.2
  24.4 25.0 %all-to-all-done = bf16[64,8,2048]{2,1,0:T(8,128)(2,1)S(1)} async-done(((bf16[64,8,2048]{2,1,0:T(8,128)(2,1)}), bf16[64,8,2048]{2,1,0:T(8,128)(2,1)S(1)}, u32[]{:S(2)}, u32[]{:S(2)}) %all-to-all-start) | async-done | bytes 2097184 | tf_op jit(solution)/shard_map/all_to_all | solution.py:677
  49.4 12.8 %train.1 = (bf16[768,512]{1,0:T(8,128)(2,1)S(1)}, bf16[512,1024]{1,0:T(8,128)(2,1)S(1)}, bf16[512,1024]{1,0:T(8,128)(2,1)S(1)}, bf16[512,1536]{1,0:T(8,128)(2,1)}) custom-call(s32[2]{0:T(128)S(1)} %pad_add_fusion.refs_0_.scal.refs_4_, s32[1,64]{1,0:T(1,128)S(1)} %copy-done.6, s32[1,64]{1,0:T(1,128)S(1)} %collective-permute-done.2.blocks_b, ...), custom_call_target="tpu_custom_call" | custom-call | tf_op jit(solution)/shard_map/train/pallas_call | solution.py:256
  62.2 3.2 collective-permute-start.4
  65.5 3.2 collective-permute-done.4.refs_3_
  69.1 2.5 collective-permute-done.7.x_b
  71.6 1.9 turn.1.refs_1_
  73.6 7.1 %update_gate.1.refs_6_ = bf16[16,4,144,256]{3,2,1,0:T(8,128)(2,1)} custom-call(s32[2]{0:T(128)S(1)} %pad_add_fusion.refs_0_.scal.refs_4_, bf16[1024,1024]{1,0:T(8,128)(2,1)S(1)} %turn.1.refs_1_, bf16[512,1536]{1,0:T(8,128)(2,1)S(1)} %copy-done.2, bf16[512,1536]{1,0:T(8,128)(2,1)S(1)} %collective-permute-done.4.refs_3_, bf16[2048,1536]{1,0:T(8,128)(2,1)} %bitcast.25), custom_call_target="tpu_custom_call" | custom-call | tf_op jit(solution)/shard_map/update_gate/pallas_call | solution.py:353
  80.7 5.2 %update_down.1 = bf16[16,4,144,256]{3,2,1,0:T(8,128)(2,1)} custom-call(s32[2]{0:T(128)S(1)} %pad_add_fusion.refs_0_.scal.refs_4_, bf16[768,512]{1,0:T(8,128)(2,1)S(1)} %get-tuple-element.25.refs_1_, bf16[768,512]{1,0:T(8,128)(2,1)S(1)} %collective-permute-done.5.refs_2_, ...), custom_call_target="tpu_custom_call", output_to_operand_aliasing={{}: (6, {})} | custom-call | tf_op jit(solution)/shard_map/update_down/pallas_call | solution.py:419
  85.9 62.7 %all_to_all.30.src = bf16[64,144,256]{2,1,0:T(8,128)(2,1)S(1)} all-to-all(bf16[64,144,256]{2,1,0:T(8,128)(2,1)} %bitcast.27), channel_id=1, replica_groups=mesh['half'=2,'ep'=64] {'ep'}, dimensions={0} | all-to-all | bytes 9437184 | tf_op jit(solution)/shard_map/all_to_all | solution.py:677
  148.7 6.9 %choose.1 = bf16[64,144,256]{2,1,0:T(8,128)(2,1)S(1)} custom-call(s32[64]{0:T(128)S(1)} %copy-done.7, bf16[64,144,256]{2,1,0:T(8,128)(2,1)S(1)} %all_to_all.30.src), custom_call_target="tpu_custom_call" | custom-call | tf_op jit(solution)/shard_map/choose/pallas_call | solution.py:444
  155.7 61.4 %all_to_all.31 = bf16[64,144,256]{2,1,0:T(8,128)(2,1)} all-to-all(bf16[64,144,256]{2,1,0:T(8,128)(2,1)S(1)} %choose.1), channel_id=1, replica_groups=mesh['half'=2,'ep'=64] {'ep'}, dimensions={0} | all-to-all | bytes 9437184 | tf_op jit(solution)/shard_map/all_to_all | solution.py:677
  217.1 3.3 collective-permute-start.9
  220.4 4.2 %shard_map.74 = bf16[512,2048]{1,0:T(8,128)(2,1)} custom-call(s32[2]{0:T(128)S(1)} %pad_add_fusion.refs_0_.scal.refs_4_, bf16[448,2048]{1,0:T(8,128)(2,1)} %bitcast.35, bf16[448,2048]{1,0:T(8,128)(2,1)S(1)} %copy-done.1, bf16[512,448]{1,0:T(8,128)(2,1)S(1)} %get-tuple-element.30.refs_3_, bf16[512,128]{1,0:T(8,128)(2,1)S(1)} %copy-done.5), custom_call_target="tpu_custom_call" | custom-call | tf_op jit(solution)/shard_map/pallas_call | solution.py:136
  224.6 4.9 %all-to-all-start.4 = ((bf16[64,8,2048]{2,1,0:T(8,128)(2,1)}), bf16[64,8,2048]{2,1,0:T(8,128)(2,1)S(1)}, u32[]{:S(2)}, u32[]{:S(2)}) async-start(bf16[64,8,2048]{2,1,0:T(8,128)(2,1)} %bitcast.31), calls=%async_computation.4 | async-start | bytes 4194304 | tf_op jit(solution)/shard_map/all_to_all | solution.py:677
  229.5 1.4 copy-done.3
  230.9 8.4 %back.1 = bf16[512,1792]{1,0:T(8,128)(2,1)} custom-call(bf16[512,1536]{1,0:T(8,128)(2,1)S(1)} %copy-done.3, bf16[2048,1536]{1,0:T(8,128)(2,1)} %bitcast.26), custom_call_target="tpu_custom_call" | custom-call | tf_op jit(solution)/shard_map/back/pallas_call | solution.py:506
  239.3 20.5 %all-to-all-done.4 = bf16[64,8,2048]{2,1,0:T(8,128)(2,1)S(1)} async-done(((bf16[64,8,2048]{2,1,0:T(8,128)(2,1)}), bf16[64,8,2048]{2,1,0:T(8,128)(2,1)S(1)}, u32[]{:S(2)}, u32[]{:S(2)}) %all-to-all-start.4) | async-done | bytes 2097184 | tf_op jit(solution)/shard_map/all_to_all | solution.py:677
  259.8 6.3 %all-to-all-start.3 = ((bf16[64,8,1792]{2,1,0:T(8,128)(2,1)}), bf16[64,8,1792]{2,1,0:T(8,128)(2,1)}, u32[]{:S(2)}, u32[]{:S(2)}) async-start(bf16[64,8,1792]{2,1,0:T(8,128)(2,1)} %bitcast.32), calls=%async_computation.3 | async-start | bytes 3670016 | tf_op jit(solution)/shard_map/all_to_all | solution.py:677
  266.1 13.2 %serve.1 = bf16[512,1792]{1,0:T(8,128)(2,1)} custom-call(s32[2]{0:T(128)S(1)} %pad_add_fusion.refs_0_.scal.refs_4_, s32[1,64]{1,0:T(1,128)S(1)} %copy-done.6, s32[1,64]{1,0:T(1,128)S(1)} %collective-permute-done.2.blocks_b, bf16[512,2048]{1,0:T(8,128)(2,1)S(1)} %bitcast.21, bf16[16,4,144,256]{3,2,1,0:T(8,128)(2,1)} %bitcast.13.w_a, ...), custom_call_target="tpu_custom_call" | custom-call | tf_op jit(solution)/shard_map/serve/pallas_call | solution.py:587
  279.4 11.9 %all-to-all-done.3 = bf16[64,8,1792]{2,1,0:T(8,128)(2,1)} async-done(((bf16[64,8,1792]{2,1,0:T(8,128)(2,1)}), bf16[64,8,1792]{2,1,0:T(8,128)(2,1)}, u32[]{:S(2)}, u32[]{:S(2)}) %all-to-all-start.3) | async-done | bytes 1835040 | tf_op jit(solution)/shard_map/all_to_all | solution.py:677
  291.2 5.5 %all-to-all-start.5 = ((bf16[64,8,1792]{2,1,0:T(8,128)(2,1)}), bf16[64,8,1792]{2,1,0:T(8,128)(2,1)S(1)}, u32[]{:S(2)}, u32[]{:S(2)}) async-start(bf16[64,8,1792]{2,1,0:T(8,128)(2,1)} %bitcast.36), calls=%async_computation.5 | async-start | bytes 3670016 | tf_op jit(solution)/shard_map/all_to_all | solution.py:677
  296.7 3.0 collective-permute-start.8
  299.7 21.4 %all-to-all-done.5 = bf16[64,8,1792]{2,1,0:T(8,128)(2,1)S(1)} async-done(((bf16[64,8,1792]{2,1,0:T(8,128)(2,1)}), bf16[64,8,1792]{2,1,0:T(8,128)(2,1)S(1)}, u32[]{:S(2)}, u32[]{:S(2)}) %all-to-all-start.5) | async-done | bytes 1835040 | tf_op jit(solution)/shard_map/all_to_all | solution.py:677
  321.1 3.5 %collective-permute-start.10 = (bf16[512,1792]{1,0:T(8,128)(2,1)S(1)}, bf16[512,1792]{1,0:T(8,128)(2,1)S(1)}, u32[]{:S(2)}, u32[]{:S(2)}) collective-permute-start(bf16[512,1792]{1,0:T(8,128)(2,1)S(1)} %bitcast.22), channel_id=1, source_target_pairs={{0,64},{64,0},{1,65},{65,1},{2,66},{66,2},{3,67},{67,3},{4,68},{68... | collective-permute-start | bytes 5505032 | tf_op jit(solution)/shard_map/ppermute | solution.py:673
  324.6 5.8 %unpack.1.refs_4_ = bf16[448,2048]{1,0:T(8,128)(2,1)S(1)} custom-call(s32[2]{0:T(128)S(1)} %pad_add_fusion.refs_0_.scal.refs_4_, bf16[448,448]{1,0:T(8,128)(2,1)S(1)} %get-tuple-element.32.refs_1_, bf16[512,1792]{1,0:T(8,128)(2,1)} %bitcast.10.refs_2_, bf16[512,1792]{1,0:T(8,128)(2,1)S(1)} %bitcast.23, s32[2]{0:T(128)S(1)} %pad_add_fusion.refs_0_.scal.refs_4_), custom_call_target="tpu_custom_call" | custom-call | tf_op jit(solution)/shard_map/unpack/pallas_call | solution.py:657
  330.4 6.1 %unpack_rest.1 = bf16[448,2048]{1,0:T(8,128)(2,1)} custom-call(s32[2]{0:T(128)S(1)} %pad_add_fusion.refs_0_.scal.refs_4_, bf16[448,448]{1,0:T(8,128)(2,1)S(1)} %get-tuple-element.19.refs_1_, bf16[512,1792]{1,0:T(8,128)(2,1)} %collective-permute-done.8.refs_2_, bf16[512,1792]{1,0:T(8,128)(2,1)S(1)} %collective-permute-done.10.refs_3_, ...), custom_call_target="tpu_custom_call" | custom-call | tf_op jit(solution)/shard_map/unpack_rest/pallas_call | solution.py:657
  (29 shorter events, 2.1 us)
Async XLA Ops:
  0.0 7.2 %collective-permute-start.3 = (bf16[448,2048]{1,0:T(8,128)(2,1)}, bf16[448,2048]{1,0:T(8,128)(2,1)S(1)}, u32[]{:S(2)}, u32[]{:S(2)}) collective-permute-start(bf16[448,2048]{1,0:T(8,128)(2,1)} %bitcast.33), channel_id=1, source_target_pairs={{0,64},{64,0},{1,65},{65,1},{2,66},{66,2},{3,67},{67,3},{4,68},{68... | collective-permute-start | bytes 5505032 | tf_op jit(solution)/shard_map/ppermute | solution.py:673
  1.4 3.6 %collective-permute-start = (s32[1,448]{1,0:T(1,128)}, s32[1,448]{1,0:T(1,128)S(1)}, u32[]{:S(2)}, u32[]{:S(2)}) collective-permute-start(s32[1,448]{1,0:T(1,128)} %bitcast.37), channel_id=1, source_target_pairs={{0,64},{64,0},{1,65},{65,1},{2,66},{66,2},{3,67},{67,3},{4,68},{68... | collective-permute-start | bytes 5384 | tf_op jit(solution)/shard_map/ppermute | solution.py:673
  1.4 3.6 %collective-permute-start.1 = (bf16[1,448]{1,0:T(2,128)(2,1)}, bf16[1,448]{1,0:T(2,128)(2,1)S(1)}, u32[]{:S(2)}, u32[]{:S(2)}) collective-permute-start(bf16[1,448]{1,0:T(2,128)(2,1)} %refs_3_.1), channel_id=1, source_target_pairs={{0,64},{64,0},{1,65},{65,1},{2,66},{66,2},{3,67},{67,3},{4,68},{68... | collective-permute-start | bytes 2696 | tf_op jit(solution)/shard_map/ppermute | solution.py:673
  7.2 3.4 %copy-start.4 = (bf16[512,128]{1,0:T(8,128)(2,1)}, bf16[512,128]{1,0:T(8,128)(2,1)S(1)}, u32[]{:S(2)}) copy-start(bf16[512,128]{1,0:T(8,128)(2,1)S(1)} %get-tuple-element.31.refs_4_) | copy-start | bytes 393220
  7.2 3.4 %copy-start = (bf16[448,2048]{1,0:T(8,128)(2,1)}, bf16[448,2048]{1,0:T(8,128)(2,1)S(1)}, u32[]{:S(2)}) copy-start(bf16[448,2048]{1,0:T(8,128)(2,1)S(1)} %collective-permute-done.3.refs_2_) | copy-start | bytes 5505028
  10.6 11.3 %copy-start.6 = (s32[1,64]{1,0:T(1,128)S(1)}, s32[1,64]{1,0:T(1,128)}, u32[]{:S(2)}) copy-start(s32[1,64]{1,0:T(1,128)} %blocks_a.3) | copy-start | bytes 772
  10.6 38.8 %all-to-all-start = ((bf16[64,8,2048]{2,1,0:T(8,128)(2,1)}), bf16[64,8,2048]{2,1,0:T(8,128)(2,1)S(1)}, u32[]{:S(2)}, u32[]{:S(2)}) async-start(bf16[64,8,2048]{2,1,0:T(8,128)(2,1)} %bitcast.30), calls=%async_computation | async-start | bytes 4194304 | tf_op jit(solution)/shard_map/all_to_all | solution.py:677
  21.9 2.5 collective-permute-start.2
  62.2 6.5 %collective-permute-start.4 = (bf16[512,1536]{1,0:T(8,128)(2,1)}, bf16[512,1536]{1,0:T(8,128)(2,1)S(1)}, u32[]{:S(2)}, u32[]{:S(2)}) collective-permute-start(bf16[512,1536]{1,0:T(8,128)(2,1)} %get-tuple-element.28.refs_2_.bg_h), channel_id=1, source_target_pairs={{0,64},{64,0},{1,65},{65,1},{2,66},{66,2},{3,67},{67,3},{4,68},{68... | collective-permute-start | bytes 4718600 | tf_op jit(solution)/shard_map/ppermute | solution.py:673
  65.4 6.2 %collective-permute-start.7 = (bf16[512,2048]{1,0:T(8,128)(2,1)S(1)}, bf16[512,2048]{1,0:T(8,128)(2,1)S(1)}, u32[]{:S(2)}, u32[]{:S(2)}) collective-permute-start(bf16[512,2048]{1,0:T(8,128)(2,1)S(1)} %bitcast.19), channel_id=1, source_target_pairs={{0,64},{64,0},{1,65},{65,1},{2,66},{66,2},{3,67},{67,3},{4,68},{68... | collective-permute-start | bytes 6291464 | tf_op jit(solution)/shard_map/ppermute | solution.py:673
  68.6 4.9 %copy-start.2 = (bf16[512,1536]{1,0:T(8,128)(2,1)S(1)}, bf16[512,1536]{1,0:T(8,128)(2,1)}, u32[]{:S(2)}) copy-start(bf16[512,1536]{1,0:T(8,128)(2,1)} %get-tuple-element.28.refs_2_.bg_h) | copy-start | bytes 4718596
  68.6 12.1 %collective-permute-start.6 = (bf16[512,1024]{1,0:T(8,128)(2,1)S(1)}, bf16[512,1024]{1,0:T(8,128)(2,1)S(1)}, u32[]{:S(2)}, u32[]{:S(2)}) collective-permute-start(bf16[512,1024]{1,0:T(8,128)(2,1)S(1)} %get-tuple-element.27), channel_id=1, source_target_pairs={{0,64},{64,0},{1,65},{65,1},{2,66},{66,2},{3,67},{67,3},{4,68},{68... | collective-permute-start | bytes 3145736 | tf_op jit(solution)/shard_map/ppermute | solution.py:673
  69.0 11.7 %collective-permute-start.5 = (bf16[768,512]{1,0:T(8,128)(2,1)S(1)}, bf16[768,512]{1,0:T(8,128)(2,1)S(1)}, u32[]{:S(2)}, u32[]{:S(2)}) collective-permute-start(bf16[768,512]{1,0:T(8,128)(2,1)S(1)} %get-tuple-element.25.refs_1_), channel_id=1, source_target_pairs={{0,64},{64,0},{1,65},{65,1},{2,66},{66,2},{3,67},{67,3},{4,68},{68... | collective-permute-start | bytes 2359304 | tf_op jit(solution)/shard_map/ppermute | solution.py:673
  85.9 62.7 %copy-start.7 = (s32[64]{0:T(128)S(1)}, s32[64]{0:T(128)}, u32[]{:S(2)}) copy-start(s32[64]{0:T(128)} %slot_map.1) | copy-start | bytes 772
  155.6 64.8 %copy-start.1 = (bf16[448,2048]{1,0:T(8,128)(2,1)S(1)}, bf16[448,2048]{1,0:T(8,128)(2,1)}, u32[]{:S(2)}) copy-start(bf16[448,2048]{1,0:T(8,128)(2,1)} %copy-done) | copy-start | bytes 5505028
  155.6 64.8 %copy-start.5 = (bf16[512,128]{1,0:T(8,128)(2,1)S(1)}, bf16[512,128]{1,0:T(8,128)(2,1)}, u32[]{:S(2)}) copy-start(bf16[512,128]{1,0:T(8,128)(2,1)} %copy-done.4) | copy-start | bytes 393220
  217.1 49.0 %collective-permute-start.9 = (bf16[64,144,256]{2,1,0:T(8,128)(2,1)}, bf16[64,144,256]{2,1,0:T(8,128)(2,1)}, u32[]{:S(2)}, u32[]{:S(2)}) collective-permute-start(bf16[64,144,256]{2,1,0:T(8,128)(2,1)} %all_to_all.31), channel_id=1, source_target_pairs={{0,64},{64,0},{1,65},{65,1},{2,66},{66,2},{3,67},{67,3},{4,68},{68... | collective-permute-start | bytes 14155784 | tf_op jit(solution)/shard_map/ppermute | solution.py:673
  224.6 35.1 %all-to-all-start.4 = ((bf16[64,8,2048]{2,1,0:T(8,128)(2,1)}), bf16[64,8,2048]{2,1,0:T(8,128)(2,1)S(1)}, u32[]{:S(2)}, u32[]{:S(2)}) async-start(bf16[64,8,2048]{2,1,0:T(8,128)(2,1)} %bitcast.31), calls=%async_computation.4 | async-start | bytes 4194304 | tf_op jit(solution)/shard_map/all_to_all | solution.py:677
  229.5 1.4 copy-start.3
  259.8 31.5 %all-to-all-start.3 = ((bf16[64,8,1792]{2,1,0:T(8,128)(2,1)}), bf16[64,8,1792]{2,1,0:T(8,128)(2,1)}, u32[]{:S(2)}, u32[]{:S(2)}) async-start(bf16[64,8,1792]{2,1,0:T(8,128)(2,1)} %bitcast.32), calls=%async_computation.3 | async-start | bytes 3670016 | tf_op jit(solution)/shard_map/all_to_all | solution.py:677
  291.2 29.9 %all-to-all-start.5 = ((bf16[64,8,1792]{2,1,0:T(8,128)(2,1)}), bf16[64,8,1792]{2,1,0:T(8,128)(2,1)S(1)}, u32[]{:S(2)}, u32[]{:S(2)}) async-start(bf16[64,8,1792]{2,1,0:T(8,128)(2,1)} %bitcast.36), calls=%async_computation.5 | async-start | bytes 3670016 | tf_op jit(solution)/shard_map/all_to_all | solution.py:677
  296.7 33.7 %collective-permute-start.8 = (bf16[512,1792]{1,0:T(8,128)(2,1)}, bf16[512,1792]{1,0:T(8,128)(2,1)}, u32[]{:S(2)}, u32[]{:S(2)}) collective-permute-start(bf16[512,1792]{1,0:T(8,128)(2,1)} %bitcast.10.refs_2_), channel_id=1, source_target_pairs={{0,64},{64,0},{1,65},{65,1},{2,66},{66,2},{3,67},{67,3},{4,68},{68... | collective-permute-start | bytes 5505032 | tf_op jit(solution)/shard_map/ppermute | solution.py:673
  321.1 9.3 %collective-permute-start.10 = (bf16[512,1792]{1,0:T(8,128)(2,1)S(1)}, bf16[512,1792]{1,0:T(8,128)(2,1)S(1)}, u32[]{:S(2)}, u32[]{:S(2)}) collective-permute-start(bf16[512,1792]{1,0:T(8,128)(2,1)S(1)} %bitcast.22), channel_id=1, source_target_pairs={{0,64},{64,0},{1,65},{65,1},{2,66},{66,2},{3,67},{67,3},{4,68},{68... | collective-permute-start | bytes 5505032 | tf_op jit(solution)/shard_map/ppermute | solution.py:673

commit v6 on v5

--- a/solution.py
+++ b/solution.py
@@ -132,7 +132,7 @@
 def pack(group, scal, tok_a, tok_b, placer, info):
     slots, rows = placer.shape
     width = tok_a.shape[1]
-    steps = 4
+    steps = 2
     return pl.pallas_call(
         lambda *refs: pack_kernel(group, *refs),
         out_shape=pltpu.HBM((slots, width), BF16),
@@ -436,7 +436,7 @@
         pltpu.make_async_copy(src.at[slot_map[i]], out.at[i], sem).start()
         return 0
 
-    lax.fori_loop(0, out.shape[0], start, 0, unroll=8)
+    lax.fori_loop(0, out.shape[0], start, 0, unroll=True)
     pltpu.make_async_copy(src, out, sem).wait()
 
 
@@ -605,13 +605,14 @@
     wide = box.shape[1] // PART
     members = box.shape[0] // BOX
     tiles = wide // LANES
+    pair = rows.shape[1] // wide
 
     def load(src, i):
         part = pl.ds(i * high, high)
         return pltpu.make_async_copy(src.at[part], box.at[part], sem.at[i])
 
     def save(c):
-        cols = pl.ds(pl.multiple_of(c * wide, wide), wide)
+        cols = pl.ds(pl.multiple_of(c * pair * wide, wide), pair * wide)
         return pltpu.make_async_copy(done.at[:, cols], out.at[:, cols], sem.at[parts + c])
 
     @pl.when(half == 0)
@@ -631,12 +632,14 @@
             wide_box[j, part, :] = box[part, j * LANES:(j + 1) * LANES].astype(F32)
 
     def one(c, _):
-        cols = pl.ds(pl.multiple_of(c * wide, wide), wide)
+        cols = pl.ds(pl.multiple_of(c * pair * wide, wide), pair * wide)
         for k in range(PART):
             for i in range(tiles):
-                rows[k * members:(k + 1) * members, i * LANES:(i + 1) * LANES] = wide_box[
-                    k * tiles + i, pl.ds(c, members, stride=BOX), :
-                ].astype(BF16)
+                for b in range(pair):
+                    lanes = slice((b * tiles + i) * LANES, (b * tiles + i + 1) * LANES)
+                    rows[k * members:(k + 1) * members, lanes] = wide_box[
+                        k * tiles + i, pl.ds(c * pair + b, members, stride=BOX), :
+                    ].astype(BF16)
         total = jnp.dot(pick[...], rows[...], preferred_element_type=F32)
         if not first:
             total = total + given[:, cols].astype(F32)
@@ -644,8 +647,8 @@
         save(c).start()
         return 0
 
-    lax.fori_loop(0, BOX, one, 0)
-    for c in range(BOX):
+    lax.fori_loop(0, BOX // pair, one, 0, unroll=2)
+    for c in range(BOX // pair):
         save(c).wait()
 
 
@@ -661,7 +664,7 @@
         out_specs=anywhere(),
         scratch_shapes=[
             pltpu.VMEM(train.shape, BF16), pltpu.VMEM((train.shape[1] // LANES, train.shape[0], LANES), F32),
-            pltpu.VMEM((slots, wide), BF16),
+            pltpu.VMEM((slots, 4 * wide), BF16),
             pltpu.VMEM((rows, d), BF16), pltpu.SemaphoreType.DMA((4 + BOX,)),
         ],
         compiler_params=params(16),

time: 337 us -> 334 us (level)
  Pallas kernels: 77.2 us -> 73.4 us
    pallas_call x2, Pallas kernels: 11.9 us -> 8.39 us  [unpack(): pl.pallas_call(lambda *refs: unpack_kernel(first, *refs), out_shape=jax.S...]
  transfers between devices with their start and end apart: 15 -> 15, of which waited for: 8 -> 8; matrix products, arithmetic and copies ran while one was open for 0% -> 0% of each run, Pallas kernels for 13% -> 12%
where the time goes in v6:
time: 334 us; the launch traced here: 333 us
  blocking collectives  124 us (37%)
  waiting for transfers between devices  87.7 us (26%)
  Pallas kernels  73.4 us (22%)
  starting transfers between devices  45.3 us (14%)
    all_to_all x2, blocking collectives, spread(): return lax.all_to_all(value, 'ep', split_axis=0, concat_axis=0, tiled=True)  124 us
    all_to_all x4, waiting for transfers between devices, spread(): return lax.all_to_all(value, 'ep', split_axis=0, concat_axis=0, tiled=True)  78.2 us
    all_to_all x4, starting transfers between devices, spread(): return lax.all_to_all(value, 'ep', split_axis=0, concat_axis=0, tiled=True)  28.2 us
    ppermute x11, starting transfers between devices, swap(): return lax.ppermute(value, 'half', SWAP)  17.1 us
    pallas_call x1, Pallas kernels, serve(): pl.pallas_call(serve_kernel, out_shape=pltpu.HBM((members * BOX, PART * d...  13.2 us
    pallas_call x1, Pallas kernels, train(): pl.pallas_call(train_kernel, out_shape=(jax.ShapeDtypeStruct((f, slots),...  12.8 us
    ppermute x11, waiting for transfers between devices, swap(): return lax.ppermute(value, 'half', SWAP)  9.52 us
    pallas_call x1, Pallas kernels, back(): pl.pallas_call(back_kernel, out_shape=pltpu.HBM(shape, BF16), in_specs=[a...  8.41 us
  transfers between devices with their start and end apart: 15, of which 8 were waited for; matrix products, arithmetic and copies ran while one was open for 0% of the time, Pallas kernels for 12%

profile of v6, /device:TPU:1, one launch (start us, length us, event | category | flops | bytes accessed | tf_op | source)
XLA Modules:
  0.0 332.7 jit_solution(13556002455379151209)
XLA Ops:
  0.0 1.4 collective-permute-start.3
  2.0 3.0 collective-permute-done.1.refs_4_
  5.0 2.2 prepare.1
  7.2 3.1 shard_map.73
  10.4 11.3 %all-to-all-start = ((bf16[64,8,2048]{2,1,0:T(8,128)(2,1)}), bf16[64,8,2048]{2,1,0:T(8,128)(2,1)S(1)}, u32[]{:S(2)}, u32[]{:S(2)}) async-start(bf16[64,8,2048]{2,1,0:T(8,128)(2,1)} %bitcast.30), calls=%async_computation | async-start | bytes 4194304 | tf_op jit(solution)/shard_map/all_to_all | solution.py:680
  21.7 1.9 collective-permute-start.2
  24.4 24.7 %all-to-all-done = bf16[64,8,2048]{2,1,0:T(8,128)(2,1)S(1)} async-done(((bf16[64,8,2048]{2,1,0:T(8,128)(2,1)}), bf16[64,8,2048]{2,1,0:T(8,128)(2,1)S(1)}, u32[]{:S(2)}, u32[]{:S(2)}) %all-to-all-start) | async-done | bytes 2097184 | tf_op jit(solution)/shard_map/all_to_all | solution.py:680
  49.1 12.8 %train.1 = (bf16[768,512]{1,0:T(8,128)(2,1)S(1)}, bf16[512,1024]{1,0:T(8,128)(2,1)S(1)}, bf16[512,1024]{1,0:T(8,128)(2,1)S(1)}, bf16[512,1536]{1,0:T(8,128)(2,1)}) custom-call(s32[2]{0:T(128)S(1)} %pad_add_fusion.refs_0_.scal.refs_4_, s32[1,64]{1,0:T(1,128)S(1)} %copy-done.6, s32[1,64]{1,0:T(1,128)S(1)} %collective-permute-done.2.blocks_b, ...), custom_call_target="tpu_custom_call" | custom-call | tf_op jit(solution)/shard_map/train/pallas_call | solution.py:256
  61.9 3.3 collective-permute-start.4
  65.3 3.2 collective-permute-done.4.refs_3_
  68.9 2.5 collective-permute-done.7.x_b
  71.4 1.9 turn.1.refs_1_
  73.3 7.1 %update_gate.1.refs_6_ = bf16[16,4,144,256]{3,2,1,0:T(8,128)(2,1)} custom-call(s32[2]{0:T(128)S(1)} %pad_add_fusion.refs_0_.scal.refs_4_, bf16[1024,1024]{1,0:T(8,128)(2,1)S(1)} %turn.1.refs_1_, bf16[512,1536]{1,0:T(8,128)(2,1)S(1)} %copy-done.2, bf16[512,1536]{1,0:T(8,128)(2,1)S(1)} %collective-permute-done.4.refs_3_, bf16[2048,1536]{1,0:T(8,128)(2,1)} %bitcast.25), custom_call_target="tpu_custom_call" | custom-call | tf_op jit(solution)/shard_map/update_gate/pallas_call | solution.py:353
  80.5 5.2 %update_down.1 = bf16[16,4,144,256]{3,2,1,0:T(8,128)(2,1)} custom-call(s32[2]{0:T(128)S(1)} %pad_add_fusion.refs_0_.scal.refs_4_, bf16[768,512]{1,0:T(8,128)(2,1)S(1)} %get-tuple-element.25.refs_1_, bf16[768,512]{1,0:T(8,128)(2,1)S(1)} %collective-permute-done.5.refs_2_, ...), custom_call_target="tpu_custom_call", output_to_operand_aliasing={{}: (6, {})} | custom-call | tf_op jit(solution)/shard_map/update_down/pallas_call | solution.py:419
  85.7 62.6 %all_to_all.30.src = bf16[64,144,256]{2,1,0:T(8,128)(2,1)S(1)} all-to-all(bf16[64,144,256]{2,1,0:T(8,128)(2,1)} %bitcast.27), channel_id=1, replica_groups=mesh['half'=2,'ep'=64] {'ep'}, dimensions={0} | all-to-all | bytes 9437184 | tf_op jit(solution)/shard_map/all_to_all | solution.py:680
  148.4 6.9 %choose.1 = bf16[64,144,256]{2,1,0:T(8,128)(2,1)S(1)} custom-call(s32[64]{0:T(128)S(1)} %copy-done.7, bf16[64,144,256]{2,1,0:T(8,128)(2,1)S(1)} %all_to_all.30.src), custom_call_target="tpu_custom_call" | custom-call | tf_op jit(solution)/shard_map/choose/pallas_call | solution.py:444
  155.3 61.6 %all_to_all.31 = bf16[64,144,256]{2,1,0:T(8,128)(2,1)} all-to-all(bf16[64,144,256]{2,1,0:T(8,128)(2,1)S(1)} %choose.1), channel_id=1, replica_groups=mesh['half'=2,'ep'=64] {'ep'}, dimensions={0} | all-to-all | bytes 9437184 | tf_op jit(solution)/shard_map/all_to_all | solution.py:680
  216.9 3.3 collective-permute-start.9
  220.2 4.2 %shard_map.74 = bf16[512,2048]{1,0:T(8,128)(2,1)} custom-call(s32[2]{0:T(128)S(1)} %pad_add_fusion.refs_0_.scal.refs_4_, bf16[448,2048]{1,0:T(8,128)(2,1)} %bitcast.35, bf16[448,2048]{1,0:T(8,128)(2,1)S(1)} %copy-done.1, bf16[512,448]{1,0:T(8,128)(2,1)S(1)} %get-tuple-element.30.refs_3_, bf16[512,128]{1,0:T(8,128)(2,1)S(1)} %copy-done.5), custom_call_target="tpu_custom_call" | custom-call | tf_op jit(solution)/shard_map/pallas_call | solution.py:136
  224.4 4.9 %all-to-all-start.4 = ((bf16[64,8,2048]{2,1,0:T(8,128)(2,1)}), bf16[64,8,2048]{2,1,0:T(8,128)(2,1)S(1)}, u32[]{:S(2)}, u32[]{:S(2)}) async-start(bf16[64,8,2048]{2,1,0:T(8,128)(2,1)} %bitcast.31), calls=%async_computation.4 | async-start | bytes 4194304 | tf_op jit(solution)/shard_map/all_to_all | solution.py:680
  229.3 1.4 copy-done.3
  230.7 8.4 %back.1 = bf16[512,1792]{1,0:T(8,128)(2,1)} custom-call(bf16[512,1536]{1,0:T(8,128)(2,1)S(1)} %copy-done.3, bf16[2048,1536]{1,0:T(8,128)(2,1)} %bitcast.26), custom_call_target="tpu_custom_call" | custom-call | tf_op jit(solution)/shard_map/back/pallas_call | solution.py:506
  239.1 19.8 %all-to-all-done.4 = bf16[64,8,2048]{2,1,0:T(8,128)(2,1)S(1)} async-done(((bf16[64,8,2048]{2,1,0:T(8,128)(2,1)}), bf16[64,8,2048]{2,1,0:T(8,128)(2,1)S(1)}, u32[]{:S(2)}, u32[]{:S(2)}) %all-to-all-start.4) | async-done | bytes 2097184 | tf_op jit(solution)/shard_map/all_to_all | solution.py:680
  259.0 6.2 %all-to-all-start.3 = ((bf16[64,8,1792]{2,1,0:T(8,128)(2,1)}), bf16[64,8,1792]{2,1,0:T(8,128)(2,1)}, u32[]{:S(2)}, u32[]{:S(2)}) async-start(bf16[64,8,1792]{2,1,0:T(8,128)(2,1)} %bitcast.32), calls=%async_computation.3 | async-start | bytes 3670016 | tf_op jit(solution)/shard_map/all_to_all | solution.py:680
  265.1 13.2 %serve.1 = bf16[512,1792]{1,0:T(8,128)(2,1)} custom-call(s32[2]{0:T(128)S(1)} %pad_add_fusion.refs_0_.scal.refs_4_, s32[1,64]{1,0:T(1,128)S(1)} %copy-done.6, s32[1,64]{1,0:T(1,128)S(1)} %collective-permute-done.2.blocks_b, bf16[512,2048]{1,0:T(8,128)(2,1)S(1)} %bitcast.21, bf16[16,4,144,256]{3,2,1,0:T(8,128)(2,1)} %bitcast.13.w_a, ...), custom_call_target="tpu_custom_call" | custom-call | tf_op jit(solution)/shard_map/serve/pallas_call | solution.py:587
  278.4 12.0 %all-to-all-done.3 = bf16[64,8,1792]{2,1,0:T(8,128)(2,1)} async-done(((bf16[64,8,1792]{2,1,0:T(8,128)(2,1)}), bf16[64,8,1792]{2,1,0:T(8,128)(2,1)}, u32[]{:S(2)}, u32[]{:S(2)}) %all-to-all-start.3) | async-done | bytes 1835040 | tf_op jit(solution)/shard_map/all_to_all | solution.py:680
  290.4 5.9 %all-to-all-start.5 = ((bf16[64,8,1792]{2,1,0:T(8,128)(2,1)}), bf16[64,8,1792]{2,1,0:T(8,128)(2,1)S(1)}, u32[]{:S(2)}, u32[]{:S(2)}) async-start(bf16[64,8,1792]{2,1,0:T(8,128)(2,1)} %bitcast.36), calls=%async_computation.5 | async-start | bytes 3670016 | tf_op jit(solution)/shard_map/all_to_all | solution.py:680
  296.3 2.5 collective-permute-start.8
  298.8 21.7 %all-to-all-done.5 = bf16[64,8,1792]{2,1,0:T(8,128)(2,1)S(1)} async-done(((bf16[64,8,1792]{2,1,0:T(8,128)(2,1)}), bf16[64,8,1792]{2,1,0:T(8,128)(2,1)S(1)}, u32[]{:S(2)}, u32[]{:S(2)}) %all-to-all-start.5) | async-done | bytes 1835040 | tf_op jit(solution)/shard_map/all_to_all | solution.py:680
  320.5 3.6 %collective-permute-start.10 = (bf16[512,1792]{1,0:T(8,128)(2,1)S(1)}, bf16[512,1792]{1,0:T(8,128)(2,1)S(1)}, u32[]{:S(2)}, u32[]{:S(2)}) collective-permute-start(bf16[512,1792]{1,0:T(8,128)(2,1)S(1)} %bitcast.22), channel_id=1, source_target_pairs={{0,64},{64,0},{1,65},{65,1},{2,66},{66,2},{3,67},{67,3},{4,68},{68... | collective-permute-start | bytes 5505032 | tf_op jit(solution)/shard_map/ppermute | solution.py:676
  324.1 3.9 %unpack.1.refs_4_ = bf16[448,2048]{1,0:T(8,128)(2,1)S(1)} custom-call(s32[2]{0:T(128)S(1)} %pad_add_fusion.refs_0_.scal.refs_4_, bf16[448,448]{1,0:T(8,128)(2,1)S(1)} %get-tuple-element.32.refs_1_, bf16[512,1792]{1,0:T(8,128)(2,1)} %bitcast.10.refs_2_, bf16[512,1792]{1,0:T(8,128)(2,1)S(1)} %bitcast.23, s32[2]{0:T(128)S(1)} %pad_add_fusion.refs_0_.scal.refs_4_), custom_call_target="tpu_custom_call" | custom-call | tf_op jit(solution)/shard_map/unpack/pallas_call | solution.py:660
  328.0 4.5 %unpack_rest.1 = bf16[448,2048]{1,0:T(8,128)(2,1)} custom-call(s32[2]{0:T(128)S(1)} %pad_add_fusion.refs_0_.scal.refs_4_, bf16[448,448]{1,0:T(8,128)(2,1)S(1)} %get-tuple-element.19.refs_1_, bf16[512,1792]{1,0:T(8,128)(2,1)} %collective-permute-done.8.refs_2_, bf16[512,1792]{1,0:T(8,128)(2,1)S(1)} %collective-permute-done.10.refs_3_, ...), custom_call_target="tpu_custom_call" | custom-call | tf_op jit(solution)/shard_map/unpack_rest/pallas_call | solution.py:660
  (29 shorter events, 2.1 us)
Async XLA Ops:
  0.0 7.2 %collective-permute-start.3 = (bf16[448,2048]{1,0:T(8,128)(2,1)}, bf16[448,2048]{1,0:T(8,128)(2,1)S(1)}, u32[]{:S(2)}, u32[]{:S(2)}) collective-permute-start(bf16[448,2048]{1,0:T(8,128)(2,1)} %bitcast.33), channel_id=1, source_target_pairs={{0,64},{64,0},{1,65},{65,1},{2,66},{66,2},{3,67},{67,3},{4,68},{68... | collective-permute-start | bytes 5505032 | tf_op jit(solution)/shard_map/ppermute | solution.py:676
  1.4 3.6 %collective-permute-start = (s32[1,448]{1,0:T(1,128)}, s32[1,448]{1,0:T(1,128)S(1)}, u32[]{:S(2)}, u32[]{:S(2)}) collective-permute-start(s32[1,448]{1,0:T(1,128)} %bitcast.37), channel_id=1, source_target_pairs={{0,64},{64,0},{1,65},{65,1},{2,66},{66,2},{3,67},{67,3},{4,68},{68... | collective-permute-start | bytes 5384 | tf_op jit(solution)/shard_map/ppermute | solution.py:676
  1.4 3.6 %collective-permute-start.1 = (bf16[1,448]{1,0:T(2,128)(2,1)}, bf16[1,448]{1,0:T(2,128)(2,1)S(1)}, u32[]{:S(2)}, u32[]{:S(2)}) collective-permute-start(bf16[1,448]{1,0:T(2,128)(2,1)} %refs_3_.1), channel_id=1, source_target_pairs={{0,64},{64,0},{1,65},{65,1},{2,66},{66,2},{3,67},{67,3},{4,68},{68... | collective-permute-start | bytes 2696 | tf_op jit(solution)/shard_map/ppermute | solution.py:676
  7.2 3.2 copy-start.4
  7.2 3.2 copy-start
  10.4 11.3 %copy-start.6 = (s32[1,64]{1,0:T(1,128)S(1)}, s32[1,64]{1,0:T(1,128)}, u32[]{:S(2)}) copy-start(s32[1,64]{1,0:T(1,128)} %blocks_a.3) | copy-start | bytes 772
  10.4 38.7 %all-to-all-start = ((bf16[64,8,2048]{2,1,0:T(8,128)(2,1)}), bf16[64,8,2048]{2,1,0:T(8,128)(2,1)S(1)}, u32[]{:S(2)}, u32[]{:S(2)}) async-start(bf16[64,8,2048]{2,1,0:T(8,128)(2,1)} %bitcast.30), calls=%async_computation | async-start | bytes 4194304 | tf_op jit(solution)/shard_map/all_to_all | solution.py:680
  21.7 2.7 collective-permute-start.2
  61.9 6.6 %collective-permute-start.4 = (bf16[512,1536]{1,0:T(8,128)(2,1)}, bf16[512,1536]{1,0:T(8,128)(2,1)S(1)}, u32[]{:S(2)}, u32[]{:S(2)}) collective-permute-start(bf16[512,1536]{1,0:T(8,128)(2,1)} %get-tuple-element.28.refs_2_.bg_h), channel_id=1, source_target_pairs={{0,64},{64,0},{1,65},{65,1},{2,66},{66,2},{3,67},{67,3},{4,68},{68... | collective-permute-start | bytes 4718600 | tf_op jit(solution)/shard_map/ppermute | solution.py:676
  65.2 6.2 %collective-permute-start.7 = (bf16[512,2048]{1,0:T(8,128)(2,1)S(1)}, bf16[512,2048]{1,0:T(8,128)(2,1)S(1)}, u32[]{:S(2)}, u32[]{:S(2)}) collective-permute-start(bf16[512,2048]{1,0:T(8,128)(2,1)S(1)} %bitcast.19), channel_id=1, source_target_pairs={{0,64},{64,0},{1,65},{65,1},{2,66},{66,2},{3,67},{67,3},{4,68},{68... | collective-permute-start | bytes 6291464 | tf_op jit(solution)/shard_map/ppermute | solution.py:676
  68.4 4.9 %copy-start.2 = (bf16[512,1536]{1,0:T(8,128)(2,1)S(1)}, bf16[512,1536]{1,0:T(8,128)(2,1)}, u32[]{:S(2)}) copy-start(bf16[512,1536]{1,0:T(8,128)(2,1)} %get-tuple-element.28.refs_2_.bg_h) | copy-start | bytes 4718596
  68.4 12.1 %collective-permute-start.6 = (bf16[512,1024]{1,0:T(8,128)(2,1)S(1)}, bf16[512,1024]{1,0:T(8,128)(2,1)S(1)}, u32[]{:S(2)}, u32[]{:S(2)}) collective-permute-start(bf16[512,1024]{1,0:T(8,128)(2,1)S(1)} %get-tuple-element.27), channel_id=1, source_target_pairs={{0,64},{64,0},{1,65},{65,1},{2,66},{66,2},{3,67},{67,3},{4,68},{68... | collective-permute-start | bytes 3145736 | tf_op jit(solution)/shard_map/ppermute | solution.py:676
  68.8 11.7 %collective-permute-start.5 = (bf16[768,512]{1,0:T(8,128)(2,1)S(1)}, bf16[768,512]{1,0:T(8,128)(2,1)S(1)}, u32[]{:S(2)}, u32[]{:S(2)}) collective-permute-start(bf16[768,512]{1,0:T(8,128)(2,1)S(1)} %get-tuple-element.25.refs_1_), channel_id=1, source_target_pairs={{0,64},{64,0},{1,65},{65,1},{2,66},{66,2},{3,67},{67,3},{4,68},{68... | collective-permute-start | bytes 2359304 | tf_op jit(solution)/shard_map/ppermute | solution.py:676
  85.7 62.7 %copy-start.7 = (s32[64]{0:T(128)S(1)}, s32[64]{0:T(128)}, u32[]{:S(2)}) copy-start(s32[64]{0:T(128)} %slot_map.1) | copy-start | bytes 772
  155.3 65.0 %copy-start.1 = (bf16[448,2048]{1,0:T(8,128)(2,1)S(1)}, bf16[448,2048]{1,0:T(8,128)(2,1)}, u32[]{:S(2)}) copy-start(bf16[448,2048]{1,0:T(8,128)(2,1)} %copy-done) | copy-start | bytes 5505028
  155.3 64.9 %copy-start.5 = (bf16[512,128]{1,0:T(8,128)(2,1)S(1)}, bf16[512,128]{1,0:T(8,128)(2,1)}, u32[]{:S(2)}) copy-start(bf16[512,128]{1,0:T(8,128)(2,1)} %copy-done.4) | copy-start | bytes 393220
  216.9 48.2 %collective-permute-start.9 = (bf16[64,144,256]{2,1,0:T(8,128)(2,1)}, bf16[64,144,256]{2,1,0:T(8,128)(2,1)}, u32[]{:S(2)}, u32[]{:S(2)}) collective-permute-start(bf16[64,144,256]{2,1,0:T(8,128)(2,1)} %all_to_all.31), channel_id=1, source_target_pairs={{0,64},{64,0},{1,65},{65,1},{2,66},{66,2},{3,67},{67,3},{4,68},{68... | collective-permute-start | bytes 14155784 | tf_op jit(solution)/shard_map/ppermute | solution.py:676
  224.4 34.5 %all-to-all-start.4 = ((bf16[64,8,2048]{2,1,0:T(8,128)(2,1)}), bf16[64,8,2048]{2,1,0:T(8,128)(2,1)S(1)}, u32[]{:S(2)}, u32[]{:S(2)}) async-start(bf16[64,8,2048]{2,1,0:T(8,128)(2,1)} %bitcast.31), calls=%async_computation.4 | async-start | bytes 4194304 | tf_op jit(solution)/shard_map/all_to_all | solution.py:680
  229.3 1.4 copy-start.3
  259.0 31.4 %all-to-all-start.3 = ((bf16[64,8,1792]{2,1,0:T(8,128)(2,1)}), bf16[64,8,1792]{2,1,0:T(8,128)(2,1)}, u32[]{:S(2)}, u32[]{:S(2)}) async-start(bf16[64,8,1792]{2,1,0:T(8,128)(2,1)} %bitcast.32), calls=%async_computation.3 | async-start | bytes 3670016 | tf_op jit(solution)/shard_map/all_to_all | solution.py:680
  290.4 30.2 %all-to-all-start.5 = ((bf16[64,8,1792]{2,1,0:T(8,128)(2,1)}), bf16[64,8,1792]{2,1,0:T(8,128)(2,1)S(1)}, u32[]{:S(2)}, u32[]{:S(2)}) async-start(bf16[64,8,1792]{2,1,0:T(8,128)(2,1)} %bitcast.36), calls=%async_computation.5 | async-start | bytes 3670016 | tf_op jit(solution)/shard_map/all_to_all | solution.py:680
  296.3 31.7 %collective-permute-start.8 = (bf16[512,1792]{1,0:T(8,128)(2,1)}, bf16[512,1792]{1,0:T(8,128)(2,1)}, u32[]{:S(2)}, u32[]{:S(2)}) collective-permute-start(bf16[512,1792]{1,0:T(8,128)(2,1)} %bitcast.10.refs_2_), channel_id=1, source_target_pairs={{0,64},{64,0},{1,65},{65,1},{2,66},{66,2},{3,67},{67,3},{4,68},{68... | collective-permute-start | bytes 5505032 | tf_op jit(solution)/shard_map/ppermute | solution.py:676
  320.5 7.5 %collective-permute-start.10 = (bf16[512,1792]{1,0:T(8,128)(2,1)S(1)}, bf16[512,1792]{1,0:T(8,128)(2,1)S(1)}, u32[]{:S(2)}, u32[]{:S(2)}) collective-permute-start(bf16[512,1792]{1,0:T(8,128)(2,1)S(1)} %bitcast.22), channel_id=1, source_target_pairs={{0,64},{64,0},{1,65},{65,1},{2,66},{66,2},{3,67},{67,3},{4,68},{68... | collective-permute-start | bytes 5505032 | tf_op jit(solution)/shard_map/ppermute | solution.py:676
